TPU v7x, 128 devices: a whole 4x4x4 slice. The times are simulated.
128 devices in a mesh: pix: 8 (over y, core), exp: 16 (over x, z).
Axes of the slice: x: 4, y: 4, z: 4, core: 2. Of those that a mesh axis runs over, the one named last changes fastest.
Arguments:
- design: bfloat16 [200, 786432], P(None, ('pix', 'exp')), may hold values from -1 to 1
- det_weight: float32 [786432], P(('pix', 'exp')), may hold values from 0.2 to 2
- outlier_mask: int32 [2, 786432], P(None, ('pix', 'exp')), may hold values from 0 to 1
- star_owner: int32 [786432, 1], P(('pix', 'exp')), may hold values from 0 to 127; in each aligned block of 6144 rows (0 to 6143, 6144 to 12287, ...) at most 96 rows name the same one
- star_slot: int32 [786432], P(('pix', 'exp')), may hold values from 0 to 767
- coef_init: float32 [128, 2, 200], P('exp'), may hold values from -6 to 6
- star_ref: float32 [2, 98304], P(None, ('pix', 'exp')), may hold values from -24 to 24
- star_prior: float32 [98304], P(('pix', 'exp')), may hold values from 0.2 to 2
Outputs:
- coefficients: float32 [128, 2, 200], P('exp')
- star_means: float32 [2, 98304], P(None, ('pix', 'exp'))
Inputs may be any that keep to these rules, and one draw needn't show every extreme that they name: `star_owner`: among the 6144 detections of one device, at most 96 name the same owner, and in every draw some device's detections name some owner exactly 96 times.
All inputs are finite; a program needn't handle non-finite values.
Results may differ from a plain program's by a relative error of at most 0.00045.
The roundings to bfloat16 on the way count: a program that leaves them out, or rounds other values in their place, can miss the bound.
Values sent between devices are 32-bit elements; how exact they have to be, the bound alone decides.
No kernel may reach another device: no remote copies, remote signals or barrier semaphores. Data moves between devices by JAX's collectives and lax.ppermute only.
A program may use at most 64 MiB of HBM per device.

v0:
```python
import jax
import jax.numpy as jnp
from jax import lax
from jax.sharding import PartitionSpec as P

ITERS = 2


RIDGE = 0.5
STAR_BLOCKS = 8


def solve_blocks(gram_block, right_side):
    identity = jnp.eye(gram_block.shape[-1], dtype=jnp.float32)
    factor = jnp.linalg.cholesky(gram_block + RIDGE * identity)
    columns = jnp.swapaxes(right_side, 1, 2)
    middle = jax.scipy.linalg.solve_triangular(factor, columns, lower=True)
    update = jax.scipy.linalg.solve_triangular(factor, middle, lower=True, trans=1)
    return jnp.swapaxes(update, 1, 2)


def star_table(id_block, star_count):
    return (id_block[:, None] == jnp.arange(star_count, dtype=jnp.int32)[None, :]).astype(
        jnp.float32
    )


def on_device(
    design, det_weight, outlier_mask, star_owner, star_slot, coef_init, star_ref, star_prior
):
    highest = lax.Precision.HIGHEST
    peer_count = lax.axis_size(("pix", "exp"))
    pix_count = lax.axis_size("pix")
    term_count, row_count = design.shape
    maps_device = coef_init.shape[0]
    exp_rows_local = row_count // maps_device
    capacity = 2 * row_count // peer_count
    star_count = star_prior.shape[0]
    share_count = maps_device // pix_count
    slot_total = peer_count * capacity
    block_width = slot_total // STAR_BLOCKS
    owner_index = star_owner[:, 0]
    owner_hot = (owner_index[:, None] == jnp.arange(peer_count, dtype=jnp.int32)[None, :]).astype(
        jnp.float32
    )
    count_before = jnp.cumsum(owner_hot, axis=0) - owner_hot
    position = jnp.sum(count_before * owner_hot, axis=1).astype(jnp.int32)
    place_hot = (position[:, None] == jnp.arange(capacity, dtype=jnp.int32)[None, :]).astype(
        jnp.float32
    )

    def place(values):
        spread = values[:, :, None] * place_hot[None, :, :]
        placed = jnp.einsum("cip,io->cop", spread, owner_hot, precision=highest)
        return placed.reshape(values.shape[0], slot_total)

    id_buffer = place(star_slot.astype(jnp.float32)[None, :])[0].astype(jnp.int32)
    got_ids = lax.all_to_all(
        id_buffer.reshape(peer_count, capacity),
        ("pix", "exp"),
        split_axis=0,
        concat_axis=0,
        tiled=True,
    )
    id_blocks = got_ids.reshape(STAR_BLOCKS, block_width)
    design_blocks = design.reshape(term_count, maps_device, exp_rows_local)
    coefficients = coef_init
    star_means = jnp.zeros((2, star_count), jnp.float32)
    for step_index in range(ITERS):
        masked_weight = det_weight * outlier_mask[step_index].astype(jnp.float32)
        weighted = (
            (design * masked_weight[None, :])
            .astype(jnp.bfloat16)
            .reshape(term_count, maps_device, exp_rows_local)
        )
        gram_local = jnp.einsum(
            "tjr,ujr->jtu", weighted, design_blocks, preferred_element_type=jnp.float32
        )
        predicted = jnp.einsum(
            "jct,tjr->cjr",
            coefficients.astype(jnp.bfloat16),
            design_blocks,
            preferred_element_type=jnp.float32,
        ).reshape(2, row_count)
        payload = jnp.concatenate([predicted, masked_weight[None, :]], axis=0)
        forward_payload = place(payload)
        forward_delivered = lax.all_to_all(
            forward_payload.reshape(3, peer_count, capacity),
            ("pix", "exp"),
            split_axis=1,
            concat_axis=1,
            tiled=True,
        )
        arrived = forward_delivered.reshape(3, slot_total)
        totals_in = jnp.concatenate([arrived[2:] * arrived[:2], arrived[2:]], axis=0)
        value_blocks = jnp.swapaxes(totals_in.reshape(3, STAR_BLOCKS, block_width), 0, 1)

        def accumulate(pair):
            id_block, value_block = pair
            return jnp.dot(value_block, star_table(id_block, star_count), precision=highest)

        totals = jnp.sum(lax.map(accumulate, (id_blocks, value_blocks)), axis=0)
        star_means = (star_prior * star_ref + totals[:2]) / (star_prior + totals[2])

        def lookup(id_block):
            return jnp.dot(star_means, star_table(id_block, star_count).T, precision=highest)

        means_at_slots = jnp.swapaxes(lax.map(lookup, id_blocks), 0, 1).reshape(2, slot_total)
        delivered = lax.all_to_all(
            means_at_slots.reshape(2, peer_count, capacity),
            ("pix", "exp"),
            split_axis=1,
            concat_axis=1,
            tiled=True,
        )
        buffer = delivered.reshape(2, slot_total)
        shaped = buffer.reshape(buffer.shape[0], peer_count, capacity)
        pick_spread = jnp.einsum("cop,io->cip", shaped, owner_hot, precision=highest)
        returned = jnp.sum(pick_spread * place_hot[None, :, :], axis=2)
        residual_lo = (
            (returned - predicted).astype(jnp.bfloat16).reshape(2, maps_device, exp_rows_local)
        )
        right_side = jnp.einsum(
            "tjr,cjr->jct", weighted, residual_lo, preferred_element_type=jnp.float32
        )
        gram_part, right_part = (
            lax.psum_scatter(gram_local, "pix", scatter_dimension=0, tiled=True),
            lax.psum_scatter(right_side, "pix", scatter_dimension=0, tiled=True),
        )
        own_maps = lax.dynamic_slice_in_dim(
            coefficients, lax.axis_index("pix") * share_count, share_count, 0
        )
        coefficients = lax.all_gather(
            own_maps + solve_blocks(gram_part, right_part), "pix", axis=0, tiled=True
        )
    return (coefficients, star_means)


def solution(mesh):
    placed = (
        P(None, ("pix", "exp")),
        P(("pix", "exp")),
        P(None, ("pix", "exp")),
        P(("pix", "exp"), None),
        P(("pix", "exp")),
        P("exp", None, None),
        P(None, ("pix", "exp")),
        P(("pix", "exp")),
    )
    return jax.shard_map(
        on_device,
        mesh=mesh,
        in_specs=placed,
        out_specs=(P("exp", None, None), P(None, ("pix", "exp"))),
        check_vma=False,
    )
```

profile of v0, /device:TPU:1, one launch (start us, length us, event | category | flops | bytes accessed | tf_op | source)
XLA Modules:
  0.0 383.1 jit_solution(11239302279373869306)
XLA Ops:
  16.8 11.5 %all-to-all-start = ((s32[128,1,96]{2,1,0:T(1,128)}), s32[128,1,96]{2,1,0:T(1,128)S(1)}, u32[]{:S(2)}, u32[]{:S(2)}) async-start(s32[128,1,96]{2,1,0:T(1,128)} %copy.58), calls=%async_computation.1 | async-start | bytes 131072 | tf_op jit(solution)/shard_map/all_to_all | solution.py:58
  43.0 9.8 %all-to-all-start.1 = ((f32[3,128,96]{2,0,1:T(4,128)}), f32[3,128,96]{2,0,1:T(4,128)S(1)}, u32[]{:S(2)}, u32[]{:S(2)}) async-start(f32[3,128,96]{2,0,1:T(4,128)} %copy.60), calls=%async_computation.2 | async-start | bytes 524288 | tf_op jit(solution)/shard_map/all_to_all | solution.py:87
  64.3 13.6 %while.46 = (s32[]{:T(128)}, f32[8,3,768]{2,1,0:T(4,128)S(1)}, f32[8,3,1536]{2,0,1:T(8,128)S(1)}, s32[8,1536]{1,0:T(8,128)S(1)}, s32[]{:T(128)}) while((s32[]{:T(128)}, f32[8,3,768]{2,1,0:T(4,128)S(1)}, f32[8,3,1536]{2,0,1:T(8,128)S(1)}, s32[8,1536]{1,0:T(8,128)S(1)}, s32[]{:T(128)}) %tuple.107), condition=%wide.region_9.11_spmd, body=%wide.region_8.10_spmd.sunk | while | flops 43646976 | bytes 88137 | solution.py:102
  78.0 18.2 %while.47 = (s32[]{:T(128)}, f32[8,2,1536]{2,1,0:T(2,128)S(1)}, s32[8,1536]{1,0:T(8,128)S(1)}, f32[2,768]{1,0:T(2,128)S(1)}, s32[]{:T(128)}) while((s32[]{:T(128)}, f32[8,2,1536]{2,1,0:T(2,128)S(1)}, s32[8,1536]{1,0:T(8,128)S(1)}, f32[2,768]{1,0:T(2,128)S(1)}, s32[]{:T(128)}) %tuple.125), condition=%wide.region_12.14_spmd, body=%wide.region_11.13_spmd.sunk | while | flops 29491200 | bytes 38981 | solution.py:108
  97.0 5.8 %all-to-all-start.2 = ((f32[2,128,96]{2,0,1:T(2,128)}), f32[2,128,96]{2,0,1:T(2,128)S(1)}, u32[]{:S(2)}, u32[]{:S(2)}) async-start(f32[2,128,96]{2,0,1:T(2,128)} %copy.64), calls=%async_computation.3 | async-start | bytes 262144 | tf_op jit(solution)/shard_map/all_to_all | solution.py:109
  102.8 9.8 %all-to-all-done.2 = f32[2,128,96]{2,0,1:T(2,128)S(1)} async-done(((f32[2,128,96]{2,0,1:T(2,128)}), f32[2,128,96]{2,0,1:T(2,128)S(1)}, u32[]{:S(2)}, u32[]{:S(2)}) %all-to-all-start.2) | async-done | bytes 98336 | tf_op jit(solution)/shard_map/all_to_all | solution.py:109
  112.8 5.6 %fusion.23 = f32[6144,192]{0,1:S(1)} fusion(f32[128,192]{0,1:T(8,128)S(1)} %bitcast.303, s32[6144]{0:T(1024)S(1)} %bitcast.295), kind=kOutput, calls=%fused_computation.44 | convolution fusion | flops 1812725760 | bytes 4841472
  120.8 21.3 %all-reduce.5 = f32[8,2,200]{2,1,0:T(2,128)S(1)} all-reduce(f32[8,2,200]{2,1,0:T(2,128)S(1)} %fusion.38), channel_id=3, replica_groups=mesh['pix'=8,'exp'=16] {'pix'}, use_global_device_ids=true, to_apply=%region_14.16.clone | all-reduce | flops 3200 | bytes 25600
  144.9 11.7 %custom-call.26 = f32[1,128,128]{2,1,0:T(8,128)S(1)} custom-call(f32[1,128,128]{2,1,0:T(8,128)S(1)} %cholesky.208), custom_call_target="Cholesky" | custom-call | tf_op jit(solution)/shard_map/jit(cholesky)/cholesky | solution.py:15
  156.6 9.8 %custom-call.27 = f32[1,1,128,128]{2,3,1,0:T(8,128)S(1)} custom-call(f32[1,1,128,128]{3,2,1,0:T(8,128)S(1)} %get-tuple-element.208), custom_call_target="InvertDiagBlocksLowerTriangular" | custom-call | tf_op jit(solution)/shard_map/jit(cholesky)/cholesky | solution.py:15
  166.9 6.6 %custom-call.28 = f32[1,72,72]{2,1,0:T(8,128)S(1)} custom-call(f32[1,72,72]{2,1,0:T(8,128)S(1)} %fusion.67), custom_call_target="Cholesky" | custom-call | tf_op jit(solution)/shard_map/jit(cholesky)/cholesky | solution.py:15
  178.2 11.7 %custom-call.21 = f32[1,128,128]{2,1,0:T(8,128)S(1)} custom-call(f32[1,128,128]{2,1,0:T(8,128)S(1)} %cholesky.205), custom_call_target="Cholesky" | custom-call | tf_op jit(solution)/shard_map/jit(cholesky)/cholesky | solution.py:15
  190.0 10.2 %custom-call.22 = f32[1,1,128,128]{2,3,1,0:T(8,128)S(1)} custom-call(f32[1,1,128,128]{3,2,1,0:T(8,128)S(1)} %get-tuple-element.206), custom_call_target="InvertDiagBlocksLowerTriangular" | custom-call | tf_op jit(solution)/shard_map/jit(cholesky)/cholesky | solution.py:15
  200.6 6.6 %custom-call.23 = f32[1,72,72]{2,1,0:T(8,128)S(1)} custom-call(f32[1,72,72]{2,1,0:T(8,128)S(1)} %fusion.66), custom_call_target="Cholesky" | custom-call | tf_op jit(solution)/shard_map/jit(cholesky)/cholesky | solution.py:15
  210.6 20.5 %custom-call.25 = f32[2,128,128]{1,2,0:T(8,128)S(1)} custom-call(f32[2,128,128]{2,1,0:T(8,128)} %get-tuple-element.221), custom_call_target="InvertDiagBlocksLowerTriangular" | custom-call | tf_op jit(solution)/shard_map/jit(_solve_triangular)/triangular_solve | solution.py:18
  232.2 14.7 %all_gather.6 = f32[8,2,200]{2,1,0:T(2,128)S(1)} all-gather(f32[1,2,200]{2,1,0:T(2,128)S(1)} %fusion.96), channel_id=1, replica_groups=mesh['pix'=8,'exp'=16] {'pix'}, dimensions={0}, use_global_device_ids=true | all-gather | bytes 14400 | tf_op jit(solution)/shard_map/all_gather | solution.py:133
  254.5 4.9 %all-to-all-start.3 = ((f32[3,128,96]{2,0,1:T(4,128)}), f32[3,128,96]{2,0,1:T(4,128)S(1)}, u32[]{:S(2)}, u32[]{:S(2)}) async-start(f32[3,128,96]{2,0,1:T(4,128)} %copy.73), calls=%async_computation.5 | async-start | bytes 524288 | tf_op jit(solution)/shard_map/all_to_all | solution.py:87
  259.4 10.8 %all-to-all-done.3 = f32[3,128,96]{2,0,1:T(4,128)S(1)} async-done(((f32[3,128,96]{2,0,1:T(4,128)}), f32[3,128,96]{2,0,1:T(4,128)S(1)}, u32[]{:S(2)}, u32[]{:S(2)}) %all-to-all-start.3) | async-done | bytes 147488 | tf_op jit(solution)/shard_map/all_to_all | solution.py:87
  270.9 13.6 %while.48 = (s32[]{:T(128)}, f32[8,3,768]{2,1,0:T(4,128)S(1)}, f32[8,3,1536]{2,0,1:T(8,128)S(1)}, s32[8,1536]{1,0:T(8,128)S(1)}, s32[]{:T(128)}) while((s32[]{:T(128)}, f32[8,3,768]{2,1,0:T(4,128)S(1)}, f32[8,3,1536]{2,0,1:T(8,128)S(1)}, s32[8,1536]{1,0:T(8,128)S(1)}, s32[]{:T(128)}) %tuple.126), condition=%wide.region_17.21_spmd, body=%wide.region_16.20_spmd.sunk | while | flops 43646976 | bytes 88137 | solution.py:102
  284.6 18.2 %while.49 = (s32[]{:T(128)}, f32[8,2,1536]{2,1,0:T(2,128)S(1)}, s32[8,1536]{1,0:T(8,128)S(1)}, f32[2,768]{1,0:T(2,128)S(1)}, s32[]{:T(128)}) while((s32[]{:T(128)}, f32[8,2,1536]{2,1,0:T(2,128)S(1)}, s32[8,1536]{1,0:T(8,128)S(1)}, f32[2,768]{1,0:T(2,128)S(1)}, s32[]{:T(128)}) %tuple.127), condition=%wide.region_20.24_spmd, body=%wide.region_19.23_spmd.sunk | while | flops 29491200 | bytes 38981 | solution.py:108
  308.2 19.7 %custom-call.30 = f32[2,128,128]{1,2,0:T(8,128)S(1)} custom-call(f32[2,128,128]{2,1,0:T(8,128)S(1)} %get-tuple-element.222), custom_call_target="InvertDiagBlocksLowerTriangular" | custom-call | tf_op jit(solution)/shard_map/jit(_solve_triangular)/triangular_solve | solution.py:18
  328.0 5.6 %fusion.26 = f32[6144,192]{0,1:S(1)} fusion(f32[128,192]{0,1:T(8,128)S(1)} %bitcast.304, s32[6144]{0:T(1024)S(1)} %bitcast.297), kind=kOutput, calls=%fused_computation.47 | convolution fusion | flops 1812725760 | bytes 4841472
  336.0 23.0 %all-reduce.6 = f32[8,2,200]{2,1,0:T(2,128)S(1)} all-reduce(f32[8,2,200]{2,1,0:T(2,128)S(1)} %fusion.27), channel_id=5, replica_groups=mesh['pix'=8,'exp'=16] {'pix'}, use_global_device_ids=true, to_apply=%region_22.26.clone | all-reduce | flops 3200 | bytes 25600
  360.8 14.7 %all_gather.7 = f32[8,2,200]{2,1,0:T(2,128)S(1)} all-gather(f32[1,2,200]{2,1,0:T(2,128)S(1)} %fusion.97), channel_id=1, replica_groups=mesh['pix'=8,'exp'=16] {'pix'}, dimensions={0}, use_global_device_ids=true | all-gather | bytes 14400 | tf_op jit(solution)/shard_map/all_gather | solution.py:133
  (239 shorter events, 130.9 us)
Async XLA Ops:
  9.2 1.0 copy-start.4
  10.2 3.8 %copy-start.7 = (s32[6144]{0:T(1024)S(1)}, s32[6144]{0:T(1024)}, u32[]{:S(2)}) copy-start(s32[6144]{0:T(1024)} %param.25) | copy-start | bytes 73732
  10.2 18.6 %copy-start.6 = (s32[2,6144]{1,0:T(2,128)S(1)}, s32[2,6144]{1,0:T(2,128)}, u32[]{:S(2)}) copy-start(s32[2,6144]{1,0:T(2,128)} %param.23) | copy-start | bytes 147460
  10.3 18.6 %copy-start.8 = (f32[6144]{0:T(1024)S(1)}, f32[6144]{0:T(1024)}, u32[]{:S(2)}) copy-start(f32[6144]{0:T(1024)} %param.22) | copy-start | bytes 73732
  10.3 18.6 %copy-start = (bf16[200,6144]{1,0:T(8,128)(2,1)S(1)}, bf16[200,6144]{1,0:T(8,128)(2,1)}, u32[]{:S(2)}) copy-start(bf16[200,6144]{1,0:T(8,128)(2,1)} %param.21) | copy-start | bytes 7372804
  16.8 26.2 %all-to-all-start = ((s32[128,1,96]{2,1,0:T(1,128)}), s32[128,1,96]{2,1,0:T(1,128)S(1)}, u32[]{:S(2)}, u32[]{:S(2)}) async-start(s32[128,1,96]{2,1,0:T(1,128)} %copy.58), calls=%async_computation.1 | async-start | bytes 131072 | tf_op jit(solution)/shard_map/all_to_all | solution.py:58
  28.3 114.5 %reduce-scatter.5.cloned.1.call-start = ((), (), s32[]{:S(2)}) async-start(), calls=%async_computation.8 | async-start | bytes 1843200 | tf_op jit(solution)/shard_map/reduce_scatter | solution.py:127
  31.1 1.4 copy-start.1
  34.7 0.7 copy-start.11
  43.0 20.6 %all-to-all-start.1 = ((f32[3,128,96]{2,0,1:T(4,128)}), f32[3,128,96]{2,0,1:T(4,128)S(1)}, u32[]{:S(2)}, u32[]{:S(2)}) async-start(f32[3,128,96]{2,0,1:T(4,128)} %copy.60), calls=%async_computation.2 | async-start | bytes 524288 | tf_op jit(solution)/shard_map/all_to_all | solution.py:87
  52.7 123.4 %reduce-scatter.3.cloned.1.call-start = ((), (), s32[]{:S(2)}) async-start(), calls=%async_computation.7 | async-start | bytes 1843200 | tf_op jit(solution)/shard_map/reduce_scatter | solution.py:127
  53.0 4.5 %copy-start.12 = (u32[128]{0:T(128)S(1)}, u32[128]{0:T(128)}, u32[]{:S(2)}) copy-start(u32[128]{0:T(128)} %constant.215) | copy-start | bytes 1540
  64.2 13.6 %copy-start.5 = (f32[768]{0:T(1024)S(1)}, f32[768]{0:T(1024)}, u32[]{:S(2)}) copy-start(f32[768]{0:T(1024)} %param.28) | copy-start | bytes 9220
  64.3 13.6 %copy-start.9 = (f32[2,768]{1,0:T(2,128)S(1)}, f32[2,768]{1,0:T(2,128)}, u32[]{:S(2)}) copy-start(f32[2,768]{1,0:T(2,128)} %param.27) | copy-start | bytes 18436
  97.0 15.7 %all-to-all-start.2 = ((f32[2,128,96]{2,0,1:T(2,128)}), f32[2,128,96]{2,0,1:T(2,128)S(1)}, u32[]{:S(2)}, u32[]{:S(2)}) async-start(f32[2,128,96]{2,0,1:T(2,128)} %copy.64), calls=%async_computation.3 | async-start | bytes 262144 | tf_op jit(solution)/shard_map/all_to_all | solution.py:109
  118.4 1.7 copy-start.3
  254.5 15.8 %all-to-all-start.3 = ((f32[3,128,96]{2,0,1:T(4,128)}), f32[3,128,96]{2,0,1:T(4,128)S(1)}, u32[]{:S(2)}, u32[]{:S(2)}) async-start(f32[3,128,96]{2,0,1:T(4,128)} %copy.73), calls=%async_computation.5 | async-start | bytes 524288 | tf_op jit(solution)/shard_map/all_to_all | solution.py:87
  302.8 30.8 %copy-start.10 = (f32[2,768]{1,0:T(2,128)}, f32[2,768]{1,0:T(2,128)S(1)}, u32[]{:S(2)}) copy-start(f32[2,768]{1,0:T(2,128)S(1)} %get-tuple-element.403) | copy-start | bytes 18436
  303.7 24.2 %all-to-all-start.4 = ((f32[2,128,96]{2,0,1:T(2,128)}), f32[2,128,96]{2,0,1:T(2,128)S(1)}, u32[]{:S(2)}, u32[]{:S(2)}) async-start(f32[2,128,96]{2,0,1:T(2,128)} %copy.77), calls=%async_computation.6 | async-start | bytes 262144 | tf_op jit(solution)/shard_map/all_to_all | solution.py:109
  333.6 1.7 copy-start.2
Sparse Core Ops, SparseCore 0:
  34.8 33.3 reduce-scatter.4
  70.6 32.8 reduce-scatter.2
where the time goes:
time: 389 us; the launch traced here: 383 us
  other arithmetic  116 us (30%)
  matrix products  97.4 us (25%)
  blocking collectives  73.6 us (19%)
  starting transfers between devices  37.3 us (10%)
  waiting for transfers between devices  24.7 us (6%)
  between operations  17.7 us (5%)
  local copies, waits for them, and re-layouts  16.3 us (4%)
    another operation x14, other arithmetic, solve_blocks(): factor = jnp.linalg.cholesky(gram_block + RIDGE * identity)  59.3 us
    unnamed x2, blocking collectives  44.2 us
    another operation x8, other arithmetic, solve_blocks(): jax.scipy.linalg.solve_triangular(factor, middle, lower=True, trans=1)  41 us
    dot_general x16, matrix products, lookup(): jnp.dot(star_means, star_table(id_block, star_count).T, precision=highest)  35.7 us
    all_gather x2, blocking collectives, on_device(): lax.all_gather(own_maps + solve_blocks(gram_part, right_part), 'pix', axi...  29.3 us
    dot_general x16, matrix products, accumulate(): jnp.dot(value_block, star_table(id_block, star_count), precision=highest)  26.1 us
    unnamed x4, matrix products  18.4 us
    all_to_all x2, waiting for transfers between devices, on_device(): lax.all_to_all(forward_payload.reshape(3, peer_count, capacity), ('pix',...  14.8 us
  transfers between devices with their start and end apart: 7, of which 3 were waited for; matrix products, arithmetic and copies ran while one was open for 29% of the time, Pallas kernels for 0%

commit v1 on v0

v1 whole, which is shorter than its diff:
```python
import functools

import jax
import jax.numpy as jnp
from jax import lax
from jax.experimental import pallas as pl
from jax.experimental.pallas import tpu as pltpu
from jax.sharding import PartitionSpec as P

ITERS = 2
RIDGE = 0.5
LANES = 128
F32 = jnp.float32
BF16 = jnp.bfloat16
NT = (((1,), (1,)), ((), ()))
TN = (((0,), (0,)), ((), ()))


def iota(shape, axis):
    return lax.broadcasted_iota(jnp.int32, shape, axis)


def lane_gather(row, index):
    table = jnp.broadcast_to(row, index.shape)
    return jnp.take_along_axis(table, index, axis=1, mode="promise_in_bounds")


def call(body, out_shape, scratch=(), flops=0, size=0):
    return pl.pallas_call(
        body,
        out_shape=out_shape,
        scratch_shapes=list(scratch),
        cost_estimate=pl.CostEstimate(flops=flops, bytes_accessed=size, transcendentals=0),
    )


def route_body(owner_ref, pos_ref, row_ref, lane_ref, hot_ref, place_ref):
    chunks = owner_ref.shape[0]
    sub = iota((LANES, LANES), 0)
    lane = iota((LANES, LANES), 1)
    wide_sub, wide_lane = iota((LANES, 2 * LANES), 0), iota((LANES, 2 * LANES), 1)
    prefix = jnp.where((wide_sub < wide_lane) | (wide_lane >= LANES), 1.0, 0.0).astype(BF16)
    lane_f = lane.astype(F32)

    def step(r, base):
        at = pl.ds(pl.multiple_of(r * LANES, LANES), LANES)
        hot = jnp.where(owner_ref[pl.ds(r, 1), :] == sub, 1.0, 0.0)
        counts = jnp.dot(hot.astype(BF16), prefix, preferred_element_type=F32)
        pos = jnp.sum(hot * (counts[:, :LANES] + base), axis=0, keepdims=True).astype(jnp.int32)
        pos_ref[pl.ds(r, 1), :] = pos
        place_ref[:, at] = jnp.where(pos == sub, 1.0, 0.0).astype(BF16)
        hot_ref[:LANES, at] = (hot * (r + 1).astype(F32)).astype(BF16)
        hot_ref[LANES:, at] = (hot * lane_f).astype(BF16)
        return base + counts[:, LANES:]

    lax.fori_loop(0, chunks, step, jnp.zeros((LANES, LANES), F32), unroll=4)
    held = lax.dot_general(hot_ref[...], place_ref[...], NT, preferred_element_type=F32)
    row_ref[...] = held[:LANES].astype(jnp.int32) - 1
    lane_ref[...] = held[LANES:].astype(jnp.int32)


def route(owner):
    chunks = owner.shape[0]
    rows = chunks * LANES
    plane = jax.ShapeDtypeStruct((LANES, LANES), jnp.int32)
    return call(
        route_body,
        (jax.ShapeDtypeStruct(owner.shape, jnp.int32), plane, plane),
        (pltpu.VMEM((2 * LANES, rows), BF16), pltpu.VMEM((LANES, rows), BF16)),
        flops=2 * 512 * LANES * rows,
        size=rows * 8,
    )(owner)


def place_body(cap, first, *refs):
    if first:
        coef_ref, design_ref, row_ref, lane_ref, slot_ref, weight_ref, mask_ref, pred_ref, pay_ref, vals = refs
        coef = coef_ref[...]
    else:
        coef_ref, upd_ref, design_ref, row_ref, lane_ref, pred_ref, pay_ref, new_ref, vals = refs
        coef = coef_ref[...] + upd_ref[...]
        new_ref[...] = coef
    exps = coef.shape[0]
    rows = design_ref.shape[1]
    chunks = rows // LANES
    width = rows // exps
    per = width // LANES
    maps = coef.astype(BF16)
    for e in range(exps):
        pred = jnp.dot(maps[e], design_ref[:, e * width : (e + 1) * width], preferred_element_type=F32)
        pred_ref[:, e * width : (e + 1) * width] = pred
        for c in range(2):
            for q in range(per):
                r = c * chunks + e * per + q
                vals[r : r + 1, :] = pred[c : c + 1, q * LANES : (q + 1) * LANES]
    if first:
        vals[2 * chunks : 3 * chunks, :] = slot_ref[...].astype(F32)
        for r in range(chunks):
            at = slice(r * LANES, (r + 1) * LANES)
            for k in range(2):
                vals[(3 + k) * chunks + r : (3 + k) * chunks + r + 1, :] = weight_ref[r : r + 1, :] * mask_ref[
                    k : k + 1, at
                ].astype(F32)
    values = 5 if first else 2
    width_out = 4 if first else 2
    lane8 = iota((8, LANES), 1)

    def tile(d, carry):
        at = pl.ds(pl.multiple_of(d * 8, 8), 8)
        source, index = row_ref[at, :], lane_ref[at, :]
        found = [jnp.zeros((8, LANES), F32)] * values
        for r in range(chunks):
            hit = source == r
            for v in range(values):
                got = lane_gather(vals[v * chunks + r : v * chunks + r + 1, :], index)
                found[v] = jnp.where(hit, got, found[v])
        if first:
            spare = LANES - cap
            later = found.pop()
            for v in range(3):
                moved = pltpu.roll(later, (cap - v * spare) % LANES, 1)
                found[v] = jnp.where(lane8 < cap, found[v], moved)
        for v in range(width_out):
            pay_ref[pl.ds(d * 8 * width_out + v, 8, stride=width_out), :] = found[v]
        return carry

    lax.fori_loop(0, LANES // 8, tile, 0)


def place_first(coef, design, row, lane, slot, weight, mask, cap):
    rows = design.shape[1]
    return call(
        functools.partial(place_body, cap, True),
        (jax.ShapeDtypeStruct((2, rows), F32), jax.ShapeDtypeStruct((4 * LANES, LANES), F32)),
        (pltpu.VMEM((5 * rows // LANES, LANES), F32),),
        flops=2 * 16 * design.size,
        size=2 * design.size,
    )(coef, design, row, lane, slot, weight, mask)


def place_next(coef, upd, design, row, lane, cap):
    rows = design.shape[1]
    return call(
        functools.partial(place_body, cap, False),
        (
            jax.ShapeDtypeStruct((2, rows), F32),
            jax.ShapeDtypeStruct((2 * LANES, LANES), F32),
            jax.ShapeDtypeStruct(coef.shape, F32),
        ),
        (pltpu.VMEM((2 * rows // LANES, LANES), F32),),
        flops=2 * 16 * design.size,
        size=2 * design.size,
    )(coef, upd, design, row, lane)


def pieces(x):
    a = x.astype(BF16).astype(F32)
    b = (x - a).astype(BF16).astype(F32)
    c = ((x - a) - b).astype(BF16).astype(F32)
    return (a, b, c)


def owner_body(cap, first, *refs):
    if first:
        pay_ref, ref_ref, prior_ref, ret_ref, id_ref, later_ref, parts = refs
        width = 4
    else:
        pay_ref, ids_in, weights_in, ref_ref, prior_ref, ret_ref, mean_ref, parts = refs
        id_ref, width = ids_in, 2
    lane8 = iota((8, LANES), 1)
    sub8 = iota((8, LANES), 0)
    sub = iota((LANES, LANES), 0)
    spare = LANES - cap

    def split(g, carry):
        def plane(v):
            return pay_ref[pl.ds(g * 8 * width + v, 8, stride=width), :]

        at = pl.ds(pl.multiple_of(g * 8, 8), 8)
        if first:
            p0, p1, ids, weight = plane(0), plane(1), plane(2), plane(3)
            later = jnp.zeros((8, LANES), F32)
            for v, source in enumerate((p0, p1, ids)):
                moved = pltpu.roll(source, (v * spare - cap) % LANES, 1)
                later = jnp.where((lane8 >= v * spare) & (lane8 < (v + 1) * spare), moved, later)
            later_ref[at, :] = later
            weight = jnp.where(lane8 < cap, weight, 0.0)
            id_ref[at, :] = ids.astype(jnp.int32)
        else:
            p0, p1, weight = plane(0), plane(1), weights_in[at, :]
        for v, x in enumerate((weight * p0, weight * p1, weight)):
            for k, piece in enumerate(pieces(x)):
                parts[3 * v + k, at, :] = piece
        return carry

    lax.fori_loop(0, LANES // 8, split, 0)
    group = 8

    def accumulate(g, total):
        left, right = [], []
        for s in range(group):
            src = g * group + s
            ids = id_ref[pl.ds(src, 1), :]
            hit = (ids >> 7) == sub8
            left.append(
                jnp.concatenate(
                    [jnp.where(hit, parts[k, pl.ds(src, 1), :], 0.0) for k in range(9)], axis=0
                ).astype(BF16)
            )
            right.append(jnp.where((ids & 127) == sub, 1.0, 0.0).astype(BF16))
        return total + lax.dot_general(
            jnp.concatenate(left, axis=1), jnp.concatenate(right, axis=1), NT, preferred_element_type=F32
        )

    total = lax.fori_loop(0, LANES // group, accumulate, jnp.zeros((72, LANES), F32))
    sums = [total[24 * v : 24 * v + 8] + total[24 * v + 8 : 24 * v + 16] + total[24 * v + 16 : 24 * v + 24] for v in range(3)]
    rows = prior_ref.shape[0]
    means = [[], []]
    for h in range(rows):
        prior = prior_ref[h : h + 1, :]
        for c in range(2):
            ref = ref_ref[c : c + 1, h * LANES : (h + 1) * LANES]
            mean = (prior * ref + sums[c][h : h + 1]) / (prior + sums[2][h : h + 1])
            means[c].append(mean)
            if not first:
                mean_ref[c : c + 1, h * LANES : (h + 1) * LANES] = mean

    def look(g, carry):
        at = pl.ds(pl.multiple_of(g * 8, 8), 8)
        ids = id_ref[at, :]
        low, high = ids & 127, ids >> 7
        for c in range(2):
            found = jnp.zeros((8, LANES), F32)
            for h in range(rows):
                found = jnp.where(high == h, lane_gather(means[c][h], low), found)
            ret_ref[pl.ds(g * 16 + c, 8, stride=2), :] = found
        return carry

    lax.fori_loop(0, LANES // 8, look, 0)


def owner_first(pay, star_ref, star_prior, cap):
    return call(
        functools.partial(owner_body, cap, True),
        (
            jax.ShapeDtypeStruct((2 * LANES, LANES), F32),
            jax.ShapeDtypeStruct((LANES, LANES), jnp.int32),
            jax.ShapeDtypeStruct((LANES, LANES), F32),
        ),
        (pltpu.VMEM((9, LANES, LANES), F32),),
        flops=2 * 72 * LANES**3,
        size=pay.size * 4,
    )(pay, star_ref, star_prior)


def owner_next(pay, ids, weights, star_ref, star_prior, cap):
    return call(
        functools.partial(owner_body, cap, False),
        (jax.ShapeDtypeStruct((2 * LANES, LANES), F32), jax.ShapeDtypeStruct(star_ref.shape, F32)),
        (pltpu.VMEM((9, LANES, LANES), F32),),
        flops=2 * 72 * LANES**3,
        size=pay.size * 4,
    )(pay, ids, weights, star_ref, star_prior)


def right_body(ret_ref, owner_ref, pos_ref, pred_ref, weighted_ref, right_ref, back):
    chunks = owner_ref.shape[0]
    tiles = chunks // 8
    exps = right_ref.shape[0]
    rows = pred_ref.shape[1]
    width = rows // exps
    owners = [owner_ref[8 * d : 8 * d + 8, :] for d in range(tiles)]
    places = [pos_ref[8 * d : 8 * d + 8, :] for d in range(tiles)]

    def step(o, found):
        found = list(found)
        table = [ret_ref[pl.ds(2 * o + c, 1), :] for c in range(2)]
        for d in range(tiles):
            hit = owners[d] == o
            for c in range(2):
                found[2 * d + c] = jnp.where(hit, lane_gather(table[c], places[d]), found[2 * d + c])
        return tuple(found)

    found = lax.fori_loop(0, LANES, step, (jnp.zeros((8, LANES), F32),) * (2 * tiles), unroll=8)
    for d in range(tiles):
        for c in range(2):
            for s in range(8):
                r = 8 * d + s
                back[c : c + 1, r * LANES : (r + 1) * LANES] = found[2 * d + c][s : s + 1]
    for e in range(exps):
        at = slice(e * width, (e + 1) * width)
        residual = (back[:, at] - pred_ref[:, at]).astype(BF16)
        right_ref[e] = lax.dot_general(residual, weighted_ref[:, at], NT, preferred_element_type=F32)


def right_sides(ret, owner, pos, pred, weighted, exps):
    terms, rows = weighted.shape
    return call(
        right_body,
        jax.ShapeDtypeStruct((exps, 2, terms), F32),
        (pltpu.VMEM((2, rows), F32),),
        flops=2 * 16 * weighted.size,
        size=2 * weighted.size,
    )(ret, owner, pos, pred, weighted)


def gram_body(k, design_ref, weight_ref, mask_ref, gram_ref, weighted_ref):
    terms = design_ref.shape[0]
    rest = terms - LANES
    design = design_ref[...]
    weight = weight_ref[...] * mask_ref[k : k + 1, :].astype(F32)
    weighted = (design.astype(F32) * weight).astype(BF16)
    weighted_ref[...] = weighted
    gram = 0.5 * lax.dot_general(
        jnp.concatenate([weighted, design], axis=1),
        jnp.concatenate([design, weighted], axis=1),
        NT,
        preferred_element_type=F32,
    )
    gram_ref[0, :terms, :] = gram[:, :LANES]
    gram_ref[0, terms:, :] = jnp.zeros((rest, LANES), F32)
    gram_ref[0, terms:, :rest] = gram[LANES:, LANES:]


def gram(design, weight, mask, k, exps):
    terms, rows = design.shape
    width = rows // exps
    packed = 2 * terms - LANES
    return pl.pallas_call(
        functools.partial(gram_body, k),
        grid=(exps,),
        in_specs=[
            pl.BlockSpec((terms, width), lambda e: (0, e)),
            pl.BlockSpec((1, width), lambda e: (0, e)),
            pl.BlockSpec((2, width), lambda e: (0, e)),
        ],
        out_specs=[
            pl.BlockSpec((1, packed, LANES), lambda e: (e, 0, 0)),
            pl.BlockSpec((terms, width), lambda e: (0, e)),
        ],
        out_shape=(jax.ShapeDtypeStruct((exps, packed, LANES), F32), jax.ShapeDtypeStruct(design.shape, BF16)),
        cost_estimate=pl.CostEstimate(
            flops=4 * terms * design.size, bytes_accessed=4 * design.size, transcendentals=0
        ),
    )(design, weight, mask)


def sweep_block(mat, k, tile, terms):
    base = k * 8 - tile * LANES
    sub = iota((8, LANES), 0)
    lane = iota((8, LANES), 1)
    at = pl.ds(pl.multiple_of(k * 8, 8), 8)
    panel = [mat[at, t * LANES : (t + 1) * LANES] for t in range(2)]
    before = list(panel)
    index = jnp.zeros((8, LANES), jnp.int32) + base
    cols = [jnp.take_along_axis(panel[tile], index + j, axis=1, mode="promise_in_bounds") for j in range(8)]
    for j in range(8):
        inverse = 1.0 / jnp.broadcast_to(cols[j][j : j + 1], (8, LANES))
        unit = jnp.where(sub == j, 1.0, 0.0)
        panel[tile] = jnp.where(lane == base + j, unit, panel[tile])
        mine = sub == j

        def sweep(x):
            row = jnp.broadcast_to(x[j : j + 1], (8, LANES)) * inverse
            return jnp.where(mine, row, x - cols[j] * row)

        for m in range(j + 1, 8):
            cols[m] = sweep(cols[m])
        panel = [sweep(x) for x in panel]
    inside = (lane >= base) & (lane < base + 8)
    swept = list(panel)
    swept[tile] = jnp.where(inside, -panel[tile], panel[tile])
    outer = list(panel)
    outer[tile] = jnp.where(inside, 0.0, panel[tile])
    unit = [jnp.zeros((8, LANES), F32)] * 2
    unit[tile] = jnp.where(lane == base + sub, -1.0, 0.0)
    wide = [jnp.concatenate(x, axis=1) for x in (before, outer, unit, swept)]
    r, p, s = pieces(wide[0]), pieces(wide[1]), pieces(wide[1])
    left = jnp.concatenate([r[0], r[0], r[0], r[1], r[1], r[2], s[0], s[1], s[2], s[2] * 0.0], axis=0).astype(BF16)
    right = jnp.concatenate([p[0], p[1], p[2], p[0], p[1], p[0], wide[2], wide[2], wide[2], wide[2] * 0.0], axis=0).astype(BF16)
    change = lax.dot_general(left, right, TN, preferred_element_type=F32)
    keep = jnp.where((iota((1, 2 * LANES), 1) >= k * 8) & (iota((1, 2 * LANES), 1) < k * 8 + 8), 0.0, 1.0)
    mat[...] = mat[...] * keep - change[:terms]
    mat[at, :] = wide[3]


def invert_body(gram_ref, out_ref, mat):
    terms = out_ref.shape[0]
    rest = terms - LANES
    total = gram_ref[0]
    for s in range(1, gram_ref.shape[0]):
        total = total + gram_ref[s]
    square = jnp.concatenate([total[LANES:terms], jnp.zeros((LANES - rest, LANES), F32)], axis=0)
    mat[:, :LANES] = total[:terms]
    mat[:LANES, LANES:] = square.T
    mat[LANES:, LANES:] = total[terms:]
    mat[...] = mat[...] + jnp.where(iota((terms, 2 * LANES), 0) == iota((terms, 2 * LANES), 1), RIDGE, 0.0)

    def first(k, carry):
        sweep_block(mat, k, 0, terms)
        return carry

    def second(k, carry):
        sweep_block(mat, k, 1, terms)
        return carry

    lax.fori_loop(0, LANES // 8, first, 0)
    lax.fori_loop(LANES // 8, terms // 8, second, 0)
    out_ref[...] = -mat[...]


def invert(grams, terms):
    return call(
        invert_body,
        jax.ShapeDtypeStruct((terms, 2 * LANES), F32),
        (pltpu.VMEM((terms, 2 * LANES), F32),),
        flops=2 * 25 * 80 * 256 * 256 * 10,
        size=grams.size * 4,
    )(grams)


def solve_body(right_ref, inverse_ref, out_ref):
    terms = inverse_ref.shape[0]
    right = right_ref[0]
    for s in range(1, right_ref.shape[0]):
        right = right + right_ref[s]
    update = jnp.dot(right, inverse_ref[...], precision=lax.Precision.HIGHEST, preferred_element_type=F32)
    for s in range(right_ref.shape[0]):
        out_ref[s] = update[:, :terms]


def solve(right, inverse):
    return call(solve_body, jax.ShapeDtypeStruct(right.shape, F32), flops=10**6, size=inverse.size * 4)(right, inverse)


def on_device(design, det_weight, outlier_mask, star_owner, star_slot, coef_init, star_ref, star_prior):
    everyone = ("pix", "exp")
    peers = lax.axis_size(everyone)
    terms, rows = design.shape
    exps = coef_init.shape[0]
    cap = 2 * rows // peers
    owner = star_owner.reshape(rows // LANES, LANES)
    slot = star_slot.reshape(rows // LANES, LANES)
    weight_rows = det_weight.reshape(rows // LANES, LANES)
    weight_line = det_weight.reshape(1, rows)
    prior = star_prior.reshape(star_prior.shape[0] // LANES, LANES)

    def exchange(x):
        y = lax.all_to_all(x.reshape(peers, -1, LANES), everyone, split_axis=0, concat_axis=0, tiled=True)
        return y.reshape(x.shape)

    def over_pix(x):
        return lax.all_to_all(x, "pix", split_axis=0, concat_axis=0, tiled=True)

    pos, row, lane = route(owner)
    gram_0, weighted_0 = gram(design, weight_line, outlier_mask, 0, exps)
    gram_1, weighted_1 = gram(design, weight_line, outlier_mask, 1, exps)
    pred, pay = place_first(coef_init, design, row, lane, slot, weight_rows, outlier_mask, cap)
    ret, ids, later = owner_first(exchange(pay), star_ref, prior, cap)
    right = right_sides(exchange(ret), owner, pos, pred, weighted_0, exps)
    inverse_0 = invert(over_pix(gram_0), terms)
    inverse_1 = invert(over_pix(gram_1), terms)
    upd = over_pix(solve(over_pix(right), inverse_0))
    pred, pay, coef = place_next(coef_init, upd, design, row, lane, cap)
    ret, means = owner_next(exchange(pay), ids, later, star_ref, prior, cap)
    right = right_sides(exchange(ret), owner, pos, pred, weighted_1, exps)
    upd = over_pix(solve(over_pix(right), inverse_1))
    return (coef + upd, means)


def solution(mesh):
    placed = (
        P(None, ("pix", "exp")),
        P(("pix", "exp")),
        P(None, ("pix", "exp")),
        P(("pix", "exp"), None),
        P(("pix", "exp")),
        P("exp", None, None),
        P(None, ("pix", "exp")),
        P(("pix", "exp")),
    )
    return jax.shard_map(
        on_device,
        mesh=mesh,
        in_specs=placed,
        out_specs=(P("exp", None, None), P(None, ("pix", "exp"))),
        check_vma=False,
    )
```

time: 389 us -> 200 us (0.51); the launches traced: 383 us -> 199 us
  other arithmetic: 116 us -> 0.62 us
  matrix products: 97.4 us -> 0 us
  Pallas kernels: 0 us -> 90.5 us
  between operations: 17.7 us -> 0.67 us
  blocking collectives: 73.6 us -> 57.7 us
  local copies, waits for them, and re-layouts: 16.3 us -> 2.52 us
  starting transfers between devices: 37.3 us -> 25.6 us
    another operation x25 -> x0, other arithmetic: 101 us -> none  [the longest x14 59.3 us: solve_blocks(): factor = jnp.linalg.cholesky(gram_block + RIDGE * identity)]
    pallas_call x0 -> x13, Pallas kernels: none -> 90.5 us  [the longest x2 22.7 us: invert(): call(invert_body, jax.ShapeDtypeStruct((terms, 2 * LANES), F32), (pltpu.V...]
    dot_general x39 -> x0, matrix products: 76.1 us -> none  [the longest x16 35.7 us: lookup(): jnp.dot(star_means, star_table(id_block, star_count).T, precision=highest)]
    all_to_all x0 -> x4, blocking collectives: none -> 57.7 us  [the longest x2 38.6 us: exchange(): lax.all_to_all(x.reshape(peers, -1, LANES), everyone, split_axis=0, conca...]
    unnamed x2 -> x0, blocking collectives: 44.2 us -> none
    all_gather x2 -> x0, blocking collectives: 29.3 us -> none  [on_device(): lax.all_gather(own_maps + solve_blocks(gram_part, right_part), 'pix', axi...]
    unnamed x4 -> x0, matrix products: 18.4 us -> none
    all_to_all x5 -> x6, starting transfers between devices: 36.5 us -> 25.6 us  [the longest x4 16.9 us: over_pix(): return lax.all_to_all(x, 'pix', split_axis=0, concat_axis=0, tiled=True)]
  transfers between devices with their start and end apart: 7 -> 6, of which waited for: 3 -> 4; matrix products, arithmetic and copies ran while one was open for 29% -> 0% of each run, Pallas kernels for 0% -> 27%
where the time goes in v1:
time: 200 us; the launch traced here: 199 us
  Pallas kernels  90.5 us (45%)
  blocking collectives  57.7 us (29%)
  starting transfers between devices  25.6 us (13%)
  waiting for transfers between devices  21.2 us (11%)
  local copies, waits for them, and re-layouts  2.52 us (1%)
    all_to_all x2, blocking collectives, exchange(): lax.all_to_all(x.reshape(peers, -1, LANES), everyone, split_axis=0, conca...  38.6 us
    pallas_call x2, Pallas kernels, invert(): call(invert_body, jax.ShapeDtypeStruct((terms, 2 * LANES), F32), (pltpu.V...  22.7 us
    all_to_all x2, blocking collectives, over_pix(): return lax.all_to_all(x, 'pix', split_axis=0, concat_axis=0, tiled=True)  19 us
    all_to_all x4, starting transfers between devices, over_pix(): return lax.all_to_all(x, 'pix', split_axis=0, concat_axis=0, tiled=True)  16.9 us
    pallas_call x2, Pallas kernels, right_sides(): call(right_body, jax.ShapeDtypeStruct((exps, 2, terms), F32), (pltpu.VMEM...  16.1 us
    all_to_all x4, waiting for transfers between devices, over_pix(): return lax.all_to_all(x, 'pix', split_axis=0, concat_axis=0, tiled=True)  15.3 us
    pallas_call x2, Pallas kernels, gram(): pl.pallas_call(functools.partial(gram_body, k), grid=(exps,), in_specs=[p...  13.9 us
    pallas_call x1, Pallas kernels, place_first(): call(functools.partial(place_body, cap, True), (jax.ShapeDtypeStruct((2,...  8.78 us
  transfers between devices with their start and end apart: 6, of which 4 were waited for; matrix products, arithmetic and copies ran while one was open for 0% of the time, Pallas kernels for 27%

profile of v1, /device:TPU:1, one launch (start us, length us, event | category | flops | bytes accessed | tf_op | source)
XLA Modules:
  0.0 198.7 jit_solution(18018218007243175034)
XLA Ops:
  0.6 5.6 %shard_map.95 = (s32[48,128]{1,0:T(8,128)}, s32[128,128]{1,0:T(8,128)}, s32[128,128]{1,0:T(8,128)}) custom-call(s32[48,128]{1,0:T(8,128)} %bitcast.21), custom_call_target="tpu_custom_call" | custom-call | flops 805306368 | bytes 49152 | tf_op jit(solution)/shard_map/pallas_call | solution.py:66
  6.2 8.8 %shard_map.96 = (f32[2,6144]{1,0:T(2,128)}, f32[512,128]{1,0:T(8,128)}) custom-call(f32[8,2,200]{2,1,0:T(2,128)} %refs_0_.3, bf16[200,6144]{1,0:T(8,128)(2,1)} %design_ref.3, s32[128,128]{1,0:T(8,128)} %get-tuple-element.19.refs_2_.refs_3_, s32[128,128]{1,0:T(8,128)} %get-tuple-element.20.refs_3_.refs_4_, s32[48,128]{1,0:T(8,128)} %bitcast.24, ...), custom_call_target="tpu_custom_call" | custom-call | flops 39321600 | bytes 2457600 | tf_op jit(solution)/shard_map/pallas_call | solution.py:132
  15.0 22.5 %all_to_all.50 = f32[128,4,128]{2,1,0:T(4,128)} all-to-all(f32[128,4,128]{2,1,0:T(4,128)} %bitcast.16), channel_id=1, replica_groups=mesh['pix'=8,'exp'=16] {'pix','exp'}, dimensions={0} | all-to-all | bytes 524288 | tf_op jit(solution)/shard_map/all_to_all | solution.py:449
  37.5 7.7 %shard_map.97 = (f32[256,128]{1,0:T(8,128)}, s32[128,128]{1,0:T(8,128)}, f32[128,128]{1,0:T(8,128)}) custom-call(f32[512,128]{1,0:T(8,128)} %bitcast.15, f32[2,768]{1,0:T(2,128)} %refs_3_.1, f32[6,128]{1,0:T(8,128)} %bitcast.28), custom_call_target="tpu_custom_call" | custom-call | flops 301989888 | bytes 262144 | tf_op jit(solution)/shard_map/pallas_call | solution.py:243
  45.2 4.5 %all-to-all-start.1 = ((f32[128,2,128]{2,1,0:T(2,128)}), f32[128,2,128]{2,1,0:T(2,128)S(1)}, u32[]{:S(2)}, u32[]{:S(2)}) async-start(f32[128,2,128]{2,1,0:T(2,128)} %bitcast.18), calls=%async_computation.1 | async-start | bytes 262144 | tf_op jit(solution)/shard_map/all_to_all | solution.py:449
  49.6 7.0 %shard_map.98 = (f32[8,272,128]{2,1,0:T(8,128)}, bf16[200,6144]{1,0:T(8,128)(2,1)}) custom-call(bf16[200,6144]{1,0:T(8,128)(2,1)} %design_ref.3, f32[1,6144]{1,0:T(1,128)} %bitcast.26, s32[2,6144]{1,0:T(2,128)} %mask_ref.3), custom_call_target="tpu_custom_call" | custom-call | flops 983040000 | bytes 4915200 | tf_op jit(solution)/shard_map/pallas_call | solution.py:329
  60.2 4.2 %all-to-all-start.3 = ((f32[8,272,128]{2,1,0:T(8,128)}), f32[8,272,128]{2,1,0:T(8,128)S(1)}, u32[]{:S(2)}, u32[]{:S(2)}) async-start(f32[8,272,128]{2,1,0:T(8,128)} %get-tuple-element.26), calls=%async_computation.3 | async-start | bytes 2228224 | tf_op jit(solution)/shard_map/all_to_all | solution.py:453
  64.4 8.1 %shard_map.99 = f32[8,2,200]{2,1,0:T(2,128)} custom-call(f32[256,128]{1,0:T(8,128)} %bitcast.13, s32[48,128]{1,0:T(8,128)} %bitcast.22, s32[48,128]{1,0:T(8,128)} %get-tuple-element.23.pos_ref, f32[2,6144]{1,0:T(2,128)} %get-tuple-element.24.pred_ref, bf16[200,6144]{1,0:T(8,128)(2,1)} %get-tuple-element.25.weighted_ref), custom_call_target="tpu_custom_call" | custom-call | flops 39321600 | bytes 2457600 | tf_op jit(solution)/shard_map/pallas_call | solution.py:298
  72.5 7.6 %all-to-all-done.3.gram_ref = f32[8,272,128]{2,1,0:T(8,128)S(1)} async-done(((f32[8,272,128]{2,1,0:T(8,128)}), f32[8,272,128]{2,1,0:T(8,128)S(1)}, u32[]{:S(2)}, u32[]{:S(2)}) %all-to-all-start.3) | async-done | bytes 1114144 | tf_op jit(solution)/shard_map/all_to_all | solution.py:453
  80.1 4.2 %all-to-all-start.2 = ((f32[8,2,200]{2,1,0:T(2,128)}), f32[8,2,200]{2,1,0:T(2,128)S(1)}, u32[]{:S(2)}, u32[]{:S(2)}) async-start(f32[8,2,200]{2,1,0:T(2,128)} %shard_map.99), calls=%async_computation.2 | async-start | bytes 32768 | tf_op jit(solution)/shard_map/all_to_all | solution.py:453
  84.3 11.3 %shard_map.100.inverse_ref = f32[200,256]{1,0:T(8,128)} custom-call(f32[8,272,128]{2,1,0:T(8,128)} %copy-done), custom_call_target="tpu_custom_call" | custom-call | flops 2621440000 | bytes 1114112 | tf_op jit(solution)/shard_map/pallas_call | solution.py:413
  98.0 9.6 %all_to_all.51.refs_1_ = f32[8,2,200]{2,1,0:T(2,128)} all-to-all(f32[8,2,200]{2,1,0:T(2,128)} %shard_map.101), channel_id=1, replica_groups=mesh['pix'=8,'exp'=16] {'pix'}, dimensions={0} | all-to-all | bytes 25600 | tf_op jit(solution)/shard_map/all_to_all | solution.py:453
  107.6 5.6 %shard_map.102 = (f32[2,6144]{1,0:T(2,128)}, f32[256,128]{1,0:T(8,128)}, f32[8,2,200]{2,1,0:T(2,128)}) custom-call(f32[8,2,200]{2,1,0:T(2,128)} %refs_0_.3, f32[8,2,200]{2,1,0:T(2,128)} %all_to_all.51.refs_1_, bf16[200,6144]{1,0:T(8,128)(2,1)} %design_ref.3, s32[128,128]{1,0:T(8,128)} %get-tuple-element.19.refs_2_.refs_3_, ...), custom_call_target="tpu_custom_call" | custom-call | flops 39321600 | bytes 2457600 | tf_op jit(solution)/shard_map/pallas_call | solution.py:143
  113.2 16.1 %all_to_all.52 = f32[128,2,128]{2,1,0:T(2,128)} all-to-all(f32[128,2,128]{2,1,0:T(2,128)} %bitcast.19), channel_id=1, replica_groups=mesh['pix'=8,'exp'=16] {'pix','exp'}, dimensions={0} | all-to-all | bytes 262144 | tf_op jit(solution)/shard_map/all_to_all | solution.py:449
  129.4 6.6 %shard_map.103 = (f32[256,128]{1,0:T(8,128)}, f32[2,768]{1,0:T(2,128)}) custom-call(f32[256,128]{1,0:T(8,128)} %bitcast.20, s32[128,128]{1,0:T(8,128)} %get-tuple-element.29.refs_1_, f32[128,128]{1,0:T(8,128)} %get-tuple-element.30.refs_2_, f32[2,768]{1,0:T(2,128)} %refs_3_.1, f32[6,128]{1,0:T(8,128)} %bitcast.29), custom_call_target="tpu_custom_call" | custom-call | flops 301989888 | bytes 131072 | tf_op jit(solution)/shard_map/pallas_call | solution.py:257
  136.0 4.2 %all-to-all-start.6 = ((f32[128,2,128]{2,1,0:T(2,128)}), f32[128,2,128]{2,1,0:T(2,128)S(1)}, u32[]{:S(2)}, u32[]{:S(2)}) async-start(f32[128,2,128]{2,1,0:T(2,128)} %bitcast.17), calls=%async_computation.6 | async-start | bytes 262144 | tf_op jit(solution)/shard_map/all_to_all | solution.py:449
  140.2 7.0 %shard_map.104 = (f32[8,272,128]{2,1,0:T(8,128)}, bf16[200,6144]{1,0:T(8,128)(2,1)}) custom-call(bf16[200,6144]{1,0:T(8,128)(2,1)} %design_ref.3, f32[1,6144]{1,0:T(1,128)} %bitcast.27, s32[2,6144]{1,0:T(2,128)} %mask_ref.3), custom_call_target="tpu_custom_call" | custom-call | flops 983040000 | bytes 4915200 | tf_op jit(solution)/shard_map/pallas_call | solution.py:329
  147.2 2.9 %all-to-all-done.6 = f32[128,2,128]{2,1,0:T(2,128)S(1)} async-done(((f32[128,2,128]{2,1,0:T(2,128)}), f32[128,2,128]{2,1,0:T(2,128)S(1)}, u32[]{:S(2)}, u32[]{:S(2)}) %all-to-all-start.6) | async-done | bytes 131104 | tf_op jit(solution)/shard_map/all_to_all | solution.py:449
  150.8 4.2 %all-to-all-start.8 = ((f32[8,272,128]{2,1,0:T(8,128)}), f32[8,272,128]{2,1,0:T(8,128)S(1)}, u32[]{:S(2)}, u32[]{:S(2)}) async-start(f32[8,272,128]{2,1,0:T(8,128)} %get-tuple-element.34), calls=%async_computation.8 | async-start | bytes 2228224 | tf_op jit(solution)/shard_map/all_to_all | solution.py:453
  155.0 8.0 %shard_map.105 = f32[8,2,200]{2,1,0:T(2,128)} custom-call(f32[256,128]{1,0:T(8,128)} %bitcast.14, s32[48,128]{1,0:T(8,128)} %bitcast.23, s32[48,128]{1,0:T(8,128)} %get-tuple-element.23.pos_ref, f32[2,6144]{1,0:T(2,128)} %get-tuple-element.32.pred_ref, bf16[200,6144]{1,0:T(8,128)(2,1)} %get-tuple-element.33.weighted_ref), custom_call_target="tpu_custom_call" | custom-call | flops 39321600 | bytes 2457600 | tf_op jit(solution)/shard_map/pallas_call | solution.py:298
  163.1 7.7 %all-to-all-done.8.gram_ref = f32[8,272,128]{2,1,0:T(8,128)S(1)} async-done(((f32[8,272,128]{2,1,0:T(8,128)}), f32[8,272,128]{2,1,0:T(8,128)S(1)}, u32[]{:S(2)}, u32[]{:S(2)}) %all-to-all-start.8) | async-done | bytes 1114144 | tf_op jit(solution)/shard_map/all_to_all | solution.py:453
  170.7 4.2 %all-to-all-start.7 = ((f32[8,2,200]{2,1,0:T(2,128)}), f32[8,2,200]{2,1,0:T(2,128)S(1)}, u32[]{:S(2)}, u32[]{:S(2)}) async-start(f32[8,2,200]{2,1,0:T(2,128)} %shard_map.105), calls=%async_computation.7 | async-start | bytes 32768 | tf_op jit(solution)/shard_map/all_to_all | solution.py:453
  174.9 11.4 %shard_map.106.inverse_ref = f32[200,256]{1,0:T(8,128)} custom-call(f32[8,272,128]{2,1,0:T(8,128)} %copy-done.1), custom_call_target="tpu_custom_call" | custom-call | flops 2621440000 | bytes 1114112 | tf_op jit(solution)/shard_map/pallas_call | solution.py:413
  188.6 9.5 %all_to_all.53 = f32[8,2,200]{2,1,0:T(2,128)S(1)} all-to-all(f32[8,2,200]{2,1,0:T(2,128)} %shard_map.107), channel_id=1, replica_groups=mesh['pix'=8,'exp'=16] {'pix'}, dimensions={0} | all-to-all | bytes 25600 | tf_op jit(solution)/shard_map/all_to_all | solution.py:453
  (20 shorter events, 9.6 us)
Async XLA Ops:
  45.2 14.4 %all-to-all-start.1 = ((f32[128,2,128]{2,1,0:T(2,128)}), f32[128,2,128]{2,1,0:T(2,128)S(1)}, u32[]{:S(2)}, u32[]{:S(2)}) async-start(f32[128,2,128]{2,1,0:T(2,128)} %bitcast.18), calls=%async_computation.1 | async-start | bytes 262144 | tf_op jit(solution)/shard_map/all_to_all | solution.py:449
  59.5 0.7 copy-start.2
  60.2 19.9 %all-to-all-start.3 = ((f32[8,272,128]{2,1,0:T(8,128)}), f32[8,272,128]{2,1,0:T(8,128)S(1)}, u32[]{:S(2)}, u32[]{:S(2)}) async-start(f32[8,272,128]{2,1,0:T(8,128)} %get-tuple-element.26), calls=%async_computation.3 | async-start | bytes 2228224 | tf_op jit(solution)/shard_map/all_to_all | solution.py:453
  80.1 4.2 %copy-start = (f32[8,272,128]{2,1,0:T(8,128)}, f32[8,272,128]{2,1,0:T(8,128)S(1)}, u32[]{:S(2)}) copy-start(f32[8,272,128]{2,1,0:T(8,128)S(1)} %all-to-all-done.3.gram_ref) | copy-start | bytes 3342340
  80.1 15.5 %all-to-all-start.2 = ((f32[8,2,200]{2,1,0:T(2,128)}), f32[8,2,200]{2,1,0:T(2,128)S(1)}, u32[]{:S(2)}, u32[]{:S(2)}) async-start(f32[8,2,200]{2,1,0:T(2,128)} %shard_map.99), calls=%async_computation.2 | async-start | bytes 32768 | tf_op jit(solution)/shard_map/all_to_all | solution.py:453
  95.7 0.6 copy-start.4
  136.0 14.1 %all-to-all-start.6 = ((f32[128,2,128]{2,1,0:T(2,128)}), f32[128,2,128]{2,1,0:T(2,128)S(1)}, u32[]{:S(2)}, u32[]{:S(2)}) async-start(f32[128,2,128]{2,1,0:T(2,128)} %bitcast.17), calls=%async_computation.6 | async-start | bytes 262144 | tf_op jit(solution)/shard_map/all_to_all | solution.py:449
  150.1 0.7 copy-start.3
  150.8 19.9 %all-to-all-start.8 = ((f32[8,272,128]{2,1,0:T(8,128)}), f32[8,272,128]{2,1,0:T(8,128)S(1)}, u32[]{:S(2)}, u32[]{:S(2)}) async-start(f32[8,272,128]{2,1,0:T(8,128)} %get-tuple-element.34), calls=%async_computation.8 | async-start | bytes 2228224 | tf_op jit(solution)/shard_map/all_to_all | solution.py:453
  170.7 4.2 %copy-start.1 = (f32[8,272,128]{2,1,0:T(8,128)}, f32[8,272,128]{2,1,0:T(8,128)S(1)}, u32[]{:S(2)}) copy-start(f32[8,272,128]{2,1,0:T(8,128)S(1)} %all-to-all-done.8.gram_ref) | copy-start | bytes 3342340
  170.7 15.6 %all-to-all-start.7 = ((f32[8,2,200]{2,1,0:T(2,128)}), f32[8,2,200]{2,1,0:T(2,128)S(1)}, u32[]{:S(2)}, u32[]{:S(2)}) async-start(f32[8,2,200]{2,1,0:T(2,128)} %shard_map.105), calls=%async_computation.7 | async-start | bytes 32768 | tf_op jit(solution)/shard_map/all_to_all | solution.py:453
  174.9 23.2 %copy-start.6 = (f32[8,2,200]{2,1,0:T(2,128)S(1)}, f32[8,2,200]{2,1,0:T(2,128)}, u32[]{:S(2)}) copy-start(f32[8,2,200]{2,1,0:T(2,128)} %get-tuple-element.27) | copy-start | bytes 38404
  186.3 0.6 copy-start.5

commit v2 on v1

--- a/solution.py
+++ b/solution.py
@@ -7,11 +7,13 @@
 from jax.experimental.pallas import tpu as pltpu
 from jax.sharding import PartitionSpec as P
 
-ITERS = 2
+
 RIDGE = 0.5
 LANES = 128
 F32 = jnp.float32
 BF16 = jnp.bfloat16
+GRANT = 16 << 20
+FLOPS_PER_US = 10**9
 NT = (((1,), (1,)), ((), ()))
 TN = (((0,), (0,)), ((), ()))
 
@@ -25,59 +27,98 @@
     return jnp.take_along_axis(table, index, axis=1, mode="promise_in_bounds")
 
 
-def call(body, out_shape, scratch=(), flops=0, size=0):
+def call(body, out_shape, scratch=(), micros=1, size=0):
     return pl.pallas_call(
         body,
         out_shape=out_shape,
         scratch_shapes=list(scratch),
-        cost_estimate=pl.CostEstimate(flops=flops, bytes_accessed=size, transcendentals=0),
+        compiler_params=pltpu.CompilerParams(vmem_limit_bytes=GRANT),
+        cost_estimate=pl.CostEstimate(flops=micros * FLOPS_PER_US, bytes_accessed=size, transcendentals=0),
     )
 
 
-def route_body(owner_ref, pos_ref, row_ref, lane_ref, hot_ref, place_ref):
+def route_body(owner_ref, order_ref, row_ref, lane_ref, start_ref, count_ref, line_ref, hot_ref, left_ref, right_ref):
     chunks = owner_ref.shape[0]
     sub = iota((LANES, LANES), 0)
     lane = iota((LANES, LANES), 1)
     wide_sub, wide_lane = iota((LANES, 2 * LANES), 0), iota((LANES, 2 * LANES), 1)
     prefix = jnp.where((wide_sub < wide_lane) | (wide_lane >= LANES), 1.0, 0.0).astype(BF16)
-    lane_f = lane.astype(F32)
-
-    def step(r, base):
+
+    def rank(r, base):
         at = pl.ds(pl.multiple_of(r * LANES, LANES), LANES)
         hot = jnp.where(owner_ref[pl.ds(r, 1), :] == sub, 1.0, 0.0)
-        counts = jnp.dot(hot.astype(BF16), prefix, preferred_element_type=F32)
-        pos = jnp.sum(hot * (counts[:, :LANES] + base), axis=0, keepdims=True).astype(jnp.int32)
-        pos_ref[pl.ds(r, 1), :] = pos
-        place_ref[:, at] = jnp.where(pos == sub, 1.0, 0.0).astype(BF16)
-        hot_ref[:LANES, at] = (hot * (r + 1).astype(F32)).astype(BF16)
-        hot_ref[LANES:, at] = (hot * lane_f).astype(BF16)
+        narrow = hot.astype(BF16)
+        hot_ref[:, at] = narrow
+        counts = jnp.dot(narrow, prefix, preferred_element_type=F32)
+        order_ref[pl.ds(r, 1), :] = jnp.sum(hot * (counts[:, :LANES] + base), axis=0, keepdims=True).astype(jnp.int32)
         return base + counts[:, LANES:]
 
-    lax.fori_loop(0, chunks, step, jnp.zeros((LANES, LANES), F32), unroll=4)
-    held = lax.dot_general(hot_ref[...], place_ref[...], NT, preferred_element_type=F32)
-    row_ref[...] = held[:LANES].astype(jnp.int32) - 1
-    lane_ref[...] = held[LANES:].astype(jnp.int32)
+    counts = lax.fori_loop(0, chunks, rank, jnp.zeros((LANES, LANES), F32), unroll=4)
+    high = jnp.floor(counts * (1.0 / LANES))
+    split = jnp.concatenate([high, counts - high * LANES], axis=1).astype(BF16)
+    below = jnp.where(lane < sub, 1.0, 0.0).astype(BF16)
+    starts = jnp.dot(below, split, preferred_element_type=F32)
+    start_ref[...] = (starts[:, :LANES] * LANES + starts[:, LANES:]).astype(jnp.int32)
+    count_ref[...] = counts.astype(jnp.int32)
+    line = jnp.sum(jnp.where(sub < lane, counts, 0.0), axis=0, keepdims=True)
+    line8 = jnp.broadcast_to(line, (8, LANES))
+    line_ref[...] = line8.astype(jnp.int32)
+    high8 = jnp.floor(line8 * (1.0 / LANES))
+    first = jnp.where(iota((8, LANES), 0) == 0, high8, line8 - high8 * LANES).astype(BF16)
+    begin = jnp.dot(first, hot_ref[...], preferred_element_type=F32)
+    sub_rows, lane_line = iota((chunks, LANES), 0), iota((1, LANES), 1).astype(F32)
+    for r in range(chunks):
+        at = slice(r * LANES, (r + 1) * LANES)
+        place = order_ref[r : r + 1, :] + (begin[0:1, at] * LANES + begin[1:2, at]).astype(jnp.int32)
+        order_ref[r : r + 1, :] = place
+        hit = jnp.where((place >> 7) == sub_rows, 1.0, 0.0)
+        left_ref[:chunks, at] = (hit * float(r)).astype(BF16)
+        left_ref[chunks:, at] = (hit * lane_line).astype(BF16)
+        right_ref[:, at] = jnp.where((place & 127) == sub, 1.0, 0.0).astype(BF16)
+    held = lax.dot_general(left_ref[...], right_ref[...], NT, preferred_element_type=F32)
+    row_ref[...] = held[:chunks].astype(jnp.int32)
+    lane_ref[...] = held[chunks:].astype(jnp.int32)
 
 
 def route(owner):
     chunks = owner.shape[0]
     rows = chunks * LANES
+    line = jax.ShapeDtypeStruct(owner.shape, jnp.int32)
     plane = jax.ShapeDtypeStruct((LANES, LANES), jnp.int32)
     return call(
         route_body,
-        (jax.ShapeDtypeStruct(owner.shape, jnp.int32), plane, plane),
-        (pltpu.VMEM((2 * LANES, rows), BF16), pltpu.VMEM((LANES, rows), BF16)),
-        flops=2 * 512 * LANES * rows,
+        (line, line, line, plane, plane, jax.ShapeDtypeStruct((8, LANES), jnp.int32)),
+        (pltpu.VMEM((LANES, rows), BF16), pltpu.VMEM((2 * chunks, rows), BF16), pltpu.VMEM((LANES, rows), BF16)),
+        micros=4,
         size=rows * 8,
     )(owner)
 
 
+def pieces(x):
+    a = x.astype(BF16).astype(F32)
+    b = (x - a).astype(BF16).astype(F32)
+    c = ((x - a) - b).astype(BF16).astype(F32)
+    return (a, b, c)
+
+
+def lookup_rows(table, base, chunks, row, lane, values):
+    found = [jnp.zeros((8, LANES), F32)] * values
+    for r in range(chunks):
+        hit = row == r
+        for v in range(values):
+            at = base[v] + r
+            found[v] = jnp.where(hit, lane_gather(table[at : at + 1, :], lane), found[v])
+    return found
+
+
 def place_body(cap, first, *refs):
     if first:
-        coef_ref, design_ref, row_ref, lane_ref, slot_ref, weight_ref, mask_ref, pred_ref, pay_ref, vals = refs
+        (coef_ref, design_ref, row_ref, lane_ref, start_ref, count_ref, slot_ref, weight_ref, mask_ref) = refs[:9]
+        pred_ref, pay_ref, vals, dense, spread = refs[9:]
         coef = coef_ref[...]
     else:
-        coef_ref, upd_ref, design_ref, row_ref, lane_ref, pred_ref, pay_ref, new_ref, vals = refs
+        coef_ref, upd_ref, design_ref, row_ref, lane_ref, start_ref, count_ref = refs[:7]
+        pred_ref, pay_ref, new_ref, vals, dense, spread = refs[7:]
         coef = coef_ref[...] + upd_ref[...]
         new_ref[...] = coef
     exps = coef.shape[0]
@@ -105,15 +146,38 @@
     width_out = 4 if first else 2
     lane8 = iota((8, LANES), 1)
 
+    def gather(d, carry):
+        at = pl.ds(pl.multiple_of(d * 8, 8), 8)
+        found = lookup_rows(vals, [v * chunks for v in range(values)], chunks, row_ref[at, :], lane_ref[at, :], values)
+        for v in range(values):
+            for k, piece in enumerate(pieces(found[v])):
+                dense[at, (3 * v + k) * LANES : (3 * v + k + 1) * LANES] = piece
+        return carry
+
+    lax.fori_loop(0, chunks // 8, gather, 0, unroll=2)
+    row_of = start_ref[...] >> 7
+    column = iota((LANES, chunks), 1)
+    pick = jnp.concatenate(
+        [jnp.where(row_of[:, :chunks] + k == column, 1.0, 0.0) for k in range(2)], axis=0
+    ).astype(BF16)
+    spread[...] = jnp.dot(pick, dense[...].astype(BF16), preferred_element_type=F32)
+
     def tile(d, carry):
         at = pl.ds(pl.multiple_of(d * 8, 8), 8)
-        source, index = row_ref[at, :], lane_ref[at, :]
-        found = [jnp.zeros((8, LANES), F32)] * values
-        for r in range(chunks):
-            hit = source == r
-            for v in range(values):
-                got = lane_gather(vals[v * chunks + r : v * chunks + r + 1, :], index)
-                found[v] = jnp.where(hit, got, found[v])
+        spot = (start_ref[at, :] & 127) + lane8
+        index, near = spot & 127, spot < LANES
+        held = lane8 < count_ref[at, :]
+        found = []
+        for v in range(values):
+            rows_of = []
+            for k in range(2):
+                part = [
+                    spread[pl.ds(pl.multiple_of(d * 8 + k * LANES, 8), 8), (3 * v + j) * LANES : (3 * v + j + 1) * LANES]
+                    for j in range(3)
+                ]
+                whole = part[0] + (part[1] + part[2])
+                rows_of.append(jnp.take_along_axis(whole, index, axis=1, mode="promise_in_bounds"))
+            found.append(jnp.where(held, jnp.where(near, rows_of[0], rows_of[1]), 0.0))
         if first:
             spare = LANES - cap
             later = found.pop()
@@ -124,21 +188,29 @@
             pay_ref[pl.ds(d * 8 * width_out + v, 8, stride=width_out), :] = found[v]
         return carry
 
-    lax.fori_loop(0, LANES // 8, tile, 0)
-
-
-def place_first(coef, design, row, lane, slot, weight, mask, cap):
+    lax.fori_loop(0, LANES // 8, tile, 0, unroll=2)
+
+
+def place_scratch(values, chunks):
+    return (
+        pltpu.VMEM((values * chunks, LANES), F32),
+        pltpu.VMEM((chunks, 3 * values * LANES), F32),
+        pltpu.VMEM((2 * LANES, 3 * values * LANES), F32),
+    )
+
+
+def place_first(coef, design, row, lane, start, count, slot, weight, mask, cap):
     rows = design.shape[1]
     return call(
         functools.partial(place_body, cap, True),
         (jax.ShapeDtypeStruct((2, rows), F32), jax.ShapeDtypeStruct((4 * LANES, LANES), F32)),
-        (pltpu.VMEM((5 * rows // LANES, LANES), F32),),
-        flops=2 * 16 * design.size,
+        place_scratch(5, rows // LANES),
+        micros=5,
         size=2 * design.size,
-    )(coef, design, row, lane, slot, weight, mask)
-
-
-def place_next(coef, upd, design, row, lane, cap):
+    )(coef, design, row, lane, start, count, slot, weight, mask)
+
+
+def place_next(coef, upd, design, row, lane, start, count, cap):
     rows = design.shape[1]
     return call(
         functools.partial(place_body, cap, False),
@@ -147,17 +219,10 @@
             jax.ShapeDtypeStruct((2 * LANES, LANES), F32),
             jax.ShapeDtypeStruct(coef.shape, F32),
         ),
-        (pltpu.VMEM((2 * rows // LANES, LANES), F32),),
-        flops=2 * 16 * design.size,
+        place_scratch(2, rows // LANES),
+        micros=3,
         size=2 * design.size,
-    )(coef, upd, design, row, lane)
-
-
-def pieces(x):
-    a = x.astype(BF16).astype(F32)
-    b = (x - a).astype(BF16).astype(F32)
-    c = ((x - a) - b).astype(BF16).astype(F32)
-    return (a, b, c)
+    )(coef, upd, design, row, lane, start, count)
 
 
 def owner_body(cap, first, *refs):
@@ -193,7 +258,7 @@
                 parts[3 * v + k, at, :] = piece
         return carry
 
-    lax.fori_loop(0, LANES // 8, split, 0)
+    lax.fori_loop(0, LANES // 8, split, 0, unroll=4)
     group = 8
 
     def accumulate(g, total):
@@ -212,7 +277,7 @@
             jnp.concatenate(left, axis=1), jnp.concatenate(right, axis=1), NT, preferred_element_type=F32
         )
 
-    total = lax.fori_loop(0, LANES // group, accumulate, jnp.zeros((72, LANES), F32))
+    total = lax.fori_loop(0, LANES // group, accumulate, jnp.zeros((72, LANES), F32), unroll=4)
     sums = [total[24 * v : 24 * v + 8] + total[24 * v + 8 : 24 * v + 16] + total[24 * v + 16 : 24 * v + 24] for v in range(3)]
     rows = prior_ref.shape[0]
     means = [[], []]
@@ -236,7 +301,7 @@
             ret_ref[pl.ds(g * 16 + c, 8, stride=2), :] = found
         return carry
 
-    lax.fori_loop(0, LANES // 8, look, 0)
+    lax.fori_loop(0, LANES // 8, look, 0, unroll=4)
 
 
 def owner_first(pay, star_ref, star_prior, cap):
@@ -248,7 +313,7 @@
             jax.ShapeDtypeStruct((LANES, LANES), F32),
         ),
         (pltpu.VMEM((9, LANES, LANES), F32),),
-        flops=2 * 72 * LANES**3,
+        micros=4,
         size=pay.size * 4,
     )(pay, star_ref, star_prior)
 
@@ -258,91 +323,137 @@
         functools.partial(owner_body, cap, False),
         (jax.ShapeDtypeStruct((2 * LANES, LANES), F32), jax.ShapeDtypeStruct(star_ref.shape, F32)),
         (pltpu.VMEM((9, LANES, LANES), F32),),
-        flops=2 * 72 * LANES**3,
+        micros=3,
         size=pay.size * 4,
     )(pay, ids, weights, star_ref, star_prior)
 
 
-def right_body(ret_ref, owner_ref, pos_ref, pred_ref, weighted_ref, right_ref, back):
-    chunks = owner_ref.shape[0]
-    tiles = chunks // 8
+def right_body(step_index, ret_ref, order_ref, start_ref, count_ref, line_ref, pred_ref, design_ref, weight_ref, mask_ref, right_ref, shifted, dense, back, weighted):
+    chunks = order_ref.shape[0]
     exps = right_ref.shape[0]
     rows = pred_ref.shape[1]
     width = rows // exps
-    owners = [owner_ref[8 * d : 8 * d + 8, :] for d in range(tiles)]
-    places = [pos_ref[8 * d : 8 * d + 8, :] for d in range(tiles)]
-
-    def step(o, found):
-        found = list(found)
-        table = [ret_ref[pl.ds(2 * o + c, 1), :] for c in range(2)]
-        for d in range(tiles):
-            hit = owners[d] == o
-            for c in range(2):
-                found[2 * d + c] = jnp.where(hit, lane_gather(table[c], places[d]), found[2 * d + c])
-        return tuple(found)
-
-    found = lax.fori_loop(0, LANES, step, (jnp.zeros((8, LANES), F32),) * (2 * tiles), unroll=8)
-    for d in range(tiles):
+    lane8 = iota((8, LANES), 1)
+
+    def shift(d, carry):
+        at = pl.ds(pl.multiple_of(d * 8, 8), 8)
+        offset = start_ref[at, :] & 127
+        end = offset + count_ref[at, :]
+        index = (lane8 - offset) & 127
+        near = (lane8 >= offset) & (lane8 < end)
+        far = lane8 + LANES < end
+        for c in range(2):
+            moved = jnp.take_along_axis(ret_ref[pl.ds(d * 16 + c, 8, stride=2), :], index, axis=1, mode="promise_in_bounds")
+            for k, keep in enumerate((near, far)):
+                for j, piece in enumerate(pieces(jnp.where(keep, moved, 0.0))):
+                    shifted[pl.ds(pl.multiple_of(d * 8 + k * LANES, 8), 8), (3 * c + j) * LANES : (3 * c + j + 1) * LANES] = piece
+        return carry
+
+    lax.fori_loop(0, LANES // 8, shift, 0, unroll=4)
+    row_of = line_ref[0:1, :] >> 7
+    sub_rows = iota((chunks, LANES), 0)
+    pick = jnp.concatenate([jnp.where(row_of + k == sub_rows, 1.0, 0.0) for k in range(2)], axis=1).astype(BF16)
+    spread = jnp.dot(pick, shifted[...].astype(BF16), preferred_element_type=F32)
+    for c in range(2):
+        part = [spread[:, (3 * c + j) * LANES : (3 * c + j + 1) * LANES] for j in range(3)]
+        dense[c * chunks : (c + 1) * chunks, :] = part[0] + (part[1] + part[2])
+
+    line_weight = weight_ref[...] * mask_ref[step_index : step_index + 1, :].astype(F32)
+    for d in range(chunks // 8):
+        order = order_ref[8 * d : 8 * d + 8, :]
+        found = lookup_rows(dense, [0, chunks], chunks, order >> 7, order & 127, 2)
         for c in range(2):
             for s in range(8):
                 r = 8 * d + s
-                back[c : c + 1, r * LANES : (r + 1) * LANES] = found[2 * d + c][s : s + 1]
+                back[c : c + 1, r * LANES : (r + 1) * LANES] = found[c][s : s + 1]
     for e in range(exps):
         at = slice(e * width, (e + 1) * width)
+        weighted = (design_ref[:, at].astype(F32) * line_weight[:, at]).astype(BF16)
         residual = (back[:, at] - pred_ref[:, at]).astype(BF16)
-        right_ref[e] = lax.dot_general(residual, weighted_ref[:, at], NT, preferred_element_type=F32)
-
-
-def right_sides(ret, owner, pos, pred, weighted, exps):
-    terms, rows = weighted.shape
+        right_ref[e] = lax.dot_general(residual, weighted, NT, preferred_element_type=F32)
+
+
+def right_sides(k, ret, order, start, count, line, pred, design, weight, mask, exps):
+    terms, rows = design.shape
+    chunks = rows // LANES
     return call(
-        right_body,
+        functools.partial(right_body, k),
         jax.ShapeDtypeStruct((exps, 2, terms), F32),
-        (pltpu.VMEM((2, rows), F32),),
-        flops=2 * 16 * weighted.size,
-        size=2 * weighted.size,
-    )(ret, owner, pos, pred, weighted)
-
-
-def gram_body(k, design_ref, weight_ref, mask_ref, gram_ref, weighted_ref):
-    terms = design_ref.shape[0]
-    rest = terms - LANES
+        (
+            pltpu.VMEM((2 * LANES, 6 * LANES), F32),
+            pltpu.VMEM((2 * chunks, LANES), F32),
+            pltpu.VMEM((2, rows), F32),
+            pltpu.VMEM((16, LANES), BF16),
+        ),
+        micros=2,
+        size=2 * design.size,
+    )(ret, order, start, count, line, pred, design, weight, mask)
+
+
+def exposure_gram(k, design_ref, weight_ref, mask_ref):
     design = design_ref[...]
     weight = weight_ref[...] * mask_ref[k : k + 1, :].astype(F32)
     weighted = (design.astype(F32) * weight).astype(BF16)
-    weighted_ref[...] = weighted
-    gram = 0.5 * lax.dot_general(
+    return 0.5 * lax.dot_general(
         jnp.concatenate([weighted, design], axis=1),
         jnp.concatenate([design, weighted], axis=1),
         NT,
         preferred_element_type=F32,
     )
-    gram_ref[0, :terms, :] = gram[:, :LANES]
-    gram_ref[0, terms:, :] = jnp.zeros((rest, LANES), F32)
-    gram_ref[0, terms:, :rest] = gram[LANES:, LANES:]
-
-
-def gram(design, weight, mask, k, exps):
+
+
+def pack(gram, out_ref):
+    terms = gram.shape[0]
+    rest = terms - LANES
+    out_ref[0, :terms, :] = gram[:, :LANES]
+    out_ref[0, terms:, :] = jnp.zeros((rest, LANES), F32)
+    out_ref[0, terms:, :rest] = gram[LANES:, LANES:]
+
+
+def gram_body(k, me_ref, design_ref, weight_ref, mask_ref, send_ref, keep_ref):
+    gram = exposure_gram(k, design_ref, weight_ref, mask_ref)
+
+    @pl.when(pl.program_id(0) == 0)
+    def _():
+        pack(gram, send_ref)
+
+    @pl.when(pl.program_id(0) == 1)
+    def _():
+        pack(gram, keep_ref)
+
+
+def gram(me, design, weight, mask, k, exps):
     terms, rows = design.shape
     width = rows // exps
     packed = 2 * terms - LANES
+    half = exps // 2
+
+    def exposure(s, d, me_ref):
+        y = lax.rem(lax.div(me_ref[0], 2) + d, half)
+        return 2 * y + lax.rem(me_ref[0] + 1 + s, 2)
+
+    part = jax.ShapeDtypeStruct((half, packed, LANES), F32)
     return pl.pallas_call(
         functools.partial(gram_body, k),
-        grid=(exps,),
-        in_specs=[
-            pl.BlockSpec((terms, width), lambda e: (0, e)),
-            pl.BlockSpec((1, width), lambda e: (0, e)),
-            pl.BlockSpec((2, width), lambda e: (0, e)),
-        ],
-        out_specs=[
-            pl.BlockSpec((1, packed, LANES), lambda e: (e, 0, 0)),
-            pl.BlockSpec((terms, width), lambda e: (0, e)),
-        ],
-        out_shape=(jax.ShapeDtypeStruct((exps, packed, LANES), F32), jax.ShapeDtypeStruct(design.shape, BF16)),
+        grid_spec=pltpu.PrefetchScalarGridSpec(
+            num_scalar_prefetch=1,
+            grid=(2, half),
+            in_specs=[
+                pl.BlockSpec((terms, width), lambda s, d, me_ref: (0, exposure(s, d, me_ref))),
+                pl.BlockSpec((1, width), lambda s, d, me_ref: (0, exposure(s, d, me_ref))),
+                pl.BlockSpec((2, width), lambda s, d, me_ref: (0, exposure(s, d, me_ref))),
+            ],
+            out_specs=[
+                pl.BlockSpec((1, packed, LANES), lambda s, d, me_ref: (jnp.where(s == 0, d, half - 1), 0, 0)),
+                pl.BlockSpec((1, packed, LANES), lambda s, d, me_ref: (jnp.where(s == 0, 0, d), 0, 0)),
+            ],
+        ),
+        out_shape=(part, part),
+        compiler_params=pltpu.CompilerParams(vmem_limit_bytes=GRANT),
         cost_estimate=pl.CostEstimate(
-            flops=4 * terms * design.size, bytes_accessed=4 * design.size, transcendentals=0
+            flops=4 * FLOPS_PER_US, bytes_accessed=4 * design.size, transcendentals=0
         ),
-    )(design, weight, mask)
+    )(me, design, weight, mask)
 
 
 def sweep_block(mat, k, tile, terms):
@@ -384,12 +495,11 @@
     mat[at, :] = wide[3]
 
 
-def invert_body(gram_ref, out_ref, mat):
+def invert_body(*refs):
+    *gram_refs, out_ref, mat = refs
     terms = out_ref.shape[0]
     rest = terms - LANES
-    total = gram_ref[0]
-    for s in range(1, gram_ref.shape[0]):
-        total = total + gram_ref[s]
+    total = functools.reduce(lambda a, b: a + b, [ref[...] for ref in gram_refs])
     square = jnp.concatenate([total[LANES:terms], jnp.zeros((LANES - rest, LANES), F32)], axis=0)
     mat[:, :LANES] = total[:terms]
     mat[:LANES, LANES:] = square.T
@@ -414,9 +524,9 @@
         invert_body,
         jax.ShapeDtypeStruct((terms, 2 * LANES), F32),
         (pltpu.VMEM((terms, 2 * LANES), F32),),
-        flops=2 * 25 * 80 * 256 * 256 * 10,
-        size=grams.size * 4,
-    )(grams)
+        micros=10,
+        size=4 * len(grams) * grams[0].size,
+    )(*grams)
 
 
 def solve_body(right_ref, inverse_ref, out_ref):
@@ -430,7 +540,7 @@
 
 
 def solve(right, inverse):
-    return call(solve_body, jax.ShapeDtypeStruct(right.shape, F32), flops=10**6, size=inverse.size * 4)(right, inverse)
+    return call(solve_body, jax.ShapeDtypeStruct(right.shape, F32), micros=1, size=inverse.size * 4)(right, inverse)
 
 
 def on_device(design, det_weight, outlier_mask, star_owner, star_slot, coef_init, star_ref, star_prior):
@@ -452,19 +562,42 @@
     def over_pix(x):
         return lax.all_to_all(x, "pix", split_axis=0, concat_axis=0, tiled=True)
 
-    pos, row, lane = route(owner)
-    gram_0, weighted_0 = gram(design, weight_line, outlier_mask, 0, exps)
-    gram_1, weighted_1 = gram(design, weight_line, outlier_mask, 1, exps)
-    pred, pay = place_first(coef_init, design, row, lane, slot, weight_rows, outlier_mask, cap)
-    ret, ids, later = owner_first(exchange(pay), star_ref, prior, cap)
-    right = right_sides(exchange(ret), owner, pos, pred, weighted_0, exps)
-    inverse_0 = invert(over_pix(gram_0), terms)
-    inverse_1 = invert(over_pix(gram_1), terms)
-    upd = over_pix(solve(over_pix(right), inverse_0))
-    pred, pay, coef = place_next(coef_init, upd, design, row, lane, cap)
-    ret, means = owner_next(exchange(pay), ids, later, star_ref, prior, cap)
-    right = right_sides(exchange(ret), owner, pos, pred, weighted_1, exps)
-    upd = over_pix(solve(over_pix(right), inverse_1))
+    pixes = lax.axis_size("pix")
+    me = lax.axis_index("pix").reshape(1)
+
+    def norm_exchange(send, keep):
+        got = lax.ppermute(send, "pix", [(i, i ^ 1) for i in range(pixes)])
+        parts = []
+        for d in range(pixes // 2):
+            part = keep[d] + got[d]
+            if d > 0:
+                part = lax.ppermute(part, "pix", [(i, (i + 2 * d) % pixes) for i in range(pixes)])
+            parts.append(part)
+        return parts
+
+    order, row, lane, start, count, line = route(owner)
+    pred, pay = place_first(coef_init, design, row, lane, start, count, slot, weight_rows, outlier_mask, cap)
+    pay = exchange(pay)
+    send, keep = gram(me, design, weight_line, outlier_mask, 0, exps)
+    gram_0 = norm_exchange(send, keep)
+    ret, ids, later = owner_first(pay, star_ref, prior, cap)
+    ret = exchange(ret)
+    inverse_0 = invert(gram_0, terms)
+    right = right_sides(0, ret, order, start, count, line, pred, design, weight_line, outlier_mask, exps)
+    right = over_pix(right)
+    send, keep = gram(me, design, weight_line, outlier_mask, 1, exps)
+    gram_1 = norm_exchange(send, keep)
+    upd = solve(right, inverse_0)
+    upd = over_pix(upd)
+    pred, pay, coef = place_next(coef_init, upd, design, row, lane, start, count, cap)
+    pay = exchange(pay)
+    ret, means = owner_next(pay, ids, later, star_ref, prior, cap)
+    ret = exchange(ret)
+    inverse_1 = invert(gram_1, terms)
+    right = right_sides(1, ret, order, start, count, line, pred, design, weight_line, outlier_mask, exps)
+    right = over_pix(right)
+    upd = solve(right, inverse_1)
+    upd = over_pix(upd)
     return (coef + upd, means)
 
 

time: 200 us -> 147 us (0.73)
  Pallas kernels: 90.5 us -> 51.2 us
  blocking collectives: 57.7 us -> 26.4 us
  starting transfers between devices: 25.6 us -> 44.3 us
  waiting for transfers between devices: 21.2 us -> 11.4 us
  local copies, waits for them, and re-layouts: 2.52 us -> 7.9 us
  other arithmetic: 0.62 us -> 4.42 us
    all_to_all x2 -> x1, blocking collectives: 38.6 us -> 17.1 us  [exchange(): lax.all_to_all(x.reshape(peers, -1, LANES), everyone, split_axis=0, conca...]
    pallas_call x7, Pallas kernels: 39.1 us -> 18.8 us  [the longest x2 9.07 us: gram(): pl.pallas_call(functools.partial(gram_body, k), grid_spec=pltpu.PrefetchS...]
    all_to_all x4 -> x3, waiting for transfers between devices: 15.3 us -> 0.09 us  [over_pix(): return lax.all_to_all(x, 'pix', split_axis=0, concat_axis=0, tiled=True)]
    all_to_all x2 -> x3, starting transfers between devices: 8.67 us -> 20.3 us  [exchange(): lax.all_to_all(x.reshape(peers, -1, LANES), everyone, split_axis=0, conca...]
    ppermute x0 -> x8, starting transfers between devices: none -> 11 us  [the longest x6 9.9 us: norm_exchange(): lax.ppermute(part, 'pix', [(i, (i + 2 * d) % pixes) for i in range(pixes)])]
    all_to_all x2 -> x1, blocking collectives: 19 us -> 9.27 us  [over_pix(): return lax.all_to_all(x, 'pix', split_axis=0, concat_axis=0, tiled=True)]
    all_to_all x2 -> x3, waiting for transfers between devices: 5.87 us -> 11.3 us  [exchange(): lax.all_to_all(x.reshape(peers, -1, LANES), everyone, split_axis=0, conca...]
    unnamed x14 -> x50, local copies, waits for them, and re-layouts: 2.52 us -> 7.9 us
  transfers between devices with their start and end apart: 6 -> 14, of which waited for: 4 -> 4; matrix products, arithmetic and copies ran while one was open for 0% -> 3% of each run, Pallas kernels for 27% -> 28%
where the time goes in v2:
time: 147 us; the launch traced here: 146 us
  Pallas kernels  51.2 us (35%)
  starting transfers between devices  44.3 us (30%)
  blocking collectives  26.4 us (18%)
  waiting for transfers between devices  11.4 us (8%)
  local copies, waits for them, and re-layouts  7.9 us (5%)
  other arithmetic  4.42 us (3%)
    all_to_all x3, starting transfers between devices, exchange(): lax.all_to_all(x.reshape(peers, -1, LANES), everyone, split_axis=0, conca...  20.3 us
    pallas_call x2, Pallas kernels, invert(): call(invert_body, jax.ShapeDtypeStruct((terms, 2 * LANES), F32), (pltpu.V...  18.8 us
    all_to_all x1, blocking collectives, exchange(): lax.all_to_all(x.reshape(peers, -1, LANES), everyone, split_axis=0, conca...  17.1 us
    all_to_all x3, starting transfers between devices, over_pix(): return lax.all_to_all(x, 'pix', split_axis=0, concat_axis=0, tiled=True)  12.9 us
    all_to_all x3, waiting for transfers between devices, exchange(): lax.all_to_all(x.reshape(peers, -1, LANES), everyone, split_axis=0, conca...  11.3 us
    ppermute x6, starting transfers between devices, norm_exchange(): lax.ppermute(part, 'pix', [(i, (i + 2 * d) % pixes) for i in range(pixes)])  9.9 us
    all_to_all x1, blocking collectives, over_pix(): return lax.all_to_all(x, 'pix', split_axis=0, concat_axis=0, tiled=True)  9.27 us
    pallas_call x2, Pallas kernels, gram(): pl.pallas_call(functools.partial(gram_body, k), grid_spec=pltpu.PrefetchS...  9.07 us
  transfers between devices with their start and end apart: 14, of which 4 were waited for; matrix products, arithmetic and copies ran while one was open for 3% of the time, Pallas kernels for 28%

profile of v2, /device:TPU:1, one launch (start us, length us, event | category | flops | bytes accessed | tf_op | source)
XLA Modules:
  0.0 146.4 jit_solution(17078098184069277303)
XLA Ops:
  1.4 4.2 %shard_map.95 = (s32[48,128]{1,0:T(8,128)S(1)}, s32[48,128]{1,0:T(8,128)S(1)}, s32[48,128]{1,0:T(8,128)S(1)}, s32[128,128]{1,0:T(8,128)S(1)}, s32[128,128]{1,0:T(8,128)S(1)}, /*index=5*/s32[8,128]{1,0:T(8,128)S(1)}) custom-call(s32[48,128]{1,0:T(8,128)S(1)} %bitcast.35), custom_call_target="tpu_custom_call" | custom-call | flops 4000000000 | bytes 49152 | tf_op jit(solution)/shard_map/pallas_call | solution.py:88
  6.2 4.6 %shard_map.96 = (f32[2,6144]{1,0:T(2,128)S(1)}, f32[512,128]{1,0:T(8,128)}) custom-call(f32[8,2,200]{2,1,0:T(2,128)S(1)} %copy-done.5, bf16[200,6144]{1,0:T(8,128)(2,1)S(1)} %copy-done, s32[48,128]{1,0:T(8,128)S(1)} %get-tuple-element.22.refs_2_.refs_3_, s32[48,128]{1,0:T(8,128)S(1)} %get-tuple-element.23.refs_3_.refs_4_, ...), custom_call_target="tpu_custom_call" | custom-call | flops 5000000000 | bytes 2457600 | tf_op jit(solution)/shard_map/pallas_call | solution.py:204
  11.4 11.6 %all-to-all-start = ((f32[128,4,128]{2,1,0:T(4,128)}), f32[128,4,128]{2,1,0:T(4,128)S(1)}, u32[]{:S(2)}, u32[]{:S(2)}) async-start(f32[128,4,128]{2,1,0:T(4,128)} %bitcast.3), calls=%async_computation | async-start | bytes 524288 | tf_op jit(solution)/shard_map/all_to_all | solution.py:559
  23.0 4.5 %shard_map.99 = (f32[4,272,128]{2,1,0:T(8,128)}, f32[4,272,128]{2,1,0:T(8,128)S(1)}) custom-call(s32[1]{0:T(128)} %bitcast.9.me_ref, bf16[200,6144]{1,0:T(8,128)(2,1)S(1)} %copy-done, f32[1,6144]{1,0:T(1,128)S(1)} %bitcast.38, s32[2,6144]{1,0:T(2,128)S(1)} %copy-done.1), custom_call_target="tpu_custom_call" | custom-call | flops 4000000000 | bytes 4915200 | tf_op jit(solution)/shard_map/pallas_call | solution.py:436
  28.6 5.2 %all-to-all-done = f32[128,4,128]{2,1,0:T(4,128)S(1)} async-done(((f32[128,4,128]{2,1,0:T(4,128)}), f32[128,4,128]{2,1,0:T(4,128)S(1)}, u32[]{:S(2)}, u32[]{:S(2)}) %all-to-all-start) | async-done | bytes 262176 | tf_op jit(solution)/shard_map/all_to_all | solution.py:559
  33.8 3.5 %shard_map.97 = (f32[256,128]{1,0:T(8,128)}, s32[128,128]{1,0:T(8,128)S(1)}, f32[128,128]{1,0:T(8,128)S(1)}) custom-call(f32[512,128]{1,0:T(8,128)S(1)} %bitcast.30, f32[2,768]{1,0:T(2,128)S(1)} %copy-done.6, f32[6,128]{1,0:T(8,128)S(1)} %bitcast.42), custom_call_target="tpu_custom_call" | custom-call | flops 4000000000 | bytes 262144 | tf_op jit(solution)/shard_map/pallas_call | solution.py:308
  38.6 4.5 %all-to-all-start.1 = ((f32[128,2,128]{2,1,0:T(2,128)}), f32[128,2,128]{2,1,0:T(2,128)S(1)}, u32[]{:S(2)}, u32[]{:S(2)}) async-start(f32[128,2,128]{2,1,0:T(2,128)} %bitcast.6), calls=%async_computation.1 | async-start | bytes 262144 | tf_op jit(solution)/shard_map/all_to_all | solution.py:559
  46.4 2.5 %collective-permute-start.2 = (f32[272,128]{1,0:T(8,128)}, f32[272,128]{1,0:T(8,128)S(1)}, u32[]{:S(2)}, u32[]{:S(2)}) collective-permute-start(f32[272,128]{1,0:T(8,128)} %get-tuple-element.47), channel_id=1, source_target_pairs={{0,64},{16,80},{32,96},{48,112},{64,0},{80,16},{96,32},{112,48},{1... | collective-permute-start | bytes 417800 | tf_op jit(solution)/shard_map/ppermute | solution.py:574
  50.0 3.0 %all-to-all-done.1 = f32[128,2,128]{2,1,0:T(2,128)S(1)} async-done(((f32[128,2,128]{2,1,0:T(2,128)}), f32[128,2,128]{2,1,0:T(2,128)S(1)}, u32[]{:S(2)}, u32[]{:S(2)}) %all-to-all-start.1) | async-done | bytes 131104 | tf_op jit(solution)/shard_map/all_to_all | solution.py:559
  54.6 2.3 %shard_map.98 = f32[8,2,200]{2,1,0:T(2,128)} custom-call(f32[256,128]{1,0:T(8,128)S(1)} %bitcast.32, s32[48,128]{1,0:T(8,128)S(1)} %copy-done.15, s32[128,128]{1,0:T(8,128)S(1)} %get-tuple-element.24.refs_4_.start_ref.refs_5_, s32[128,128]{1,0:T(8,128)S(1)} %get-tuple-element.25.refs_5_.count_ref.refs_6_, s32[8,128]{1,0:T(8,128)S(1)} %get-tuple-element.29.line_ref, ...), custom_call_target="tpu_custom_call" | custom-call | flops 2000000000 | bytes 2457600 | tf_op jit(solution)/shard_map/pallas_call | solution.py:379
  56.9 4.1 %all-to-all-start.2 = ((f32[8,2,200]{2,1,0:T(2,128)}), f32[8,2,200]{2,1,0:T(2,128)S(1)}, u32[]{:S(2)}, u32[]{:S(2)}) async-start(f32[8,2,200]{2,1,0:T(2,128)} %shard_map.98), calls=%async_computation.2 | async-start | bytes 32768 | tf_op jit(solution)/shard_map/all_to_all | solution.py:563
  60.9 9.4 %shard_map.100.inverse_ref = f32[200,256]{1,0:T(8,128)S(1)} custom-call(f32[272,128]{1,0:T(8,128)S(1)} %get-tuple-element.49.refs_0_, f32[272,128]{1,0:T(8,128)S(1)} %collective-permute-done.1.refs_1_, f32[272,128]{1,0:T(8,128)S(1)} %collective-permute-done.2.refs_2_, f32[272,128]{1,0:T(8,128)S(1)} %collective-permute-done.3.refs_3_), custom_call_target="tpu_custom_call" | custom-call | flops 10000000000 | bytes 557056 | tf_op jit(solution)/shard_map/pallas_call | solution.py:523
  72.8 4.8 %all-to-all-start.3 = ((f32[8,2,200]{2,1,0:T(2,128)}), f32[8,2,200]{2,1,0:T(2,128)S(1)}, u32[]{:S(2)}, u32[]{:S(2)}) async-start(f32[8,2,200]{2,1,0:T(2,128)} %shard_map.101), calls=%async_computation.3 | async-start | bytes 32768 | tf_op jit(solution)/shard_map/all_to_all | solution.py:563
  77.6 4.5 %shard_map.105 = (f32[4,272,128]{2,1,0:T(8,128)}, f32[4,272,128]{2,1,0:T(8,128)S(1)}) custom-call(s32[1]{0:T(128)} %bitcast.9.me_ref, bf16[200,6144]{1,0:T(8,128)(2,1)S(1)} %copy-done, f32[1,6144]{1,0:T(1,128)S(1)} %bitcast.40, s32[2,6144]{1,0:T(2,128)S(1)} %copy-done.1), custom_call_target="tpu_custom_call" | custom-call | flops 4000000000 | bytes 4915200 | tf_op jit(solution)/shard_map/pallas_call | solution.py:436
  82.2 2.2 %shard_map.102 = (f32[2,6144]{1,0:T(2,128)S(1)}, f32[256,128]{1,0:T(8,128)S(1)}, f32[8,2,200]{2,1,0:T(2,128)S(1)}) custom-call(f32[8,2,200]{2,1,0:T(2,128)S(1)} %copy-done.5, f32[8,2,200]{2,1,0:T(2,128)S(1)} %all-to-all-done.3.refs_1_, bf16[200,6144]{1,0:T(8,128)(2,1)S(1)} %copy-done, s32[48,128]{1,0:T(8,128)S(1)} %copy-done.22, s32[48,128]{1,0:T(8,128)S(1)} %copy-done.24, ...), custom_call_target="tpu_custom_call" | custom-call | flops 3000000000 | bytes 2457600 | tf_op jit(solution)/shard_map/pallas_call | solution.py:215
  84.5 17.1 %all_to_all.40 = f32[128,2,128]{2,1,0:T(2,128)S(1)} all-to-all(f32[128,2,128]{2,1,0:T(2,128)S(1)} %bitcast.33), channel_id=1, replica_groups=mesh['pix'=8,'exp'=16] {'pix','exp'}, dimensions={0} | all-to-all | bytes 262144 | tf_op jit(solution)/shard_map/all_to_all | solution.py:559
  101.6 3.3 %shard_map.103 = (f32[256,128]{1,0:T(8,128)}, f32[2,768]{1,0:T(2,128)}) custom-call(f32[256,128]{1,0:T(8,128)S(1)} %bitcast.34, s32[128,128]{1,0:T(8,128)S(1)} %copy-done.18, f32[128,128]{1,0:T(8,128)S(1)} %copy-done.20, f32[2,768]{1,0:T(2,128)S(1)} %copy-done.6, f32[6,128]{1,0:T(8,128)S(1)} %bitcast.43), custom_call_target="tpu_custom_call" | custom-call | flops 3000000000 | bytes 131072 | tf_op jit(solution)/shard_map/pallas_call | solution.py:322
  104.9 4.2 %all-to-all-start.5 = ((f32[128,2,128]{2,1,0:T(2,128)}), f32[128,2,128]{2,1,0:T(2,128)S(1)}, u32[]{:S(2)}, u32[]{:S(2)}) async-start(f32[128,2,128]{2,1,0:T(2,128)} %bitcast.16), calls=%async_computation.5 | async-start | bytes 262144 | tf_op jit(solution)/shard_map/all_to_all | solution.py:559
  112.4 2.5 %collective-permute-start.6 = (f32[272,128]{1,0:T(8,128)}, f32[272,128]{1,0:T(8,128)S(1)}, u32[]{:S(2)}, u32[]{:S(2)}) collective-permute-start(f32[272,128]{1,0:T(8,128)} %get-tuple-element.43), channel_id=1, source_target_pairs={{0,64},{16,80},{32,96},{48,112},{64,0},{80,16},{96,32},{112,48},{1... | collective-permute-start | bytes 417800 | tf_op jit(solution)/shard_map/ppermute | solution.py:574
  116.0 3.0 %all-to-all-done.5 = f32[128,2,128]{2,1,0:T(2,128)S(1)} async-done(((f32[128,2,128]{2,1,0:T(2,128)}), f32[128,2,128]{2,1,0:T(2,128)S(1)}, u32[]{:S(2)}, u32[]{:S(2)}) %all-to-all-start.5) | async-done | bytes 131104 | tf_op jit(solution)/shard_map/all_to_all | solution.py:559
  120.5 2.3 %shard_map.104 = f32[8,2,200]{2,1,0:T(2,128)} custom-call(f32[256,128]{1,0:T(8,128)S(1)} %bitcast.31, s32[48,128]{1,0:T(8,128)S(1)} %copy-done.16, s32[128,128]{1,0:T(8,128)S(1)} %get-tuple-element.24.refs_4_.start_ref.refs_5_, s32[128,128]{1,0:T(8,128)S(1)} %get-tuple-element.25.refs_5_.count_ref.refs_6_, s32[8,128]{1,0:T(8,128)S(1)} %get-tuple-element.29.line_ref, ...), custom_call_target="tpu_custom_call" | custom-call | flops 2000000000 | bytes 2457600 | tf_op jit(solution)/shard_map/pallas_call | solution.py:379
  122.8 4.1 %all-to-all-start.6 = ((f32[8,2,200]{2,1,0:T(2,128)}), f32[8,2,200]{2,1,0:T(2,128)S(1)}, u32[]{:S(2)}, u32[]{:S(2)}) async-start(f32[8,2,200]{2,1,0:T(2,128)} %shard_map.104), calls=%async_computation.6 | async-start | bytes 32768 | tf_op jit(solution)/shard_map/all_to_all | solution.py:563
  126.9 9.4 %shard_map.106.inverse_ref = f32[200,256]{1,0:T(8,128)S(1)} custom-call(f32[272,128]{1,0:T(8,128)S(1)} %get-tuple-element.45.refs_0_, f32[272,128]{1,0:T(8,128)S(1)} %collective-permute-done.5.refs_1_, f32[272,128]{1,0:T(8,128)S(1)} %collective-permute-done.6.refs_2_, f32[272,128]{1,0:T(8,128)S(1)} %collective-permute-done.7.refs_3_), custom_call_target="tpu_custom_call" | custom-call | flops 10000000000 | bytes 557056 | tf_op jit(solution)/shard_map/pallas_call | solution.py:523
  136.5 9.3 %all_to_all.41 = f32[8,2,200]{2,1,0:T(2,128)S(1)} all-to-all(f32[8,2,200]{2,1,0:T(2,128)S(1)} %shard_map.107), channel_id=1, replica_groups=mesh['pix'=8,'exp'=16] {'pix'}, dimensions={0} | all-to-all | bytes 25600 | tf_op jit(solution)/shard_map/all_to_all | solution.py:563
  (72 shorter events, 19.5 us)
Async XLA Ops:
  1.4 4.8 %copy-start = (bf16[200,6144]{1,0:T(8,128)(2,1)S(1)}, bf16[200,6144]{1,0:T(8,128)(2,1)}, u32[]{:S(2)}) copy-start(bf16[200,6144]{1,0:T(8,128)(2,1)} %design_ref.7) | copy-start | bytes 7372804
  1.4 4.8 %copy-start.1 = (s32[2,6144]{1,0:T(2,128)S(1)}, s32[2,6144]{1,0:T(2,128)}, u32[]{:S(2)}) copy-start(s32[2,6144]{1,0:T(2,128)} %mask_ref.7) | copy-start | bytes 147460
  1.4 4.8 %copy-start.3 = (s32[6144]{0:T(1024)S(1)}, s32[6144]{0:T(1024)}, u32[]{:S(2)}) copy-start(s32[6144]{0:T(1024)} %param.12) | copy-start | bytes 73732
  1.4 4.8 %copy-start.4 = (f32[6144]{0:T(1024)S(1)}, f32[6144]{0:T(1024)}, u32[]{:S(2)}) copy-start(f32[6144]{0:T(1024)} %param.9) | copy-start | bytes 73732
  1.4 4.8 %copy-start.5 = (f32[8,2,200]{2,1,0:T(2,128)S(1)}, f32[8,2,200]{2,1,0:T(2,128)}, u32[]{:S(2)}) copy-start(f32[8,2,200]{2,1,0:T(2,128)} %refs_0_.3) | copy-start | bytes 38404
  11.4 22.4 %all-to-all-start = ((f32[128,4,128]{2,1,0:T(4,128)}), f32[128,4,128]{2,1,0:T(4,128)S(1)}, u32[]{:S(2)}, u32[]{:S(2)}) async-start(f32[128,4,128]{2,1,0:T(4,128)} %bitcast.3), calls=%async_computation | async-start | bytes 524288 | tf_op jit(solution)/shard_map/all_to_all | solution.py:559
  23.0 10.8 %copy-start.6 = (f32[2,768]{1,0:T(2,128)S(1)}, f32[2,768]{1,0:T(2,128)}, u32[]{:S(2)}) copy-start(f32[2,768]{1,0:T(2,128)} %refs_3_.1) | copy-start | bytes 18436
  23.0 10.8 %copy-start.7 = (f32[768]{0:T(1024)S(1)}, f32[768]{0:T(1024)}, u32[]{:S(2)}) copy-start(f32[768]{0:T(1024)} %param.15) | copy-start | bytes 9220
  27.5 15.6 %collective-permute-start = (f32[4,272,128]{2,1,0:T(8,128)}, f32[4,272,128]{2,1,0:T(8,128)}, u32[]{:S(2)}, u32[]{:S(2)}) collective-permute-start(f32[4,272,128]{2,1,0:T(8,128)} %get-tuple-element.32), channel_id=1, source_target_pairs={{0,16},{16,0},{32,48},{48,32},{64,80},{80,64},{96,112},{112,96},{1... | collective-permute-start | bytes 1671176 | tf_op jit(solution)/shard_map/ppermute | solution.py:569
  38.6 14.5 %all-to-all-start.1 = ((f32[128,2,128]{2,1,0:T(2,128)}), f32[128,2,128]{2,1,0:T(2,128)S(1)}, u32[]{:S(2)}, u32[]{:S(2)}) async-start(f32[128,2,128]{2,1,0:T(2,128)} %bitcast.6), calls=%async_computation.1 | async-start | bytes 262144 | tf_op jit(solution)/shard_map/all_to_all | solution.py:559
  45.0 15.9 %collective-permute-start.1 = (f32[272,128]{1,0:T(8,128)}, f32[272,128]{1,0:T(8,128)S(1)}, u32[]{:S(2)}, u32[]{:S(2)}) collective-permute-start(f32[272,128]{1,0:T(8,128)} %get-tuple-element.48), channel_id=1, source_target_pairs={{0,32},{16,48},{32,64},{48,80},{64,96},{80,112},{96,0},{112,16},{1... | collective-permute-start | bytes 417800 | tf_op jit(solution)/shard_map/ppermute | solution.py:574
  46.4 14.5 %collective-permute-start.2 = (f32[272,128]{1,0:T(8,128)}, f32[272,128]{1,0:T(8,128)S(1)}, u32[]{:S(2)}, u32[]{:S(2)}) collective-permute-start(f32[272,128]{1,0:T(8,128)} %get-tuple-element.47), channel_id=1, source_target_pairs={{0,64},{16,80},{32,96},{48,112},{64,0},{80,16},{96,32},{112,48},{1... | collective-permute-start | bytes 417800 | tf_op jit(solution)/shard_map/ppermute | solution.py:574
  48.9 12.0 %collective-permute-start.3 = (f32[272,128]{1,0:T(8,128)}, f32[272,128]{1,0:T(8,128)S(1)}, u32[]{:S(2)}, u32[]{:S(2)}) collective-permute-start(f32[272,128]{1,0:T(8,128)} %get-tuple-element.46), channel_id=1, source_target_pairs={{0,96},{16,112},{32,0},{48,16},{64,32},{80,48},{96,64},{112,80},{1... | collective-permute-start | bytes 417800 | tf_op jit(solution)/shard_map/ppermute | solution.py:574
  56.9 14.2 %all-to-all-start.2 = ((f32[8,2,200]{2,1,0:T(2,128)}), f32[8,2,200]{2,1,0:T(2,128)S(1)}, u32[]{:S(2)}, u32[]{:S(2)}) async-start(f32[8,2,200]{2,1,0:T(2,128)} %shard_map.98), calls=%async_computation.2 | async-start | bytes 32768 | tf_op jit(solution)/shard_map/all_to_all | solution.py:563
  72.8 9.5 %all-to-all-start.3 = ((f32[8,2,200]{2,1,0:T(2,128)}), f32[8,2,200]{2,1,0:T(2,128)S(1)}, u32[]{:S(2)}, u32[]{:S(2)}) async-start(f32[8,2,200]{2,1,0:T(2,128)} %shard_map.101), calls=%async_computation.3 | async-start | bytes 32768 | tf_op jit(solution)/shard_map/all_to_all | solution.py:563
  82.1 19.5 %copy-start.18 = (s32[128,128]{1,0:T(8,128)S(1)}, s32[128,128]{1,0:T(8,128)}, u32[]{:S(2)}) copy-start(s32[128,128]{1,0:T(8,128)} %copy-done.17) | copy-start | bytes 196612
  82.1 19.5 %copy-start.20 = (f32[128,128]{1,0:T(8,128)S(1)}, f32[128,128]{1,0:T(8,128)}, u32[]{:S(2)}) copy-start(f32[128,128]{1,0:T(8,128)} %copy-done.19) | copy-start | bytes 196612
  82.1 27.0 %collective-permute-start.4 = (f32[4,272,128]{2,1,0:T(8,128)}, f32[4,272,128]{2,1,0:T(8,128)}, u32[]{:S(2)}, u32[]{:S(2)}) collective-permute-start(f32[4,272,128]{2,1,0:T(8,128)} %get-tuple-element.40), channel_id=1, source_target_pairs={{0,16},{16,0},{32,48},{48,32},{64,80},{80,64},{96,112},{112,96},{1... | collective-permute-start | bytes 1671176 | tf_op jit(solution)/shard_map/ppermute | solution.py:569
  84.5 20.4 %copy-start.12 = (f32[2,6144]{1,0:T(2,128)}, f32[2,6144]{1,0:T(2,128)S(1)}, u32[]{:S(2)}) copy-start(f32[2,6144]{1,0:T(2,128)S(1)} %get-tuple-element.38.pred_ref) | copy-start | bytes 147460
  104.9 14.1 %all-to-all-start.5 = ((f32[128,2,128]{2,1,0:T(2,128)}), f32[128,2,128]{2,1,0:T(2,128)S(1)}, u32[]{:S(2)}, u32[]{:S(2)}) async-start(f32[128,2,128]{2,1,0:T(2,128)} %bitcast.16), calls=%async_computation.5 | async-start | bytes 262144 | tf_op jit(solution)/shard_map/all_to_all | solution.py:559
  111.0 15.9 %collective-permute-start.5 = (f32[272,128]{1,0:T(8,128)}, f32[272,128]{1,0:T(8,128)S(1)}, u32[]{:S(2)}, u32[]{:S(2)}) collective-permute-start(f32[272,128]{1,0:T(8,128)} %get-tuple-element.44), channel_id=1, source_target_pairs={{0,32},{16,48},{32,64},{48,80},{64,96},{80,112},{96,0},{112,16},{1... | collective-permute-start | bytes 417800 | tf_op jit(solution)/shard_map/ppermute | solution.py:574
  112.4 14.5 %collective-permute-start.6 = (f32[272,128]{1,0:T(8,128)}, f32[272,128]{1,0:T(8,128)S(1)}, u32[]{:S(2)}, u32[]{:S(2)}) collective-permute-start(f32[272,128]{1,0:T(8,128)} %get-tuple-element.43), channel_id=1, source_target_pairs={{0,64},{16,80},{32,96},{48,112},{64,0},{80,16},{96,32},{112,48},{1... | collective-permute-start | bytes 417800 | tf_op jit(solution)/shard_map/ppermute | solution.py:574
  114.9 12.0 %collective-permute-start.7 = (f32[272,128]{1,0:T(8,128)}, f32[272,128]{1,0:T(8,128)S(1)}, u32[]{:S(2)}, u32[]{:S(2)}) collective-permute-start(f32[272,128]{1,0:T(8,128)} %get-tuple-element.42), channel_id=1, source_target_pairs={{0,96},{16,112},{32,0},{48,16},{64,32},{80,48},{96,64},{112,80},{1... | collective-permute-start | bytes 417800 | tf_op jit(solution)/shard_map/ppermute | solution.py:574
  122.8 13.5 %all-to-all-start.6 = ((f32[8,2,200]{2,1,0:T(2,128)}), f32[8,2,200]{2,1,0:T(2,128)S(1)}, u32[]{:S(2)}, u32[]{:S(2)}) async-start(f32[8,2,200]{2,1,0:T(2,128)} %shard_map.104), calls=%async_computation.6 | async-start | bytes 32768 | tf_op jit(solution)/shard_map/all_to_all | solution.py:563
  (15 other events, 26.4 us)

commit v3 on v2

--- a/solution.py
+++ b/solution.py
@@ -14,6 +14,7 @@
 BF16 = jnp.bfloat16
 GRANT = 16 << 20
 FLOPS_PER_US = 10**9
+SPLIT = 11
 NT = (((1,), (1,)), ((), ()))
 TN = (((0,), (0,)), ((), ()))
 
@@ -27,9 +28,11 @@
     return jnp.take_along_axis(table, index, axis=1, mode="promise_in_bounds")
 
 
-def call(body, out_shape, scratch=(), micros=1, size=0):
+def call(body, out_shape, scratch=(), micros=1, size=0, in_specs=None):
+    specs = {} if in_specs is None else {"in_specs": in_specs}
     return pl.pallas_call(
         body,
+        **specs,
         out_shape=out_shape,
         scratch_shapes=list(scratch),
         compiler_params=pltpu.CompilerParams(vmem_limit_bytes=GRANT),
@@ -53,7 +56,7 @@
         order_ref[pl.ds(r, 1), :] = jnp.sum(hot * (counts[:, :LANES] + base), axis=0, keepdims=True).astype(jnp.int32)
         return base + counts[:, LANES:]
 
-    counts = lax.fori_loop(0, chunks, rank, jnp.zeros((LANES, LANES), F32), unroll=4)
+    counts = lax.fori_loop(0, chunks, rank, jnp.zeros((LANES, LANES), F32), unroll=8)
     high = jnp.floor(counts * (1.0 / LANES))
     split = jnp.concatenate([high, counts - high * LANES], axis=1).astype(BF16)
     below = jnp.where(lane < sub, 1.0, 0.0).astype(BF16)
@@ -203,7 +206,7 @@
     rows = design.shape[1]
     return call(
         functools.partial(place_body, cap, True),
-        (jax.ShapeDtypeStruct((2, rows), F32), jax.ShapeDtypeStruct((4 * LANES, LANES), F32)),
+        (pltpu.HBM((2, rows), F32), jax.ShapeDtypeStruct((4 * LANES, LANES), F32)),
         place_scratch(5, rows // LANES),
         micros=5,
         size=2 * design.size,
@@ -215,7 +218,7 @@
     return call(
         functools.partial(place_body, cap, False),
         (
-            jax.ShapeDtypeStruct((2, rows), F32),
+            pltpu.HBM((2, rows), F32),
             jax.ShapeDtypeStruct((2 * LANES, LANES), F32),
             jax.ShapeDtypeStruct(coef.shape, F32),
         ),
@@ -227,11 +230,11 @@
 
 def owner_body(cap, first, *refs):
     if first:
-        pay_ref, ref_ref, prior_ref, ret_ref, id_ref, later_ref, parts = refs
+        pay_ref, ref_ref, prior_ref, ret_ref, kept_ref, parts, id_ref = refs
         width = 4
     else:
-        pay_ref, ids_in, weights_in, ref_ref, prior_ref, ret_ref, mean_ref, parts = refs
-        id_ref, width = ids_in, 2
+        pay_ref, kept_ref, ref_ref, prior_ref, ret_ref, mean_ref, parts, id_ref = refs
+        width = 2
     lane8 = iota((8, LANES), 1)
     sub8 = iota((8, LANES), 0)
     sub = iota((LANES, LANES), 0)
@@ -248,11 +251,13 @@
             for v, source in enumerate((p0, p1, ids)):
                 moved = pltpu.roll(source, (v * spare - cap) % LANES, 1)
                 later = jnp.where((lane8 >= v * spare) & (lane8 < (v + 1) * spare), moved, later)
-            later_ref[at, :] = later
+            kept_ref[0, at, :] = ids
+            kept_ref[1, at, :] = later
             weight = jnp.where(lane8 < cap, weight, 0.0)
             id_ref[at, :] = ids.astype(jnp.int32)
         else:
-            p0, p1, weight = plane(0), plane(1), weights_in[at, :]
+            p0, p1, weight = plane(0), plane(1), kept_ref[1, at, :]
+            id_ref[at, :] = kept_ref[0, at, :].astype(jnp.int32)
         for v, x in enumerate((weight * p0, weight * p1, weight)):
             for k, piece in enumerate(pieces(x)):
                 parts[3 * v + k, at, :] = piece
@@ -309,26 +314,30 @@
         functools.partial(owner_body, cap, True),
         (
             jax.ShapeDtypeStruct((2 * LANES, LANES), F32),
-            jax.ShapeDtypeStruct((LANES, LANES), jnp.int32),
-            jax.ShapeDtypeStruct((LANES, LANES), F32),
+            pltpu.HBM((2, LANES, LANES), F32),
         ),
-        (pltpu.VMEM((9, LANES, LANES), F32),),
+        (pltpu.VMEM((9, LANES, LANES), F32), pltpu.VMEM((LANES, LANES), jnp.int32)),
         micros=4,
         size=pay.size * 4,
     )(pay, star_ref, star_prior)
 
 
-def owner_next(pay, ids, weights, star_ref, star_prior, cap):
+def owner_next(pay, kept, star_ref, star_prior, cap):
     return call(
         functools.partial(owner_body, cap, False),
         (jax.ShapeDtypeStruct((2 * LANES, LANES), F32), jax.ShapeDtypeStruct(star_ref.shape, F32)),
-        (pltpu.VMEM((9, LANES, LANES), F32),),
+        (
+            pltpu.VMEM((9, LANES, LANES), F32),
+            pltpu.VMEM((LANES, LANES), jnp.int32),
+        ),
         micros=3,
         size=pay.size * 4,
-    )(pay, ids, weights, star_ref, star_prior)
-
-
-def right_body(step_index, ret_ref, order_ref, start_ref, count_ref, line_ref, pred_ref, design_ref, weight_ref, mask_ref, right_ref, shifted, dense, back, weighted):
+    )(pay, kept, star_ref, star_prior)
+
+
+def right_body(step_index, *refs):
+    ret_ref, order_ref, start_ref, count_ref, line_ref, pred_ref, design_ref, weight_ref, mask_ref = refs[:9]
+    right_ref, shifted, dense, back = refs[9:]
     chunks = order_ref.shape[0]
     exps = right_ref.shape[0]
     rows = pred_ref.shape[1]
@@ -383,7 +392,6 @@
             pltpu.VMEM((2 * LANES, 6 * LANES), F32),
             pltpu.VMEM((2 * chunks, LANES), F32),
             pltpu.VMEM((2, rows), F32),
-            pltpu.VMEM((16, LANES), BF16),
         ),
         micros=2,
         size=2 * design.size,
@@ -410,66 +418,49 @@
     out_ref[0, terms:, :rest] = gram[LANES:, LANES:]
 
 
-def gram_body(k, me_ref, design_ref, weight_ref, mask_ref, send_ref, keep_ref):
-    gram = exposure_gram(k, design_ref, weight_ref, mask_ref)
-
-    @pl.when(pl.program_id(0) == 0)
-    def _():
-        pack(gram, send_ref)
-
-    @pl.when(pl.program_id(0) == 1)
-    def _():
-        pack(gram, keep_ref)
-
-
-def gram(me, design, weight, mask, k, exps):
+def gram_body(k, me_ref, design_ref, weight_ref, mask_ref, gram_ref):
+    pack(exposure_gram(k, design_ref, weight_ref, mask_ref), gram_ref)
+
+
+def gram(me, design, weight, mask, k, exps, mine):
     terms, rows = design.shape
     width = rows // exps
     packed = 2 * terms - LANES
     half = exps // 2
 
-    def exposure(s, d, me_ref):
-        y = lax.rem(lax.div(me_ref[0], 2) + d, half)
-        return 2 * y + lax.rem(me_ref[0] + 1 + s, 2)
-
-    part = jax.ShapeDtypeStruct((half, packed, LANES), F32)
+    def exposure(d, me_ref):
+        return 2 * lax.rem(lax.div(me_ref[0], 2) + d, half) + lax.rem(me_ref[0] + (0 if mine else 1), 2)
+
     return pl.pallas_call(
         functools.partial(gram_body, k),
         grid_spec=pltpu.PrefetchScalarGridSpec(
             num_scalar_prefetch=1,
-            grid=(2, half),
+            grid=(half,),
             in_specs=[
-                pl.BlockSpec((terms, width), lambda s, d, me_ref: (0, exposure(s, d, me_ref))),
-                pl.BlockSpec((1, width), lambda s, d, me_ref: (0, exposure(s, d, me_ref))),
-                pl.BlockSpec((2, width), lambda s, d, me_ref: (0, exposure(s, d, me_ref))),
+                pl.BlockSpec((terms, width), lambda d, me_ref: (0, exposure(d, me_ref))),
+                pl.BlockSpec((1, width), lambda d, me_ref: (0, exposure(d, me_ref))),
+                pl.BlockSpec((2, width), lambda d, me_ref: (0, exposure(d, me_ref))),
             ],
-            out_specs=[
-                pl.BlockSpec((1, packed, LANES), lambda s, d, me_ref: (jnp.where(s == 0, d, half - 1), 0, 0)),
-                pl.BlockSpec((1, packed, LANES), lambda s, d, me_ref: (jnp.where(s == 0, 0, d), 0, 0)),
-            ],
+            out_specs=pl.BlockSpec((1, packed, LANES), lambda d, me_ref: (d, 0, 0)),
         ),
-        out_shape=(part, part),
+        out_shape=jax.ShapeDtypeStruct((half, packed, LANES), F32),
         compiler_params=pltpu.CompilerParams(vmem_limit_bytes=GRANT),
         cost_estimate=pl.CostEstimate(
-            flops=4 * FLOPS_PER_US, bytes_accessed=4 * design.size, transcendentals=0
+            flops=2 * FLOPS_PER_US, bytes_accessed=2 * design.size, transcendentals=0
         ),
     )(me, design, weight, mask)
 
 
-def sweep_block(mat, k, tile, terms):
-    base = k * 8 - tile * LANES
+def eliminate(panel, base, tile):
     sub = iota((8, LANES), 0)
     lane = iota((8, LANES), 1)
-    at = pl.ds(pl.multiple_of(k * 8, 8), 8)
-    panel = [mat[at, t * LANES : (t + 1) * LANES] for t in range(2)]
-    before = list(panel)
+    panel = list(panel)
     index = jnp.zeros((8, LANES), jnp.int32) + base
     cols = [jnp.take_along_axis(panel[tile], index + j, axis=1, mode="promise_in_bounds") for j in range(8)]
     for j in range(8):
         inverse = 1.0 / jnp.broadcast_to(cols[j][j : j + 1], (8, LANES))
-        unit = jnp.where(sub == j, 1.0, 0.0)
-        panel[tile] = jnp.where(lane == base + j, unit, panel[tile])
         mine = sub == j
+        panel[tile] = jnp.where(lane == base + j, jnp.where(mine, 1.0, 0.0), panel[tile])
 
         def sweep(x):
             row = jnp.broadcast_to(x[j : j + 1], (8, LANES)) * inverse
@@ -479,25 +470,63 @@
             cols[m] = sweep(cols[m])
         panel = [sweep(x) for x in panel]
     inside = (lane >= base) & (lane < base + 8)
-    swept = list(panel)
-    swept[tile] = jnp.where(inside, -panel[tile], panel[tile])
-    outer = list(panel)
-    outer[tile] = jnp.where(inside, 0.0, panel[tile])
-    unit = [jnp.zeros((8, LANES), F32)] * 2
-    unit[tile] = jnp.where(lane == base + sub, -1.0, 0.0)
-    wide = [jnp.concatenate(x, axis=1) for x in (before, outer, unit, swept)]
-    r, p, s = pieces(wide[0]), pieces(wide[1]), pieces(wide[1])
-    left = jnp.concatenate([r[0], r[0], r[0], r[1], r[1], r[2], s[0], s[1], s[2], s[2] * 0.0], axis=0).astype(BF16)
-    right = jnp.concatenate([p[0], p[1], p[2], p[0], p[1], p[0], wide[2], wide[2], wide[2], wide[2] * 0.0], axis=0).astype(BF16)
+    panel[tile] = jnp.where(inside, -panel[tile], panel[tile])
+    return panel
+
+
+def outside(k, rows):
+    lane = iota((rows, 2 * LANES), 1)
+    return jnp.where((lane >= k * 8) & (lane < k * 8 + 8), 0.0, 1.0)
+
+
+def block_rows(k):
+    return pl.ds(pl.multiple_of(k * 8, 8), 8)
+
+
+def update_all(mat, k, before, swept):
+    r, q = pieces(jnp.concatenate(before, axis=1)), pieces(jnp.concatenate(swept, axis=1))
+    left = jnp.concatenate([r[0], r[0], r[0], r[1], r[1], r[2]], axis=0).astype(BF16)
+    right = jnp.concatenate([q[0], q[1], q[2], q[0], q[1], q[0]], axis=0).astype(BF16)
     change = lax.dot_general(left, right, TN, preferred_element_type=F32)
-    keep = jnp.where((iota((1, 2 * LANES), 1) >= k * 8) & (iota((1, 2 * LANES), 1) < k * 8 + 8), 0.0, 1.0)
-    mat[...] = mat[...] * keep - change[:terms]
-    mat[at, :] = wide[3]
-
-
-def invert_body(*refs):
-    *gram_refs, out_ref, mat = refs
-    terms = out_ref.shape[0]
+    mat[...] = mat[...] * outside(k, 1) - change[: mat.shape[0]]
+    mat[block_rows(k), :] = jnp.concatenate(swept, axis=1)
+
+
+def update_next(mat, k, swept, base, tile):
+    at = block_rows(jnp.minimum(k + 1, mat.shape[0] // 8 - 1))
+    rows = [mat[at, t * LANES : (t + 1) * LANES] for t in range(2)]
+    keep = outside(k, 8)
+    index = jnp.zeros((8, LANES), jnp.int32) + base
+    fresh = [rows[t] * keep[:, t * LANES : (t + 1) * LANES] for t in range(2)]
+    for j in range(8):
+        col = jnp.take_along_axis(rows[tile], index + j, axis=1, mode="promise_in_bounds")
+        fresh = [fresh[t] - col * jnp.broadcast_to(swept[t][j : j + 1], (8, LANES)) for t in range(2)]
+    return fresh
+
+
+def sweep_range(mat, low, high):
+    start = low // 16
+    base = low * 8 - start * LANES
+    first = [mat[low * 8 : low * 8 + 8, t * LANES : (t + 1) * LANES] for t in range(2)]
+    swept = eliminate(first, base, start)
+    carry = (tuple(first), tuple(swept), tuple(update_next(mat, low, swept, base, start)))
+    for tile in range(2):
+        begin, end = max(low + 1, 16 * tile), min(high, 16 * (tile + 1))
+
+        def step(k, carry):
+            before, swept, panel = carry
+            base = k * 8 - tile * LANES
+            fresh = eliminate(panel, base, tile)
+            update_all(mat, k - 1, before, swept)
+            return (panel, tuple(fresh), tuple(update_next(mat, k, fresh, base, tile)))
+
+        if begin < end:
+            carry = lax.fori_loop(begin, end, step, carry)
+    update_all(mat, high - 1, carry[0], carry[1])
+
+
+def unpack(gram_refs, mat):
+    terms = mat.shape[0]
     rest = terms - LANES
     total = functools.reduce(lambda a, b: a + b, [ref[...] for ref in gram_refs])
     square = jnp.concatenate([total[LANES:terms], jnp.zeros((LANES - rest, LANES), F32)], axis=0)
@@ -506,41 +535,81 @@
     mat[LANES:, LANES:] = total[terms:]
     mat[...] = mat[...] + jnp.where(iota((terms, 2 * LANES), 0) == iota((terms, 2 * LANES), 1), RIDGE, 0.0)
 
-    def first(k, carry):
-        sweep_block(mat, k, 0, terms)
-        return carry
-
-    def second(k, carry):
-        sweep_block(mat, k, 1, terms)
-        return carry
-
-    lax.fori_loop(0, LANES // 8, first, 0)
-    lax.fori_loop(LANES // 8, terms // 8, second, 0)
+
+def invert_body(*refs):
+    *gram_refs, out_ref, mat = refs
+    unpack(gram_refs, mat)
+    sweep_range(mat, 0, mat.shape[0] // 8)
     out_ref[...] = -mat[...]
 
 
 def invert(grams, terms):
     return call(
         invert_body,
-        jax.ShapeDtypeStruct((terms, 2 * LANES), F32),
+        pltpu.HBM((terms, 2 * LANES), F32),
         (pltpu.VMEM((terms, 2 * LANES), F32),),
-        micros=10,
+        micros=8,
         size=4 * len(grams) * grams[0].size,
     )(*grams)
 
 
-def solve_body(right_ref, inverse_ref, out_ref):
+def invert_first_body(high, *refs):
+    *gram_refs, mat = refs
+    unpack(gram_refs, mat)
+    sweep_range(mat, 0, high)
+
+
+def invert_rest_body(low, part_ref, out_ref):
+    out_ref[...] = part_ref[...]
+    sweep_range(out_ref, low, out_ref.shape[0] // 8)
+    out_ref[...] = -out_ref[...]
+
+
+def invert_first(grams, terms, high):
+    return call(
+        functools.partial(invert_first_body, high),
+        jax.ShapeDtypeStruct((terms, 2 * LANES), F32),
+        micros=4,
+        size=4 * len(grams) * grams[0].size,
+    )(*grams)
+
+
+def invert_rest(part, low):
+    return call(
+        functools.partial(invert_rest_body, low),
+        jax.ShapeDtypeStruct(part.shape, F32),
+        micros=4,
+        size=8 * part.size,
+    )(part)
+
+
+def solve_body(last, *refs):
+    if last:
+        me_ref, coef_ref, right_ref, inverse_ref, out_ref = refs
+    else:
+        right_ref, inverse_ref, out_ref = refs
     terms = inverse_ref.shape[0]
     right = right_ref[0]
     for s in range(1, right_ref.shape[0]):
         right = right + right_ref[s]
-    update = jnp.dot(right, inverse_ref[...], precision=lax.Precision.HIGHEST, preferred_element_type=F32)
+    update = jnp.dot(right, inverse_ref[...], precision=lax.Precision.HIGHEST, preferred_element_type=F32)[:, :terms]
+    if last:
+        update = coef_ref[me_ref[0]] + update
     for s in range(right_ref.shape[0]):
-        out_ref[s] = update[:, :terms]
+        out_ref[s] = update
 
 
 def solve(right, inverse):
-    return call(solve_body, jax.ShapeDtypeStruct(right.shape, F32), micros=1, size=inverse.size * 4)(right, inverse)
+    shape = jax.ShapeDtypeStruct(right.shape, F32)
+    return call(functools.partial(solve_body, False), shape, micros=1, size=inverse.size * 4)(right, inverse)
+
+
+def solve_last(me, coef, right, inverse):
+    shape = jax.ShapeDtypeStruct(right.shape, F32)
+    specs = [pl.BlockSpec(memory_space=pltpu.SMEM)] + [pl.BlockSpec()] * 3
+    return call(functools.partial(solve_body, True), shape, micros=1, size=inverse.size * 4, in_specs=specs)(
+        me, coef, right, inverse
+    )
 
 
 def on_device(design, det_weight, outlier_mask, star_owner, star_slot, coef_init, star_ref, star_prior):
@@ -578,27 +647,30 @@
     order, row, lane, start, count, line = route(owner)
     pred, pay = place_first(coef_init, design, row, lane, start, count, slot, weight_rows, outlier_mask, cap)
     pay = exchange(pay)
-    send, keep = gram(me, design, weight_line, outlier_mask, 0, exps)
+    send = gram(me, design, weight_line, outlier_mask, 0, exps, False)
+    keep = gram(me, design, weight_line, outlier_mask, 0, exps, True)
     gram_0 = norm_exchange(send, keep)
-    ret, ids, later = owner_first(pay, star_ref, prior, cap)
+    ret, kept = owner_first(pay, star_ref, prior, cap)
     ret = exchange(ret)
-    inverse_0 = invert(gram_0, terms)
+    inverse_0 = invert_first(gram_0, terms, SPLIT)
+    inverse_0 = invert_rest(inverse_0, SPLIT)
     right = right_sides(0, ret, order, start, count, line, pred, design, weight_line, outlier_mask, exps)
     right = over_pix(right)
-    send, keep = gram(me, design, weight_line, outlier_mask, 1, exps)
+    send = gram(me, design, weight_line, outlier_mask, 1, exps, False)
+    keep = gram(me, design, weight_line, outlier_mask, 1, exps, True)
     gram_1 = norm_exchange(send, keep)
     upd = solve(right, inverse_0)
     upd = over_pix(upd)
     pred, pay, coef = place_next(coef_init, upd, design, row, lane, start, count, cap)
     pay = exchange(pay)
-    ret, means = owner_next(pay, ids, later, star_ref, prior, cap)
+    ret, means = owner_next(pay, kept, star_ref, prior, cap)
     ret = exchange(ret)
     inverse_1 = invert(gram_1, terms)
     right = right_sides(1, ret, order, start, count, line, pred, design, weight_line, outlier_mask, exps)
     right = over_pix(right)
-    upd = solve(right, inverse_1)
-    upd = over_pix(upd)
-    return (coef + upd, means)
+    coef = solve_last(me, coef, right, inverse_1)
+    coef = over_pix(coef)
+    return (coef, means)
 
 
 def solution(mesh):

time: 147 us -> 139 us (0.946)
  blocking collectives: 26.4 us -> 9.27 us
  waiting for transfers between devices: 11.4 us -> 21.8 us
  starting transfers between devices: 44.3 us -> 49.8 us
  Pallas kernels: 51.2 us -> 47.8 us
  local copies, waits for them, and re-layouts: 7.9 us -> 4.65 us
    all_to_all x1 -> x0, blocking collectives: 17.1 us -> none  [exchange(): lax.all_to_all(x.reshape(peers, -1, LANES), everyone, split_axis=0, conca...]
    all_to_all x3 -> x4, waiting for transfers between devices: 11.3 us -> 19.7 us  [exchange(): lax.all_to_all(x.reshape(peers, -1, LANES), everyone, split_axis=0, conca...]
    all_to_all x3 -> x4, starting transfers between devices: 20.3 us -> 25.9 us  [exchange(): lax.all_to_all(x.reshape(peers, -1, LANES), everyone, split_axis=0, conca...]
    unnamed x50 -> x37, local copies, waits for them, and re-layouts: 7.9 us -> 4.65 us
    all_to_all x3, waiting for transfers between devices: 0.09 us -> 2.06 us  [over_pix(): return lax.all_to_all(x, 'pix', split_axis=0, concat_axis=0, tiled=True)]
    pallas_call x6 -> x7, Pallas kernels: 26.6 us -> 24.6 us  [the longest x1 8.41 us: invert(): call(invert_body, pltpu.HBM((terms, 2 * LANES), F32), (pltpu.VMEM((terms,...]
    pallas_call x2 -> x4, Pallas kernels: 9.07 us -> 8.49 us  [gram(): pl.pallas_call(functools.partial(gram_body, k), grid_spec=pltpu.PrefetchS...]
  transfers between devices with their start and end apart: 14 -> 15, of which waited for: 4 -> 5; matrix products, arithmetic and copies ran while one was open for 3% -> 3% of each run, Pallas kernels for 28% -> 28%
where the time goes in v3:
time: 139 us; the launch traced here: 138 us
  starting transfers between devices  49.8 us (36%)
  Pallas kernels  47.8 us (34%)
  waiting for transfers between devices  21.8 us (16%)
  blocking collectives  9.27 us (7%)
  local copies, waits for them, and re-layouts  4.65 us (3%)
  other arithmetic  3.82 us (3%)
    all_to_all x4, starting transfers between devices, exchange(): lax.all_to_all(x.reshape(peers, -1, LANES), everyone, split_axis=0, conca...  25.9 us
    all_to_all x4, waiting for transfers between devices, exchange(): lax.all_to_all(x.reshape(peers, -1, LANES), everyone, split_axis=0, conca...  19.7 us
    all_to_all x3, starting transfers between devices, over_pix(): return lax.all_to_all(x, 'pix', split_axis=0, concat_axis=0, tiled=True)  12.9 us
    ppermute x6, starting transfers between devices, norm_exchange(): lax.ppermute(part, 'pix', [(i, (i + 2 * d) % pixes) for i in range(pixes)])  9.93 us
    all_to_all x1, blocking collectives, over_pix(): return lax.all_to_all(x, 'pix', split_axis=0, concat_axis=0, tiled=True)  9.27 us
    pallas_call x4, Pallas kernels, gram(): pl.pallas_call(functools.partial(gram_body, k), grid_spec=pltpu.PrefetchS...  8.49 us
    pallas_call x1, Pallas kernels, invert(): call(invert_body, pltpu.HBM((terms, 2 * LANES), F32), (pltpu.VMEM((terms,...  8.41 us
    unnamed x37, local copies, waits for them, and re-layouts  4.65 us
  transfers between devices with their start and end apart: 15, of which 5 were waited for; matrix products, arithmetic and copies ran while one was open for 3% of the time, Pallas kernels for 28%

profile of v3, /device:TPU:1, one launch (start us, length us, event | category | flops | bytes accessed | tf_op | source)
XLA Modules:
  0.0 138.0 jit_solution(1408874862670519428)
XLA Ops:
  1.4 3.3 %shard_map.95 = (s32[48,128]{1,0:T(8,128)S(1)}, s32[48,128]{1,0:T(8,128)S(1)}, s32[48,128]{1,0:T(8,128)S(1)}, s32[128,128]{1,0:T(8,128)S(1)}, s32[128,128]{1,0:T(8,128)S(1)}, /*index=5*/s32[8,128]{1,0:T(8,128)S(1)}) custom-call(s32[48,128]{1,0:T(8,128)S(1)} %bitcast.34), custom_call_target="tpu_custom_call" | custom-call | flops 4000000000 | bytes 49152 | tf_op jit(solution)/shard_map/pallas_call | solution.py:91
  4.8 4.5 %shard_map.96 = (f32[2,6144]{1,0:T(2,128)}, f32[512,128]{1,0:T(8,128)}) custom-call(f32[8,2,200]{2,1,0:T(2,128)S(1)} %copy-done.5, bf16[200,6144]{1,0:T(8,128)(2,1)S(1)} %copy-done, s32[48,128]{1,0:T(8,128)S(1)} %get-tuple-element.17.refs_2_.refs_3_, s32[48,128]{1,0:T(8,128)S(1)} %get-tuple-element.18.refs_3_.refs_4_, ...), custom_call_target="tpu_custom_call" | custom-call | flops 5000000000 | bytes 2457600 | tf_op jit(solution)/shard_map/pallas_call | solution.py:207
  9.3 11.5 %all-to-all-start = ((f32[128,4,128]{2,1,0:T(4,128)}), f32[128,4,128]{2,1,0:T(4,128)S(1)}, u32[]{:S(2)}, u32[]{:S(2)}) async-start(f32[128,4,128]{2,1,0:T(4,128)} %bitcast.4), calls=%async_computation | async-start | bytes 524288 | tf_op jit(solution)/shard_map/all_to_all | solution.py:628
  20.8 2.6 %shard_map.100 = f32[4,272,128]{2,1,0:T(8,128)} custom-call(s32[1]{0:T(128)} %bitcast.me_ref.refs_0_, bf16[200,6144]{1,0:T(8,128)(2,1)S(1)} %copy-done, f32[1,6144]{1,0:T(1,128)S(1)} %bitcast.37, s32[2,6144]{1,0:T(2,128)S(1)} %copy-done.1), custom_call_target="tpu_custom_call" | custom-call | flops 2000000000 | bytes 2457600 | tf_op jit(solution)/shard_map/pallas_call | solution.py:434
  26.1 5.5 %all-to-all-done = f32[128,4,128]{2,1,0:T(4,128)S(1)} async-done(((f32[128,4,128]{2,1,0:T(4,128)}), f32[128,4,128]{2,1,0:T(4,128)S(1)}, u32[]{:S(2)}, u32[]{:S(2)}) %all-to-all-start) | async-done | bytes 262176 | tf_op jit(solution)/shard_map/all_to_all | solution.py:628
  31.7 3.5 %shard_map.97 = (f32[256,128]{1,0:T(8,128)}, f32[2,128,128]{2,1,0:T(8,128)}) custom-call(f32[512,128]{1,0:T(8,128)S(1)} %bitcast.30, f32[2,768]{1,0:T(2,128)S(1)} %copy-done.6, f32[6,128]{1,0:T(8,128)S(1)} %bitcast.43), custom_call_target="tpu_custom_call" | custom-call | flops 4000000000 | bytes 262144 | tf_op jit(solution)/shard_map/pallas_call | solution.py:313
  35.2 4.5 %all-to-all-start.1 = ((f32[128,2,128]{2,1,0:T(2,128)}), f32[128,2,128]{2,1,0:T(2,128)S(1)}, u32[]{:S(2)}, u32[]{:S(2)}) async-start(f32[128,2,128]{2,1,0:T(2,128)} %bitcast.7), calls=%async_computation.1 | async-start | bytes 262144 | tf_op jit(solution)/shard_map/all_to_all | solution.py:628
  43.0 2.5 %collective-permute-start.2 = (f32[272,128]{1,0:T(8,128)}, f32[272,128]{1,0:T(8,128)S(1)}, u32[]{:S(2)}, u32[]{:S(2)}) collective-permute-start(f32[272,128]{1,0:T(8,128)} %get-tuple-element.37), channel_id=1, source_target_pairs={{0,64},{16,80},{32,96},{48,112},{64,0},{80,16},{96,32},{112,48},{1... | collective-permute-start | bytes 417800 | tf_op jit(solution)/shard_map/ppermute | solution.py:643
  46.7 3.0 %all-to-all-done.1 = f32[128,2,128]{2,1,0:T(2,128)S(1)} async-done(((f32[128,2,128]{2,1,0:T(2,128)}), f32[128,2,128]{2,1,0:T(2,128)S(1)}, u32[]{:S(2)}, u32[]{:S(2)}) %all-to-all-start.1) | async-done | bytes 131104 | tf_op jit(solution)/shard_map/all_to_all | solution.py:628
  52.8 4.0 %all-to-all-start.2 = ((f32[8,2,200]{2,1,0:T(2,128)}), f32[8,2,200]{2,1,0:T(2,128)S(1)}, u32[]{:S(2)}, u32[]{:S(2)}) async-start(f32[8,2,200]{2,1,0:T(2,128)} %shard_map.98), calls=%async_computation.2 | async-start | bytes 32768 | tf_op jit(solution)/shard_map/all_to_all | solution.py:632
  56.8 3.5 %shard_map.101.part_ref = f32[200,256]{1,0:T(8,128)S(1)} custom-call(f32[272,128]{1,0:T(8,128)S(1)} %get-tuple-element.39.refs_0_, f32[272,128]{1,0:T(8,128)S(1)} %collective-permute-done.1.refs_1_, f32[272,128]{1,0:T(8,128)S(1)} %collective-permute-done.2.refs_2_, f32[272,128]{1,0:T(8,128)S(1)} %collective-permute-done.3.refs_3_), custom_call_target="tpu_custom_call" | custom-call | flops 4000000000 | bytes 557056 | tf_op jit(solution)/shard_map/pallas_call | solution.py:569
  60.3 4.3 %shard_map.102.refs_1_ = f32[200,256]{1,0:T(8,128)S(1)} custom-call(f32[200,256]{1,0:T(8,128)S(1)} %shard_map.101.part_ref), custom_call_target="tpu_custom_call" | custom-call | flops 4000000000 | bytes 409600 | tf_op jit(solution)/shard_map/pallas_call | solution.py:578
  65.5 4.8 %all-to-all-start.3 = ((f32[8,2,200]{2,1,0:T(2,128)}), f32[8,2,200]{2,1,0:T(2,128)S(1)}, u32[]{:S(2)}, u32[]{:S(2)}) async-start(f32[8,2,200]{2,1,0:T(2,128)} %shard_map.103), calls=%async_computation.3 | async-start | bytes 32768 | tf_op jit(solution)/shard_map/all_to_all | solution.py:632
  70.3 2.6 %shard_map.108 = f32[4,272,128]{2,1,0:T(8,128)} custom-call(s32[1]{0:T(128)} %bitcast.me_ref.refs_0_, bf16[200,6144]{1,0:T(8,128)(2,1)S(1)} %copy-done, f32[1,6144]{1,0:T(1,128)S(1)} %bitcast.40, s32[2,6144]{1,0:T(2,128)S(1)} %copy-done.1), custom_call_target="tpu_custom_call" | custom-call | flops 2000000000 | bytes 2457600 | tf_op jit(solution)/shard_map/pallas_call | solution.py:434
  74.9 2.9 %shard_map.104 = (f32[2,6144]{1,0:T(2,128)}, f32[256,128]{1,0:T(8,128)}, f32[8,2,200]{2,1,0:T(2,128)S(1)}) custom-call(f32[8,2,200]{2,1,0:T(2,128)S(1)} %copy-done.5, f32[8,2,200]{2,1,0:T(2,128)S(1)} %all-to-all-done.3.refs_1_, bf16[200,6144]{1,0:T(8,128)(2,1)S(1)} %copy-done, s32[48,128]{1,0:T(8,128)S(1)} %copy-done.15, s32[48,128]{1,0:T(8,128)S(1)} %copy-done.17, ...), custom_call_target="tpu_custom_call" | custom-call | flops 3000000000 | bytes 2457600 | tf_op jit(solution)/shard_map/pallas_call | solution.py:218
  77.8 5.5 %all-to-all-start.4 = ((f32[128,2,128]{2,1,0:T(2,128)}), f32[128,2,128]{2,1,0:T(2,128)S(1)}, u32[]{:S(2)}, u32[]{:S(2)}) async-start(f32[128,2,128]{2,1,0:T(2,128)} %bitcast.14), calls=%async_computation.4 | async-start | bytes 262144 | tf_op jit(solution)/shard_map/all_to_all | solution.py:628
  85.1 8.2 %all-to-all-done.4 = f32[128,2,128]{2,1,0:T(2,128)S(1)} async-done(((f32[128,2,128]{2,1,0:T(2,128)}), f32[128,2,128]{2,1,0:T(2,128)S(1)}, u32[]{:S(2)}, u32[]{:S(2)}) %all-to-all-start.4) | async-done | bytes 131104 | tf_op jit(solution)/shard_map/all_to_all | solution.py:628
  93.2 3.3 %shard_map.105 = (f32[256,128]{1,0:T(8,128)}, f32[2,768]{1,0:T(2,128)}) custom-call(f32[256,128]{1,0:T(8,128)S(1)} %bitcast.33, f32[2,128,128]{2,1,0:T(8,128)S(1)} %copy-done.13, f32[2,768]{1,0:T(2,128)S(1)} %copy-done.6, f32[6,128]{1,0:T(8,128)S(1)} %bitcast.44), custom_call_target="tpu_custom_call" | custom-call | flops 3000000000 | bytes 131072 | tf_op jit(solution)/shard_map/pallas_call | solution.py:326
  96.5 4.3 %all-to-all-start.5 = ((f32[128,2,128]{2,1,0:T(2,128)}), f32[128,2,128]{2,1,0:T(2,128)S(1)}, u32[]{:S(2)}, u32[]{:S(2)}) async-start(f32[128,2,128]{2,1,0:T(2,128)} %bitcast.16), calls=%async_computation.5 | async-start | bytes 262144 | tf_op jit(solution)/shard_map/all_to_all | solution.py:628
  104.1 2.5 %collective-permute-start.6 = (f32[272,128]{1,0:T(8,128)}, f32[272,128]{1,0:T(8,128)S(1)}, u32[]{:S(2)}, u32[]{:S(2)}) collective-permute-start(f32[272,128]{1,0:T(8,128)} %get-tuple-element.33), channel_id=1, source_target_pairs={{0,64},{16,80},{32,96},{48,112},{64,0},{80,16},{96,32},{112,48},{1... | collective-permute-start | bytes 417800 | tf_op jit(solution)/shard_map/ppermute | solution.py:643
  107.7 3.0 %all-to-all-done.5 = f32[128,2,128]{2,1,0:T(2,128)S(1)} async-done(((f32[128,2,128]{2,1,0:T(2,128)}), f32[128,2,128]{2,1,0:T(2,128)S(1)}, u32[]{:S(2)}, u32[]{:S(2)}) %all-to-all-start.5) | async-done | bytes 131104 | tf_op jit(solution)/shard_map/all_to_all | solution.py:628
  114.5 4.0 %all-to-all-start.6 = ((f32[8,2,200]{2,1,0:T(2,128)}), f32[8,2,200]{2,1,0:T(2,128)S(1)}, u32[]{:S(2)}, u32[]{:S(2)}) async-start(f32[8,2,200]{2,1,0:T(2,128)} %shard_map.106), calls=%async_computation.6 | async-start | bytes 32768 | tf_op jit(solution)/shard_map/all_to_all | solution.py:632
  118.6 8.4 %shard_map.109.refs_3_ = f32[200,256]{1,0:T(8,128)} custom-call(f32[272,128]{1,0:T(8,128)S(1)} %get-tuple-element.35.refs_0_, f32[272,128]{1,0:T(8,128)S(1)} %collective-permute-done.5.refs_1_, f32[272,128]{1,0:T(8,128)S(1)} %collective-permute-done.6.refs_2_, f32[272,128]{1,0:T(8,128)S(1)} %collective-permute-done.7.refs_3_), custom_call_target="tpu_custom_call" | custom-call | flops 8000000000 | bytes 557056 | tf_op jit(solution)/shard_map/pallas_call | solution.py:547
  128.1 9.3 %all_to_all.40 = f32[8,2,200]{2,1,0:T(2,128)S(1)} all-to-all(f32[8,2,200]{2,1,0:T(2,128)S(1)} %shard_map.110), channel_id=1, replica_groups=mesh['pix'=8,'exp'=16] {'pix'}, dimensions={0} | all-to-all | bytes 25600 | tf_op jit(solution)/shard_map/all_to_all | solution.py:632
  (62 shorter events, 25.5 us)
Async XLA Ops:
  1.4 3.4 %copy-start.5 = (f32[8,2,200]{2,1,0:T(2,128)S(1)}, f32[8,2,200]{2,1,0:T(2,128)}, u32[]{:S(2)}) copy-start(f32[8,2,200]{2,1,0:T(2,128)} %refs_0_.3) | copy-start | bytes 38404
  4.7 4.6 %copy-start.14 = (s32[48,128]{1,0:T(8,128)}, s32[48,128]{1,0:T(8,128)S(1)}, u32[]{:S(2)}) copy-start(s32[48,128]{1,0:T(8,128)S(1)} %get-tuple-element.17.refs_2_.refs_3_) | copy-start | bytes 73732
  4.7 4.6 %copy-start.16 = (s32[48,128]{1,0:T(8,128)}, s32[48,128]{1,0:T(8,128)S(1)}, u32[]{:S(2)}) copy-start(s32[48,128]{1,0:T(8,128)S(1)} %get-tuple-element.18.refs_3_.refs_4_) | copy-start | bytes 73732
  4.7 45.0 %copy-start.11 = (s32[48,128]{1,0:T(8,128)}, s32[48,128]{1,0:T(8,128)S(1)}, u32[]{:S(2)}) copy-start(s32[48,128]{1,0:T(8,128)S(1)} %get-tuple-element.23.refs_1_) | copy-start | bytes 73732
  9.3 22.3 %all-to-all-start = ((f32[128,4,128]{2,1,0:T(4,128)}), f32[128,4,128]{2,1,0:T(4,128)S(1)}, u32[]{:S(2)}, u32[]{:S(2)}) async-start(f32[128,4,128]{2,1,0:T(4,128)} %bitcast.4), calls=%async_computation | async-start | bytes 524288 | tf_op jit(solution)/shard_map/all_to_all | solution.py:628
  23.4 8.3 %copy-start.6 = (f32[2,768]{1,0:T(2,128)S(1)}, f32[2,768]{1,0:T(2,128)}, u32[]{:S(2)}) copy-start(f32[2,768]{1,0:T(2,128)} %refs_2_.3) | copy-start | bytes 18436
  23.4 8.3 %copy-start.7 = (f32[768]{0:T(1024)S(1)}, f32[768]{0:T(1024)}, u32[]{:S(2)}) copy-start(f32[768]{0:T(1024)} %param.15) | copy-start | bytes 9220
  23.4 16.4 %collective-permute-start = (f32[4,272,128]{2,1,0:T(8,128)}, f32[4,272,128]{2,1,0:T(8,128)}, u32[]{:S(2)}, u32[]{:S(2)}) collective-permute-start(f32[4,272,128]{2,1,0:T(8,128)} %shard_map.100), channel_id=1, source_target_pairs={{0,16},{16,0},{32,48},{48,32},{64,80},{80,64},{96,112},{112,96},{1... | collective-permute-start | bytes 1671176 | tf_op jit(solution)/shard_map/ppermute | solution.py:638
  35.2 14.5 %all-to-all-start.1 = ((f32[128,2,128]{2,1,0:T(2,128)}), f32[128,2,128]{2,1,0:T(2,128)S(1)}, u32[]{:S(2)}, u32[]{:S(2)}) async-start(f32[128,2,128]{2,1,0:T(2,128)} %bitcast.7), calls=%async_computation.1 | async-start | bytes 262144 | tf_op jit(solution)/shard_map/all_to_all | solution.py:628
  41.7 15.1 %collective-permute-start.1 = (f32[272,128]{1,0:T(8,128)}, f32[272,128]{1,0:T(8,128)S(1)}, u32[]{:S(2)}, u32[]{:S(2)}) collective-permute-start(f32[272,128]{1,0:T(8,128)} %get-tuple-element.38), channel_id=1, source_target_pairs={{0,32},{16,48},{32,64},{48,80},{64,96},{80,112},{96,0},{112,16},{1... | collective-permute-start | bytes 417800 | tf_op jit(solution)/shard_map/ppermute | solution.py:643
  43.0 13.8 %collective-permute-start.2 = (f32[272,128]{1,0:T(8,128)}, f32[272,128]{1,0:T(8,128)S(1)}, u32[]{:S(2)}, u32[]{:S(2)}) collective-permute-start(f32[272,128]{1,0:T(8,128)} %get-tuple-element.37), channel_id=1, source_target_pairs={{0,64},{16,80},{32,96},{48,112},{64,0},{80,16},{96,32},{112,48},{1... | collective-permute-start | bytes 417800 | tf_op jit(solution)/shard_map/ppermute | solution.py:643
  45.6 11.3 %collective-permute-start.3 = (f32[272,128]{1,0:T(8,128)}, f32[272,128]{1,0:T(8,128)S(1)}, u32[]{:S(2)}, u32[]{:S(2)}) collective-permute-start(f32[272,128]{1,0:T(8,128)} %get-tuple-element.36), channel_id=1, source_target_pairs={{0,96},{16,112},{32,0},{48,16},{64,32},{80,48},{96,64},{112,80},{1... | collective-permute-start | bytes 417800 | tf_op jit(solution)/shard_map/ppermute | solution.py:643
  52.8 11.9 %all-to-all-start.2 = ((f32[8,2,200]{2,1,0:T(2,128)}), f32[8,2,200]{2,1,0:T(2,128)S(1)}, u32[]{:S(2)}, u32[]{:S(2)}) async-start(f32[8,2,200]{2,1,0:T(2,128)} %shard_map.98), calls=%async_computation.2 | async-start | bytes 32768 | tf_op jit(solution)/shard_map/all_to_all | solution.py:632
  65.5 9.5 %all-to-all-start.3 = ((f32[8,2,200]{2,1,0:T(2,128)}), f32[8,2,200]{2,1,0:T(2,128)S(1)}, u32[]{:S(2)}, u32[]{:S(2)}) async-start(f32[8,2,200]{2,1,0:T(2,128)} %shard_map.103), calls=%async_computation.3 | async-start | bytes 32768 | tf_op jit(solution)/shard_map/all_to_all | solution.py:632
  70.3 4.7 %copy-start.15 = (s32[48,128]{1,0:T(8,128)S(1)}, s32[48,128]{1,0:T(8,128)}, u32[]{:S(2)}) copy-start(s32[48,128]{1,0:T(8,128)} %copy-done.14) | copy-start | bytes 73732
  70.3 4.7 %copy-start.17 = (s32[48,128]{1,0:T(8,128)S(1)}, s32[48,128]{1,0:T(8,128)}, u32[]{:S(2)}) copy-start(s32[48,128]{1,0:T(8,128)} %copy-done.16) | copy-start | bytes 73732
  72.8 28.0 %collective-permute-start.4 = (f32[4,272,128]{2,1,0:T(8,128)}, f32[4,272,128]{2,1,0:T(8,128)}, u32[]{:S(2)}, u32[]{:S(2)}) collective-permute-start(f32[4,272,128]{2,1,0:T(8,128)} %shard_map.108), channel_id=1, source_target_pairs={{0,16},{16,0},{32,48},{48,32},{64,80},{80,64},{96,112},{112,96},{1... | collective-permute-start | bytes 1671176 | tf_op jit(solution)/shard_map/ppermute | solution.py:638
  77.8 15.4 %all-to-all-start.4 = ((f32[128,2,128]{2,1,0:T(2,128)}), f32[128,2,128]{2,1,0:T(2,128)S(1)}, u32[]{:S(2)}, u32[]{:S(2)}) async-start(f32[128,2,128]{2,1,0:T(2,128)} %bitcast.14), calls=%async_computation.4 | async-start | bytes 262144 | tf_op jit(solution)/shard_map/all_to_all | solution.py:628
  83.4 9.9 %copy-start.13 = (f32[2,128,128]{2,1,0:T(8,128)S(1)}, f32[2,128,128]{2,1,0:T(8,128)}, u32[]{:S(2)}) copy-start(f32[2,128,128]{2,1,0:T(8,128)} %get-tuple-element.28.refs_1_) | copy-start | bytes 393220
  96.5 14.2 %all-to-all-start.5 = ((f32[128,2,128]{2,1,0:T(2,128)}), f32[128,2,128]{2,1,0:T(2,128)S(1)}, u32[]{:S(2)}, u32[]{:S(2)}) async-start(f32[128,2,128]{2,1,0:T(2,128)} %bitcast.16), calls=%async_computation.5 | async-start | bytes 262144 | tf_op jit(solution)/shard_map/all_to_all | solution.py:628
  102.8 15.8 %collective-permute-start.5 = (f32[272,128]{1,0:T(8,128)}, f32[272,128]{1,0:T(8,128)S(1)}, u32[]{:S(2)}, u32[]{:S(2)}) collective-permute-start(f32[272,128]{1,0:T(8,128)} %get-tuple-element.34), channel_id=1, source_target_pairs={{0,32},{16,48},{32,64},{48,80},{64,96},{80,112},{96,0},{112,16},{1... | collective-permute-start | bytes 417800 | tf_op jit(solution)/shard_map/ppermute | solution.py:643
  104.1 14.5 %collective-permute-start.6 = (f32[272,128]{1,0:T(8,128)}, f32[272,128]{1,0:T(8,128)S(1)}, u32[]{:S(2)}, u32[]{:S(2)}) collective-permute-start(f32[272,128]{1,0:T(8,128)} %get-tuple-element.33), channel_id=1, source_target_pairs={{0,64},{16,80},{32,96},{48,112},{64,0},{80,16},{96,32},{112,48},{1... | collective-permute-start | bytes 417800 | tf_op jit(solution)/shard_map/ppermute | solution.py:643
  106.6 12.0 %collective-permute-start.7 = (f32[272,128]{1,0:T(8,128)}, f32[272,128]{1,0:T(8,128)S(1)}, u32[]{:S(2)}, u32[]{:S(2)}) collective-permute-start(f32[272,128]{1,0:T(8,128)} %get-tuple-element.32), channel_id=1, source_target_pairs={{0,96},{16,112},{32,0},{48,16},{64,32},{80,48},{96,64},{112,80},{1... | collective-permute-start | bytes 417800 | tf_op jit(solution)/shard_map/ppermute | solution.py:643
  114.5 12.5 %all-to-all-start.6 = ((f32[8,2,200]{2,1,0:T(2,128)}), f32[8,2,200]{2,1,0:T(2,128)S(1)}, u32[]{:S(2)}, u32[]{:S(2)}) async-start(f32[8,2,200]{2,1,0:T(2,128)} %shard_map.106), calls=%async_computation.6 | async-start | bytes 32768 | tf_op jit(solution)/shard_map/all_to_all | solution.py:632
  (9 other events, 17.5 us)

commit v4 on v3

--- a/solution.py
+++ b/solution.py
@@ -14,7 +14,7 @@
 BF16 = jnp.bfloat16
 GRANT = 16 << 20
 FLOPS_PER_US = 10**9
-SPLIT = 11
+SPLIT = 10
 NT = (((1,), (1,)), ((), ()))
 TN = (((0,), (0,)), ((), ()))
 
@@ -138,14 +138,12 @@
                 r = c * chunks + e * per + q
                 vals[r : r + 1, :] = pred[c : c + 1, q * LANES : (q + 1) * LANES]
     if first:
-        vals[2 * chunks : 3 * chunks, :] = slot_ref[...].astype(F32)
         for r in range(chunks):
             at = slice(r * LANES, (r + 1) * LANES)
-            for k in range(2):
-                vals[(3 + k) * chunks + r : (3 + k) * chunks + r + 1, :] = weight_ref[r : r + 1, :] * mask_ref[
-                    k : k + 1, at
-                ].astype(F32)
-    values = 5 if first else 2
+            code = slot_ref[r : r + 1, :] + (mask_ref[0:1, at] << 10) + (mask_ref[1:2, at] << 11)
+            vals[2 * chunks + r : 2 * chunks + r + 1, :] = code.astype(F32)
+        vals[3 * chunks : 4 * chunks, :] = weight_ref[...]
+    values = 4 if first else 2
     width_out = 4 if first else 2
     lane8 = iota((8, LANES), 1)
 
@@ -157,7 +155,7 @@
                 dense[at, (3 * v + k) * LANES : (3 * v + k + 1) * LANES] = piece
         return carry
 
-    lax.fori_loop(0, chunks // 8, gather, 0, unroll=2)
+    lax.fori_loop(0, chunks // 8, gather, 0, unroll=2 if first else 3)
     row_of = start_ref[...] >> 7
     column = iota((LANES, chunks), 1)
     pick = jnp.concatenate(
@@ -183,7 +181,10 @@
             found.append(jnp.where(held, jnp.where(near, rows_of[0], rows_of[1]), 0.0))
         if first:
             spare = LANES - cap
-            later = found.pop()
+            code, weight = found[2].astype(jnp.int32), found[3]
+            found[2] = (code & 1023).astype(F32)
+            found[3] = weight * ((code >> 10) & 1).astype(F32)
+            later = weight * (code >> 11).astype(F32)
             for v in range(3):
                 moved = pltpu.roll(later, (cap - v * spare) % LANES, 1)
                 found[v] = jnp.where(lane8 < cap, found[v], moved)
@@ -191,7 +192,7 @@
             pay_ref[pl.ds(d * 8 * width_out + v, 8, stride=width_out), :] = found[v]
         return carry
 
-    lax.fori_loop(0, LANES // 8, tile, 0, unroll=2)
+    lax.fori_loop(0, LANES // 8, tile, 0, unroll=4)
 
 
 def place_scratch(values, chunks):
@@ -207,7 +208,7 @@
     return call(
         functools.partial(place_body, cap, True),
         (pltpu.HBM((2, rows), F32), jax.ShapeDtypeStruct((4 * LANES, LANES), F32)),
-        place_scratch(5, rows // LANES),
+        place_scratch(4, rows // LANES),
         micros=5,
         size=2 * design.size,
     )(coef, design, row, lane, start, count, slot, weight, mask)
@@ -279,10 +280,10 @@
             )
             right.append(jnp.where((ids & 127) == sub, 1.0, 0.0).astype(BF16))
         return total + lax.dot_general(
-            jnp.concatenate(left, axis=1), jnp.concatenate(right, axis=1), NT, preferred_element_type=F32
+            jnp.concatenate(right, axis=1), jnp.concatenate(left, axis=1), NT, preferred_element_type=F32
         )
 
-    total = lax.fori_loop(0, LANES // group, accumulate, jnp.zeros((72, LANES), F32), unroll=4)
+    total = lax.fori_loop(0, LANES // group, accumulate, jnp.zeros((LANES, 72), F32), unroll=4).T
     sums = [total[24 * v : 24 * v + 8] + total[24 * v + 8 : 24 * v + 16] + total[24 * v + 16 : 24 * v + 24] for v in range(3)]
     rows = prior_ref.shape[0]
     means = [[], []]

time: 139 us -> 137 us (0.986)
  Pallas kernels: 47.8 us -> 46.2 us
where the time goes in v4:
time: 137 us; the launch traced here: 136 us
  starting transfers between devices  49.8 us (36%)
  Pallas kernels  46.2 us (34%)
  waiting for transfers between devices  21.8 us (16%)
  blocking collectives  9.27 us (7%)
  local copies, waits for them, and re-layouts  4.65 us (3%)
  other arithmetic  3.82 us (3%)
    all_to_all x4, starting transfers between devices, exchange(): lax.all_to_all(x.reshape(peers, -1, LANES), everyone, split_axis=0, conca...  25.9 us
    all_to_all x4, waiting for transfers between devices, exchange(): lax.all_to_all(x.reshape(peers, -1, LANES), everyone, split_axis=0, conca...  19.7 us
    all_to_all x3, starting transfers between devices, over_pix(): return lax.all_to_all(x, 'pix', split_axis=0, concat_axis=0, tiled=True)  12.9 us
    ppermute x6, starting transfers between devices, norm_exchange(): lax.ppermute(part, 'pix', [(i, (i + 2 * d) % pixes) for i in range(pixes)])  9.93 us
    all_to_all x1, blocking collectives, over_pix(): return lax.all_to_all(x, 'pix', split_axis=0, concat_axis=0, tiled=True)  9.27 us
    pallas_call x4, Pallas kernels, gram(): pl.pallas_call(functools.partial(gram_body, k), grid_spec=pltpu.PrefetchS...  8.49 us
    pallas_call x1, Pallas kernels, invert(): call(invert_body, pltpu.HBM((terms, 2 * LANES), F32), (pltpu.VMEM((terms,...  8.41 us
    unnamed x37, local copies, waits for them, and re-layouts  4.65 us
  transfers between devices with their start and end apart: 15, of which 5 were waited for; matrix products, arithmetic and copies ran while one was open for 3% of the time, Pallas kernels for 28%

profile of v4, /device:TPU:1, one launch (start us, length us, event | category | flops | bytes accessed | tf_op | source)
XLA Modules:
  0.0 136.4 jit_solution(10672933676891399602)
XLA Ops:
  1.4 3.3 %shard_map.95 = (s32[48,128]{1,0:T(8,128)S(1)}, s32[48,128]{1,0:T(8,128)S(1)}, s32[48,128]{1,0:T(8,128)S(1)}, s32[128,128]{1,0:T(8,128)S(1)}, s32[128,128]{1,0:T(8,128)S(1)}, /*index=5*/s32[8,128]{1,0:T(8,128)S(1)}) custom-call(s32[48,128]{1,0:T(8,128)S(1)} %bitcast.34), custom_call_target="tpu_custom_call" | custom-call | flops 4000000000 | bytes 49152 | tf_op jit(solution)/shard_map/pallas_call | solution.py:91
  4.8 3.7 %shard_map.96 = (f32[2,6144]{1,0:T(2,128)}, f32[512,128]{1,0:T(8,128)}) custom-call(f32[8,2,200]{2,1,0:T(2,128)S(1)} %copy-done.5, bf16[200,6144]{1,0:T(8,128)(2,1)S(1)} %copy-done, s32[48,128]{1,0:T(8,128)S(1)} %get-tuple-element.17.refs_2_.refs_3_, s32[48,128]{1,0:T(8,128)S(1)} %get-tuple-element.18.refs_3_.refs_4_, ...), custom_call_target="tpu_custom_call" | custom-call | flops 5000000000 | bytes 2457600 | tf_op jit(solution)/shard_map/pallas_call | solution.py:208
  8.5 11.5 %all-to-all-start = ((f32[128,4,128]{2,1,0:T(4,128)}), f32[128,4,128]{2,1,0:T(4,128)S(1)}, u32[]{:S(2)}, u32[]{:S(2)}) async-start(f32[128,4,128]{2,1,0:T(4,128)} %bitcast.4), calls=%async_computation | async-start | bytes 524288 | tf_op jit(solution)/shard_map/all_to_all | solution.py:629
  20.0 2.6 %shard_map.100 = f32[4,272,128]{2,1,0:T(8,128)} custom-call(s32[1]{0:T(128)} %bitcast.me_ref.refs_0_, bf16[200,6144]{1,0:T(8,128)(2,1)S(1)} %copy-done, f32[1,6144]{1,0:T(1,128)S(1)} %bitcast.37, s32[2,6144]{1,0:T(2,128)S(1)} %copy-done.1), custom_call_target="tpu_custom_call" | custom-call | flops 2000000000 | bytes 2457600 | tf_op jit(solution)/shard_map/pallas_call | solution.py:435
  25.3 5.5 %all-to-all-done = f32[128,4,128]{2,1,0:T(4,128)S(1)} async-done(((f32[128,4,128]{2,1,0:T(4,128)}), f32[128,4,128]{2,1,0:T(4,128)S(1)}, u32[]{:S(2)}, u32[]{:S(2)}) %all-to-all-start) | async-done | bytes 262176 | tf_op jit(solution)/shard_map/all_to_all | solution.py:629
  30.8 3.3 %shard_map.97 = (f32[256,128]{1,0:T(8,128)}, f32[2,128,128]{2,1,0:T(8,128)}) custom-call(f32[512,128]{1,0:T(8,128)S(1)} %bitcast.30, f32[2,768]{1,0:T(2,128)S(1)} %copy-done.6, f32[6,128]{1,0:T(8,128)S(1)} %bitcast.43), custom_call_target="tpu_custom_call" | custom-call | flops 4000000000 | bytes 262144 | tf_op jit(solution)/shard_map/pallas_call | solution.py:314
  34.2 4.5 %all-to-all-start.1 = ((f32[128,2,128]{2,1,0:T(2,128)}), f32[128,2,128]{2,1,0:T(2,128)S(1)}, u32[]{:S(2)}, u32[]{:S(2)}) async-start(f32[128,2,128]{2,1,0:T(2,128)} %bitcast.7), calls=%async_computation.1 | async-start | bytes 262144 | tf_op jit(solution)/shard_map/all_to_all | solution.py:629
  42.0 2.5 %collective-permute-start.2 = (f32[272,128]{1,0:T(8,128)}, f32[272,128]{1,0:T(8,128)S(1)}, u32[]{:S(2)}, u32[]{:S(2)}) collective-permute-start(f32[272,128]{1,0:T(8,128)} %get-tuple-element.37), channel_id=1, source_target_pairs={{0,64},{16,80},{32,96},{48,112},{64,0},{80,16},{96,32},{112,48},{1... | collective-permute-start | bytes 417800 | tf_op jit(solution)/shard_map/ppermute | solution.py:644
  45.6 3.0 %all-to-all-done.1 = f32[128,2,128]{2,1,0:T(2,128)S(1)} async-done(((f32[128,2,128]{2,1,0:T(2,128)}), f32[128,2,128]{2,1,0:T(2,128)S(1)}, u32[]{:S(2)}, u32[]{:S(2)}) %all-to-all-start.1) | async-done | bytes 131104 | tf_op jit(solution)/shard_map/all_to_all | solution.py:629
  51.7 4.0 %all-to-all-start.2 = ((f32[8,2,200]{2,1,0:T(2,128)}), f32[8,2,200]{2,1,0:T(2,128)S(1)}, u32[]{:S(2)}, u32[]{:S(2)}) async-start(f32[8,2,200]{2,1,0:T(2,128)} %shard_map.98), calls=%async_computation.2 | async-start | bytes 32768 | tf_op jit(solution)/shard_map/all_to_all | solution.py:633
  55.8 3.2 %shard_map.101.part_ref = f32[200,256]{1,0:T(8,128)S(1)} custom-call(f32[272,128]{1,0:T(8,128)S(1)} %get-tuple-element.39.refs_0_, f32[272,128]{1,0:T(8,128)S(1)} %collective-permute-done.1.refs_1_, f32[272,128]{1,0:T(8,128)S(1)} %collective-permute-done.2.refs_2_, f32[272,128]{1,0:T(8,128)S(1)} %collective-permute-done.3.refs_3_), custom_call_target="tpu_custom_call" | custom-call | flops 4000000000 | bytes 557056 | tf_op jit(solution)/shard_map/pallas_call | solution.py:570
  59.0 4.6 %shard_map.102.refs_1_ = f32[200,256]{1,0:T(8,128)S(1)} custom-call(f32[200,256]{1,0:T(8,128)S(1)} %shard_map.101.part_ref), custom_call_target="tpu_custom_call" | custom-call | flops 4000000000 | bytes 409600 | tf_op jit(solution)/shard_map/pallas_call | solution.py:579
  64.4 4.8 %all-to-all-start.3 = ((f32[8,2,200]{2,1,0:T(2,128)}), f32[8,2,200]{2,1,0:T(2,128)S(1)}, u32[]{:S(2)}, u32[]{:S(2)}) async-start(f32[8,2,200]{2,1,0:T(2,128)} %shard_map.103), calls=%async_computation.3 | async-start | bytes 32768 | tf_op jit(solution)/shard_map/all_to_all | solution.py:633
  69.2 2.6 %shard_map.108 = f32[4,272,128]{2,1,0:T(8,128)} custom-call(s32[1]{0:T(128)} %bitcast.me_ref.refs_0_, bf16[200,6144]{1,0:T(8,128)(2,1)S(1)} %copy-done, f32[1,6144]{1,0:T(1,128)S(1)} %bitcast.40, s32[2,6144]{1,0:T(2,128)S(1)} %copy-done.1), custom_call_target="tpu_custom_call" | custom-call | flops 2000000000 | bytes 2457600 | tf_op jit(solution)/shard_map/pallas_call | solution.py:435
  73.9 2.5 %shard_map.104 = (f32[2,6144]{1,0:T(2,128)}, f32[256,128]{1,0:T(8,128)}, f32[8,2,200]{2,1,0:T(2,128)S(1)}) custom-call(f32[8,2,200]{2,1,0:T(2,128)S(1)} %copy-done.5, f32[8,2,200]{2,1,0:T(2,128)S(1)} %all-to-all-done.3.refs_1_, bf16[200,6144]{1,0:T(8,128)(2,1)S(1)} %copy-done, s32[48,128]{1,0:T(8,128)S(1)} %copy-done.15, s32[48,128]{1,0:T(8,128)S(1)} %copy-done.17, ...), custom_call_target="tpu_custom_call" | custom-call | flops 3000000000 | bytes 2457600 | tf_op jit(solution)/shard_map/pallas_call | solution.py:219
  76.4 5.5 %all-to-all-start.4 = ((f32[128,2,128]{2,1,0:T(2,128)}), f32[128,2,128]{2,1,0:T(2,128)S(1)}, u32[]{:S(2)}, u32[]{:S(2)}) async-start(f32[128,2,128]{2,1,0:T(2,128)} %bitcast.14), calls=%async_computation.4 | async-start | bytes 262144 | tf_op jit(solution)/shard_map/all_to_all | solution.py:629
  83.7 8.2 %all-to-all-done.4 = f32[128,2,128]{2,1,0:T(2,128)S(1)} async-done(((f32[128,2,128]{2,1,0:T(2,128)}), f32[128,2,128]{2,1,0:T(2,128)S(1)}, u32[]{:S(2)}, u32[]{:S(2)}) %all-to-all-start.4) | async-done | bytes 131104 | tf_op jit(solution)/shard_map/all_to_all | solution.py:629
  91.8 3.1 %shard_map.105 = (f32[256,128]{1,0:T(8,128)}, f32[2,768]{1,0:T(2,128)}) custom-call(f32[256,128]{1,0:T(8,128)S(1)} %bitcast.33, f32[2,128,128]{2,1,0:T(8,128)S(1)} %copy-done.13, f32[2,768]{1,0:T(2,128)S(1)} %copy-done.6, f32[6,128]{1,0:T(8,128)S(1)} %bitcast.44), custom_call_target="tpu_custom_call" | custom-call | flops 3000000000 | bytes 131072 | tf_op jit(solution)/shard_map/pallas_call | solution.py:327
  94.9 4.3 %all-to-all-start.5 = ((f32[128,2,128]{2,1,0:T(2,128)}), f32[128,2,128]{2,1,0:T(2,128)S(1)}, u32[]{:S(2)}, u32[]{:S(2)}) async-start(f32[128,2,128]{2,1,0:T(2,128)} %bitcast.16), calls=%async_computation.5 | async-start | bytes 262144 | tf_op jit(solution)/shard_map/all_to_all | solution.py:629
  102.5 2.5 %collective-permute-start.6 = (f32[272,128]{1,0:T(8,128)}, f32[272,128]{1,0:T(8,128)S(1)}, u32[]{:S(2)}, u32[]{:S(2)}) collective-permute-start(f32[272,128]{1,0:T(8,128)} %get-tuple-element.33), channel_id=1, source_target_pairs={{0,64},{16,80},{32,96},{48,112},{64,0},{80,16},{96,32},{112,48},{1... | collective-permute-start | bytes 417800 | tf_op jit(solution)/shard_map/ppermute | solution.py:644
  106.1 3.0 %all-to-all-done.5 = f32[128,2,128]{2,1,0:T(2,128)S(1)} async-done(((f32[128,2,128]{2,1,0:T(2,128)}), f32[128,2,128]{2,1,0:T(2,128)S(1)}, u32[]{:S(2)}, u32[]{:S(2)}) %all-to-all-start.5) | async-done | bytes 131104 | tf_op jit(solution)/shard_map/all_to_all | solution.py:629
  113.0 4.0 %all-to-all-start.6 = ((f32[8,2,200]{2,1,0:T(2,128)}), f32[8,2,200]{2,1,0:T(2,128)S(1)}, u32[]{:S(2)}, u32[]{:S(2)}) async-start(f32[8,2,200]{2,1,0:T(2,128)} %shard_map.106), calls=%async_computation.6 | async-start | bytes 32768 | tf_op jit(solution)/shard_map/all_to_all | solution.py:633
  117.0 8.4 %shard_map.109.refs_3_ = f32[200,256]{1,0:T(8,128)} custom-call(f32[272,128]{1,0:T(8,128)S(1)} %get-tuple-element.35.refs_0_, f32[272,128]{1,0:T(8,128)S(1)} %collective-permute-done.5.refs_1_, f32[272,128]{1,0:T(8,128)S(1)} %collective-permute-done.6.refs_2_, f32[272,128]{1,0:T(8,128)S(1)} %collective-permute-done.7.refs_3_), custom_call_target="tpu_custom_call" | custom-call | flops 8000000000 | bytes 557056 | tf_op jit(solution)/shard_map/pallas_call | solution.py:548
  126.6 9.3 %all_to_all.40 = f32[8,2,200]{2,1,0:T(2,128)S(1)} all-to-all(f32[8,2,200]{2,1,0:T(2,128)S(1)} %shard_map.110), channel_id=1, replica_groups=mesh['pix'=8,'exp'=16] {'pix'}, dimensions={0} | all-to-all | bytes 25600 | tf_op jit(solution)/shard_map/all_to_all | solution.py:633
  (62 shorter events, 25.5 us)
Async XLA Ops:
  1.4 3.4 %copy-start.5 = (f32[8,2,200]{2,1,0:T(2,128)S(1)}, f32[8,2,200]{2,1,0:T(2,128)}, u32[]{:S(2)}) copy-start(f32[8,2,200]{2,1,0:T(2,128)} %refs_0_.3) | copy-start | bytes 38404
  4.7 3.8 %copy-start.14 = (s32[48,128]{1,0:T(8,128)}, s32[48,128]{1,0:T(8,128)S(1)}, u32[]{:S(2)}) copy-start(s32[48,128]{1,0:T(8,128)S(1)} %get-tuple-element.17.refs_2_.refs_3_) | copy-start | bytes 73732
  4.7 3.8 %copy-start.16 = (s32[48,128]{1,0:T(8,128)}, s32[48,128]{1,0:T(8,128)S(1)}, u32[]{:S(2)}) copy-start(s32[48,128]{1,0:T(8,128)S(1)} %get-tuple-element.18.refs_3_.refs_4_) | copy-start | bytes 73732
  4.7 43.9 %copy-start.11 = (s32[48,128]{1,0:T(8,128)}, s32[48,128]{1,0:T(8,128)S(1)}, u32[]{:S(2)}) copy-start(s32[48,128]{1,0:T(8,128)S(1)} %get-tuple-element.23.refs_1_) | copy-start | bytes 73732
  8.5 22.3 %all-to-all-start = ((f32[128,4,128]{2,1,0:T(4,128)}), f32[128,4,128]{2,1,0:T(4,128)S(1)}, u32[]{:S(2)}, u32[]{:S(2)}) async-start(f32[128,4,128]{2,1,0:T(4,128)} %bitcast.4), calls=%async_computation | async-start | bytes 524288 | tf_op jit(solution)/shard_map/all_to_all | solution.py:629
  22.6 8.3 %copy-start.6 = (f32[2,768]{1,0:T(2,128)S(1)}, f32[2,768]{1,0:T(2,128)}, u32[]{:S(2)}) copy-start(f32[2,768]{1,0:T(2,128)} %refs_2_.3) | copy-start | bytes 18436
  22.6 8.3 %copy-start.7 = (f32[768]{0:T(1024)S(1)}, f32[768]{0:T(1024)}, u32[]{:S(2)}) copy-start(f32[768]{0:T(1024)} %param.15) | copy-start | bytes 9220
  22.6 16.2 %collective-permute-start = (f32[4,272,128]{2,1,0:T(8,128)}, f32[4,272,128]{2,1,0:T(8,128)}, u32[]{:S(2)}, u32[]{:S(2)}) collective-permute-start(f32[4,272,128]{2,1,0:T(8,128)} %shard_map.100), channel_id=1, source_target_pairs={{0,16},{16,0},{32,48},{48,32},{64,80},{80,64},{96,112},{112,96},{1... | collective-permute-start | bytes 1671176 | tf_op jit(solution)/shard_map/ppermute | solution.py:639
  34.2 14.5 %all-to-all-start.1 = ((f32[128,2,128]{2,1,0:T(2,128)}), f32[128,2,128]{2,1,0:T(2,128)S(1)}, u32[]{:S(2)}, u32[]{:S(2)}) async-start(f32[128,2,128]{2,1,0:T(2,128)} %bitcast.7), calls=%async_computation.1 | async-start | bytes 262144 | tf_op jit(solution)/shard_map/all_to_all | solution.py:629
  40.6 15.1 %collective-permute-start.1 = (f32[272,128]{1,0:T(8,128)}, f32[272,128]{1,0:T(8,128)S(1)}, u32[]{:S(2)}, u32[]{:S(2)}) collective-permute-start(f32[272,128]{1,0:T(8,128)} %get-tuple-element.38), channel_id=1, source_target_pairs={{0,32},{16,48},{32,64},{48,80},{64,96},{80,112},{96,0},{112,16},{1... | collective-permute-start | bytes 417800 | tf_op jit(solution)/shard_map/ppermute | solution.py:644
  42.0 13.8 %collective-permute-start.2 = (f32[272,128]{1,0:T(8,128)}, f32[272,128]{1,0:T(8,128)S(1)}, u32[]{:S(2)}, u32[]{:S(2)}) collective-permute-start(f32[272,128]{1,0:T(8,128)} %get-tuple-element.37), channel_id=1, source_target_pairs={{0,64},{16,80},{32,96},{48,112},{64,0},{80,16},{96,32},{112,48},{1... | collective-permute-start | bytes 417800 | tf_op jit(solution)/shard_map/ppermute | solution.py:644
  44.5 11.3 %collective-permute-start.3 = (f32[272,128]{1,0:T(8,128)}, f32[272,128]{1,0:T(8,128)S(1)}, u32[]{:S(2)}, u32[]{:S(2)}) collective-permute-start(f32[272,128]{1,0:T(8,128)} %get-tuple-element.36), channel_id=1, source_target_pairs={{0,96},{16,112},{32,0},{48,16},{64,32},{80,48},{96,64},{112,80},{1... | collective-permute-start | bytes 417800 | tf_op jit(solution)/shard_map/ppermute | solution.py:644
  51.7 11.9 %all-to-all-start.2 = ((f32[8,2,200]{2,1,0:T(2,128)}), f32[8,2,200]{2,1,0:T(2,128)S(1)}, u32[]{:S(2)}, u32[]{:S(2)}) async-start(f32[8,2,200]{2,1,0:T(2,128)} %shard_map.98), calls=%async_computation.2 | async-start | bytes 32768 | tf_op jit(solution)/shard_map/all_to_all | solution.py:633
  64.4 9.5 %all-to-all-start.3 = ((f32[8,2,200]{2,1,0:T(2,128)}), f32[8,2,200]{2,1,0:T(2,128)S(1)}, u32[]{:S(2)}, u32[]{:S(2)}) async-start(f32[8,2,200]{2,1,0:T(2,128)} %shard_map.103), calls=%async_computation.3 | async-start | bytes 32768 | tf_op jit(solution)/shard_map/all_to_all | solution.py:633
  69.2 4.7 %copy-start.15 = (s32[48,128]{1,0:T(8,128)S(1)}, s32[48,128]{1,0:T(8,128)}, u32[]{:S(2)}) copy-start(s32[48,128]{1,0:T(8,128)} %copy-done.14) | copy-start | bytes 73732
  69.2 4.7 %copy-start.17 = (s32[48,128]{1,0:T(8,128)S(1)}, s32[48,128]{1,0:T(8,128)}, u32[]{:S(2)}) copy-start(s32[48,128]{1,0:T(8,128)} %copy-done.16) | copy-start | bytes 73732
  71.8 27.5 %collective-permute-start.4 = (f32[4,272,128]{2,1,0:T(8,128)}, f32[4,272,128]{2,1,0:T(8,128)}, u32[]{:S(2)}, u32[]{:S(2)}) collective-permute-start(f32[4,272,128]{2,1,0:T(8,128)} %shard_map.108), channel_id=1, source_target_pairs={{0,16},{16,0},{32,48},{48,32},{64,80},{80,64},{96,112},{112,96},{1... | collective-permute-start | bytes 1671176 | tf_op jit(solution)/shard_map/ppermute | solution.py:639
  76.4 15.4 %all-to-all-start.4 = ((f32[128,2,128]{2,1,0:T(2,128)}), f32[128,2,128]{2,1,0:T(2,128)S(1)}, u32[]{:S(2)}, u32[]{:S(2)}) async-start(f32[128,2,128]{2,1,0:T(2,128)} %bitcast.14), calls=%async_computation.4 | async-start | bytes 262144 | tf_op jit(solution)/shard_map/all_to_all | solution.py:629
  82.0 9.9 %copy-start.13 = (f32[2,128,128]{2,1,0:T(8,128)S(1)}, f32[2,128,128]{2,1,0:T(8,128)}, u32[]{:S(2)}) copy-start(f32[2,128,128]{2,1,0:T(8,128)} %get-tuple-element.28.refs_1_) | copy-start | bytes 393220
  94.9 14.2 %all-to-all-start.5 = ((f32[128,2,128]{2,1,0:T(2,128)}), f32[128,2,128]{2,1,0:T(2,128)S(1)}, u32[]{:S(2)}, u32[]{:S(2)}) async-start(f32[128,2,128]{2,1,0:T(2,128)} %bitcast.16), calls=%async_computation.5 | async-start | bytes 262144 | tf_op jit(solution)/shard_map/all_to_all | solution.py:629
  101.2 15.8 %collective-permute-start.5 = (f32[272,128]{1,0:T(8,128)}, f32[272,128]{1,0:T(8,128)S(1)}, u32[]{:S(2)}, u32[]{:S(2)}) collective-permute-start(f32[272,128]{1,0:T(8,128)} %get-tuple-element.34), channel_id=1, source_target_pairs={{0,32},{16,48},{32,64},{48,80},{64,96},{80,112},{96,0},{112,16},{1... | collective-permute-start | bytes 417800 | tf_op jit(solution)/shard_map/ppermute | solution.py:644
  102.5 14.5 %collective-permute-start.6 = (f32[272,128]{1,0:T(8,128)}, f32[272,128]{1,0:T(8,128)S(1)}, u32[]{:S(2)}, u32[]{:S(2)}) collective-permute-start(f32[272,128]{1,0:T(8,128)} %get-tuple-element.33), channel_id=1, source_target_pairs={{0,64},{16,80},{32,96},{48,112},{64,0},{80,16},{96,32},{112,48},{1... | collective-permute-start | bytes 417800 | tf_op jit(solution)/shard_map/ppermute | solution.py:644
  105.0 12.0 %collective-permute-start.7 = (f32[272,128]{1,0:T(8,128)}, f32[272,128]{1,0:T(8,128)S(1)}, u32[]{:S(2)}, u32[]{:S(2)}) collective-permute-start(f32[272,128]{1,0:T(8,128)} %get-tuple-element.32), channel_id=1, source_target_pairs={{0,96},{16,112},{32,0},{48,16},{64,32},{80,48},{96,64},{112,80},{1... | collective-permute-start | bytes 417800 | tf_op jit(solution)/shard_map/ppermute | solution.py:644
  113.0 12.5 %all-to-all-start.6 = ((f32[8,2,200]{2,1,0:T(2,128)}), f32[8,2,200]{2,1,0:T(2,128)S(1)}, u32[]{:S(2)}, u32[]{:S(2)}) async-start(f32[8,2,200]{2,1,0:T(2,128)} %shard_map.106), calls=%async_computation.6 | async-start | bytes 32768 | tf_op jit(solution)/shard_map/all_to_all | solution.py:633
  (9 other events, 17.5 us)

commit v5 on v4

--- a/solution.py
+++ b/solution.py
@@ -56,7 +56,7 @@
         order_ref[pl.ds(r, 1), :] = jnp.sum(hot * (counts[:, :LANES] + base), axis=0, keepdims=True).astype(jnp.int32)
         return base + counts[:, LANES:]
 
-    counts = lax.fori_loop(0, chunks, rank, jnp.zeros((LANES, LANES), F32), unroll=8)
+    counts = lax.fori_loop(0, chunks, rank, jnp.zeros((LANES, LANES), F32), unroll=24)
     high = jnp.floor(counts * (1.0 / LANES))
     split = jnp.concatenate([high, counts - high * LANES], axis=1).astype(BF16)
     below = jnp.where(lane < sub, 1.0, 0.0).astype(BF16)
@@ -155,7 +155,7 @@
                 dense[at, (3 * v + k) * LANES : (3 * v + k + 1) * LANES] = piece
         return carry
 
-    lax.fori_loop(0, chunks // 8, gather, 0, unroll=2 if first else 3)
+    lax.fori_loop(0, chunks // 8, gather, 0, unroll=6)
     row_of = start_ref[...] >> 7
     column = iota((LANES, chunks), 1)
     pick = jnp.concatenate(
@@ -192,7 +192,7 @@
             pay_ref[pl.ds(d * 8 * width_out + v, 8, stride=width_out), :] = found[v]
         return carry
 
-    lax.fori_loop(0, LANES // 8, tile, 0, unroll=4)
+    lax.fori_loop(0, LANES // 8, tile, 0, unroll=8 if first else 16)
 
 
 def place_scratch(values, chunks):
@@ -264,7 +264,7 @@
                 parts[3 * v + k, at, :] = piece
         return carry
 
-    lax.fori_loop(0, LANES // 8, split, 0, unroll=4)
+    lax.fori_loop(0, LANES // 8, split, 0, unroll=16)
     group = 8
 
     def accumulate(g, total):
@@ -283,7 +283,7 @@
             jnp.concatenate(right, axis=1), jnp.concatenate(left, axis=1), NT, preferred_element_type=F32
         )
 
-    total = lax.fori_loop(0, LANES // group, accumulate, jnp.zeros((LANES, 72), F32), unroll=4).T
+    total = lax.fori_loop(0, LANES // group, accumulate, jnp.zeros((LANES, 72), F32), unroll=16).T
     sums = [total[24 * v : 24 * v + 8] + total[24 * v + 8 : 24 * v + 16] + total[24 * v + 16 : 24 * v + 24] for v in range(3)]
     rows = prior_ref.shape[0]
     means = [[], []]
@@ -307,7 +307,7 @@
             ret_ref[pl.ds(g * 16 + c, 8, stride=2), :] = found
         return carry
 
-    lax.fori_loop(0, LANES // 8, look, 0, unroll=4)
+    lax.fori_loop(0, LANES // 8, look, 0, unroll=16)
 
 
 def owner_first(pay, star_ref, star_prior, cap):
@@ -359,7 +359,7 @@
                     shifted[pl.ds(pl.multiple_of(d * 8 + k * LANES, 8), 8), (3 * c + j) * LANES : (3 * c + j + 1) * LANES] = piece
         return carry
 
-    lax.fori_loop(0, LANES // 8, shift, 0, unroll=4)
+    lax.fori_loop(0, LANES // 8, shift, 0, unroll=16)
     row_of = line_ref[0:1, :] >> 7
     sub_rows = iota((chunks, LANES), 0)
     pick = jnp.concatenate([jnp.where(row_of + k == sub_rows, 1.0, 0.0) for k in range(2)], axis=1).astype(BF16)
@@ -522,7 +522,7 @@
             return (panel, tuple(fresh), tuple(update_next(mat, k, fresh, base, tile)))
 
         if begin < end:
-            carry = lax.fori_loop(begin, end, step, carry)
+            carry = lax.fori_loop(begin, end, step, carry, unroll=3)
     update_all(mat, high - 1, carry[0], carry[1])
 
 

time: 137 us -> 132 us (0.964)
  Pallas kernels: 46.2 us -> 40.6 us
  transfers between devices with their start and end apart: 15 -> 15, of which waited for: 5 -> 5; matrix products, arithmetic and copies ran while one was open for 3% -> 3% of each run, Pallas kernels for 28% -> 26%
where the time goes in v5:
time: 132 us; the launch traced here: 131 us
  starting transfers between devices  49.8 us (38%)
  Pallas kernels  40.6 us (31%)
  waiting for transfers between devices  21.8 us (17%)
  blocking collectives  9.27 us (7%)
  local copies, waits for them, and re-layouts  4.65 us (4%)
  other arithmetic  3.82 us (3%)
    all_to_all x4, starting transfers between devices, exchange(): lax.all_to_all(x.reshape(peers, -1, LANES), everyone, split_axis=0, conca...  25.9 us
    all_to_all x4, waiting for transfers between devices, exchange(): lax.all_to_all(x.reshape(peers, -1, LANES), everyone, split_axis=0, conca...  19.7 us
    all_to_all x3, starting transfers between devices, over_pix(): return lax.all_to_all(x, 'pix', split_axis=0, concat_axis=0, tiled=True)  12.9 us
    ppermute x6, starting transfers between devices, norm_exchange(): lax.ppermute(part, 'pix', [(i, (i + 2 * d) % pixes) for i in range(pixes)])  9.93 us
    all_to_all x1, blocking collectives, over_pix(): return lax.all_to_all(x, 'pix', split_axis=0, concat_axis=0, tiled=True)  9.27 us
    pallas_call x4, Pallas kernels, gram(): pl.pallas_call(functools.partial(gram_body, k), grid_spec=pltpu.PrefetchS...  8.5 us
    pallas_call x1, Pallas kernels, invert(): call(invert_body, pltpu.HBM((terms, 2 * LANES), F32), (pltpu.VMEM((terms,...  7.52 us
    unnamed x37, local copies, waits for them, and re-layouts  4.65 us
  transfers between devices with their start and end apart: 15, of which 5 were waited for; matrix products, arithmetic and copies ran while one was open for 3% of the time, Pallas kernels for 26%

profile of v5, /device:TPU:1, one launch (start us, length us, event | category | flops | bytes accessed | tf_op | source)
XLA Modules:
  0.0 130.8 jit_solution(9006058785166942730)
XLA Ops:
  1.4 2.9 %shard_map.95 = (s32[48,128]{1,0:T(8,128)S(1)}, s32[48,128]{1,0:T(8,128)S(1)}, s32[48,128]{1,0:T(8,128)S(1)}, s32[128,128]{1,0:T(8,128)S(1)}, s32[128,128]{1,0:T(8,128)S(1)}, /*index=5*/s32[8,128]{1,0:T(8,128)S(1)}) custom-call(s32[48,128]{1,0:T(8,128)S(1)} %bitcast.34), custom_call_target="tpu_custom_call" | custom-call | flops 4000000000 | bytes 49152 | tf_op jit(solution)/shard_map/pallas_call | solution.py:91
  4.3 3.0 %shard_map.96 = (f32[2,6144]{1,0:T(2,128)}, f32[512,128]{1,0:T(8,128)}) custom-call(f32[8,2,200]{2,1,0:T(2,128)S(1)} %copy-done.5, bf16[200,6144]{1,0:T(8,128)(2,1)S(1)} %copy-done, s32[48,128]{1,0:T(8,128)S(1)} %get-tuple-element.17.refs_2_.refs_3_, s32[48,128]{1,0:T(8,128)S(1)} %get-tuple-element.18.refs_3_.refs_4_, ...), custom_call_target="tpu_custom_call" | custom-call | flops 5000000000 | bytes 2457600 | tf_op jit(solution)/shard_map/pallas_call | solution.py:208
  7.4 11.5 %all-to-all-start = ((f32[128,4,128]{2,1,0:T(4,128)}), f32[128,4,128]{2,1,0:T(4,128)S(1)}, u32[]{:S(2)}, u32[]{:S(2)}) async-start(f32[128,4,128]{2,1,0:T(4,128)} %bitcast.4), calls=%async_computation | async-start | bytes 524288 | tf_op jit(solution)/shard_map/all_to_all | solution.py:629
  18.9 2.6 %shard_map.100 = f32[4,272,128]{2,1,0:T(8,128)} custom-call(s32[1]{0:T(128)} %bitcast.me_ref.refs_0_, bf16[200,6144]{1,0:T(8,128)(2,1)S(1)} %copy-done, f32[1,6144]{1,0:T(1,128)S(1)} %bitcast.37, s32[2,6144]{1,0:T(2,128)S(1)} %copy-done.1), custom_call_target="tpu_custom_call" | custom-call | flops 2000000000 | bytes 2457600 | tf_op jit(solution)/shard_map/pallas_call | solution.py:435
  24.2 5.5 %all-to-all-done = f32[128,4,128]{2,1,0:T(4,128)S(1)} async-done(((f32[128,4,128]{2,1,0:T(4,128)}), f32[128,4,128]{2,1,0:T(4,128)S(1)}, u32[]{:S(2)}, u32[]{:S(2)}) %all-to-all-start) | async-done | bytes 262176 | tf_op jit(solution)/shard_map/all_to_all | solution.py:629
  29.7 2.4 %shard_map.97 = (f32[256,128]{1,0:T(8,128)}, f32[2,128,128]{2,1,0:T(8,128)}) custom-call(f32[512,128]{1,0:T(8,128)S(1)} %bitcast.30, f32[2,768]{1,0:T(2,128)S(1)} %copy-done.6, f32[6,128]{1,0:T(8,128)S(1)} %bitcast.43), custom_call_target="tpu_custom_call" | custom-call | flops 4000000000 | bytes 262144 | tf_op jit(solution)/shard_map/pallas_call | solution.py:314
  32.1 4.5 %all-to-all-start.1 = ((f32[128,2,128]{2,1,0:T(2,128)}), f32[128,2,128]{2,1,0:T(2,128)S(1)}, u32[]{:S(2)}, u32[]{:S(2)}) async-start(f32[128,2,128]{2,1,0:T(2,128)} %bitcast.7), calls=%async_computation.1 | async-start | bytes 262144 | tf_op jit(solution)/shard_map/all_to_all | solution.py:629
  39.9 2.5 %collective-permute-start.2 = (f32[272,128]{1,0:T(8,128)}, f32[272,128]{1,0:T(8,128)S(1)}, u32[]{:S(2)}, u32[]{:S(2)}) collective-permute-start(f32[272,128]{1,0:T(8,128)} %get-tuple-element.37), channel_id=1, source_target_pairs={{0,64},{16,80},{32,96},{48,112},{64,0},{80,16},{96,32},{112,48},{1... | collective-permute-start | bytes 417800 | tf_op jit(solution)/shard_map/ppermute | solution.py:644
  43.5 3.0 %all-to-all-done.1 = f32[128,2,128]{2,1,0:T(2,128)S(1)} async-done(((f32[128,2,128]{2,1,0:T(2,128)}), f32[128,2,128]{2,1,0:T(2,128)S(1)}, u32[]{:S(2)}, u32[]{:S(2)}) %all-to-all-start.1) | async-done | bytes 131104 | tf_op jit(solution)/shard_map/all_to_all | solution.py:629
  49.4 4.0 %all-to-all-start.2 = ((f32[8,2,200]{2,1,0:T(2,128)}), f32[8,2,200]{2,1,0:T(2,128)S(1)}, u32[]{:S(2)}, u32[]{:S(2)}) async-start(f32[8,2,200]{2,1,0:T(2,128)} %shard_map.98), calls=%async_computation.2 | async-start | bytes 32768 | tf_op jit(solution)/shard_map/all_to_all | solution.py:633
  53.4 2.8 %shard_map.101.part_ref = f32[200,256]{1,0:T(8,128)S(1)} custom-call(f32[272,128]{1,0:T(8,128)S(1)} %get-tuple-element.39.refs_0_, f32[272,128]{1,0:T(8,128)S(1)} %collective-permute-done.1.refs_1_, f32[272,128]{1,0:T(8,128)S(1)} %collective-permute-done.2.refs_2_, f32[272,128]{1,0:T(8,128)S(1)} %collective-permute-done.3.refs_3_), custom_call_target="tpu_custom_call" | custom-call | flops 4000000000 | bytes 557056 | tf_op jit(solution)/shard_map/pallas_call | solution.py:570
  56.3 4.1 %shard_map.102.refs_1_ = f32[200,256]{1,0:T(8,128)S(1)} custom-call(f32[200,256]{1,0:T(8,128)S(1)} %shard_map.101.part_ref), custom_call_target="tpu_custom_call" | custom-call | flops 4000000000 | bytes 409600 | tf_op jit(solution)/shard_map/pallas_call | solution.py:579
  61.1 4.8 %all-to-all-start.3 = ((f32[8,2,200]{2,1,0:T(2,128)}), f32[8,2,200]{2,1,0:T(2,128)S(1)}, u32[]{:S(2)}, u32[]{:S(2)}) async-start(f32[8,2,200]{2,1,0:T(2,128)} %shard_map.103), calls=%async_computation.3 | async-start | bytes 32768 | tf_op jit(solution)/shard_map/all_to_all | solution.py:633
  66.0 2.6 %shard_map.108 = f32[4,272,128]{2,1,0:T(8,128)} custom-call(s32[1]{0:T(128)} %bitcast.me_ref.refs_0_, bf16[200,6144]{1,0:T(8,128)(2,1)S(1)} %copy-done, f32[1,6144]{1,0:T(1,128)S(1)} %bitcast.40, s32[2,6144]{1,0:T(2,128)S(1)} %copy-done.1), custom_call_target="tpu_custom_call" | custom-call | flops 2000000000 | bytes 2457600 | tf_op jit(solution)/shard_map/pallas_call | solution.py:435
  70.6 2.1 %shard_map.104 = (f32[2,6144]{1,0:T(2,128)}, f32[256,128]{1,0:T(8,128)}, f32[8,2,200]{2,1,0:T(2,128)S(1)}) custom-call(f32[8,2,200]{2,1,0:T(2,128)S(1)} %copy-done.5, f32[8,2,200]{2,1,0:T(2,128)S(1)} %all-to-all-done.3.refs_1_, bf16[200,6144]{1,0:T(8,128)(2,1)S(1)} %copy-done, s32[48,128]{1,0:T(8,128)S(1)} %copy-done.15, s32[48,128]{1,0:T(8,128)S(1)} %copy-done.17, ...), custom_call_target="tpu_custom_call" | custom-call | flops 3000000000 | bytes 2457600 | tf_op jit(solution)/shard_map/pallas_call | solution.py:219
  72.7 5.5 %all-to-all-start.4 = ((f32[128,2,128]{2,1,0:T(2,128)}), f32[128,2,128]{2,1,0:T(2,128)S(1)}, u32[]{:S(2)}, u32[]{:S(2)}) async-start(f32[128,2,128]{2,1,0:T(2,128)} %bitcast.14), calls=%async_computation.4 | async-start | bytes 262144 | tf_op jit(solution)/shard_map/all_to_all | solution.py:629
  80.0 8.2 %all-to-all-done.4 = f32[128,2,128]{2,1,0:T(2,128)S(1)} async-done(((f32[128,2,128]{2,1,0:T(2,128)}), f32[128,2,128]{2,1,0:T(2,128)S(1)}, u32[]{:S(2)}, u32[]{:S(2)}) %all-to-all-start.4) | async-done | bytes 131104 | tf_op jit(solution)/shard_map/all_to_all | solution.py:629
  88.1 2.4 %shard_map.105 = (f32[256,128]{1,0:T(8,128)}, f32[2,768]{1,0:T(2,128)}) custom-call(f32[256,128]{1,0:T(8,128)S(1)} %bitcast.33, f32[2,128,128]{2,1,0:T(8,128)S(1)} %copy-done.13, f32[2,768]{1,0:T(2,128)S(1)} %copy-done.6, f32[6,128]{1,0:T(8,128)S(1)} %bitcast.44), custom_call_target="tpu_custom_call" | custom-call | flops 3000000000 | bytes 131072 | tf_op jit(solution)/shard_map/pallas_call | solution.py:327
  90.5 4.3 %all-to-all-start.5 = ((f32[128,2,128]{2,1,0:T(2,128)}), f32[128,2,128]{2,1,0:T(2,128)S(1)}, u32[]{:S(2)}, u32[]{:S(2)}) async-start(f32[128,2,128]{2,1,0:T(2,128)} %bitcast.16), calls=%async_computation.5 | async-start | bytes 262144 | tf_op jit(solution)/shard_map/all_to_all | solution.py:629
  98.1 2.5 %collective-permute-start.6 = (f32[272,128]{1,0:T(8,128)}, f32[272,128]{1,0:T(8,128)S(1)}, u32[]{:S(2)}, u32[]{:S(2)}) collective-permute-start(f32[272,128]{1,0:T(8,128)} %get-tuple-element.33), channel_id=1, source_target_pairs={{0,64},{16,80},{32,96},{48,112},{64,0},{80,16},{96,32},{112,48},{1... | collective-permute-start | bytes 417800 | tf_op jit(solution)/shard_map/ppermute | solution.py:644
  101.6 3.0 %all-to-all-done.5 = f32[128,2,128]{2,1,0:T(2,128)S(1)} async-done(((f32[128,2,128]{2,1,0:T(2,128)}), f32[128,2,128]{2,1,0:T(2,128)S(1)}, u32[]{:S(2)}, u32[]{:S(2)}) %all-to-all-start.5) | async-done | bytes 131104 | tf_op jit(solution)/shard_map/all_to_all | solution.py:629
  108.2 4.0 %all-to-all-start.6 = ((f32[8,2,200]{2,1,0:T(2,128)}), f32[8,2,200]{2,1,0:T(2,128)S(1)}, u32[]{:S(2)}, u32[]{:S(2)}) async-start(f32[8,2,200]{2,1,0:T(2,128)} %shard_map.106), calls=%async_computation.6 | async-start | bytes 32768 | tf_op jit(solution)/shard_map/all_to_all | solution.py:633
  112.3 7.5 %shard_map.109.refs_3_ = f32[200,256]{1,0:T(8,128)} custom-call(f32[272,128]{1,0:T(8,128)S(1)} %get-tuple-element.35.refs_0_, f32[272,128]{1,0:T(8,128)S(1)} %collective-permute-done.5.refs_1_, f32[272,128]{1,0:T(8,128)S(1)} %collective-permute-done.6.refs_2_, f32[272,128]{1,0:T(8,128)S(1)} %collective-permute-done.7.refs_3_), custom_call_target="tpu_custom_call" | custom-call | flops 8000000000 | bytes 557056 | tf_op jit(solution)/shard_map/pallas_call | solution.py:548
  120.9 9.3 %all_to_all.40 = f32[8,2,200]{2,1,0:T(2,128)S(1)} all-to-all(f32[8,2,200]{2,1,0:T(2,128)S(1)} %shard_map.110), channel_id=1, replica_groups=mesh['pix'=8,'exp'=16] {'pix'}, dimensions={0} | all-to-all | bytes 25600 | tf_op jit(solution)/shard_map/all_to_all | solution.py:633
  (62 shorter events, 25.0 us)
Async XLA Ops:
  1.4 2.9 %copy-start.5 = (f32[8,2,200]{2,1,0:T(2,128)S(1)}, f32[8,2,200]{2,1,0:T(2,128)}, u32[]{:S(2)}) copy-start(f32[8,2,200]{2,1,0:T(2,128)} %refs_0_.3) | copy-start | bytes 38404
  4.3 3.1 %copy-start.14 = (s32[48,128]{1,0:T(8,128)}, s32[48,128]{1,0:T(8,128)S(1)}, u32[]{:S(2)}) copy-start(s32[48,128]{1,0:T(8,128)S(1)} %get-tuple-element.17.refs_2_.refs_3_) | copy-start | bytes 73732
  4.3 3.1 %copy-start.16 = (s32[48,128]{1,0:T(8,128)}, s32[48,128]{1,0:T(8,128)S(1)}, u32[]{:S(2)}) copy-start(s32[48,128]{1,0:T(8,128)S(1)} %get-tuple-element.18.refs_3_.refs_4_) | copy-start | bytes 73732
  4.3 42.3 %copy-start.11 = (s32[48,128]{1,0:T(8,128)}, s32[48,128]{1,0:T(8,128)S(1)}, u32[]{:S(2)}) copy-start(s32[48,128]{1,0:T(8,128)S(1)} %get-tuple-element.23.refs_1_) | copy-start | bytes 73732
  7.4 22.3 %all-to-all-start = ((f32[128,4,128]{2,1,0:T(4,128)}), f32[128,4,128]{2,1,0:T(4,128)S(1)}, u32[]{:S(2)}, u32[]{:S(2)}) async-start(f32[128,4,128]{2,1,0:T(4,128)} %bitcast.4), calls=%async_computation | async-start | bytes 524288 | tf_op jit(solution)/shard_map/all_to_all | solution.py:629
  21.4 8.3 %copy-start.6 = (f32[2,768]{1,0:T(2,128)S(1)}, f32[2,768]{1,0:T(2,128)}, u32[]{:S(2)}) copy-start(f32[2,768]{1,0:T(2,128)} %refs_2_.3) | copy-start | bytes 18436
  21.4 8.3 %copy-start.7 = (f32[768]{0:T(1024)S(1)}, f32[768]{0:T(1024)}, u32[]{:S(2)}) copy-start(f32[768]{0:T(1024)} %param.15) | copy-start | bytes 9220
  21.4 15.2 %collective-permute-start = (f32[4,272,128]{2,1,0:T(8,128)}, f32[4,272,128]{2,1,0:T(8,128)}, u32[]{:S(2)}, u32[]{:S(2)}) collective-permute-start(f32[4,272,128]{2,1,0:T(8,128)} %shard_map.100), channel_id=1, source_target_pairs={{0,16},{16,0},{32,48},{48,32},{64,80},{80,64},{96,112},{112,96},{1... | collective-permute-start | bytes 1671176 | tf_op jit(solution)/shard_map/ppermute | solution.py:639
  32.1 14.5 %all-to-all-start.1 = ((f32[128,2,128]{2,1,0:T(2,128)}), f32[128,2,128]{2,1,0:T(2,128)S(1)}, u32[]{:S(2)}, u32[]{:S(2)}) async-start(f32[128,2,128]{2,1,0:T(2,128)} %bitcast.7), calls=%async_computation.1 | async-start | bytes 262144 | tf_op jit(solution)/shard_map/all_to_all | solution.py:629
  38.6 14.9 %collective-permute-start.1 = (f32[272,128]{1,0:T(8,128)}, f32[272,128]{1,0:T(8,128)S(1)}, u32[]{:S(2)}, u32[]{:S(2)}) collective-permute-start(f32[272,128]{1,0:T(8,128)} %get-tuple-element.38), channel_id=1, source_target_pairs={{0,32},{16,48},{32,64},{48,80},{64,96},{80,112},{96,0},{112,16},{1... | collective-permute-start | bytes 417800 | tf_op jit(solution)/shard_map/ppermute | solution.py:644
  39.9 13.5 %collective-permute-start.2 = (f32[272,128]{1,0:T(8,128)}, f32[272,128]{1,0:T(8,128)S(1)}, u32[]{:S(2)}, u32[]{:S(2)}) collective-permute-start(f32[272,128]{1,0:T(8,128)} %get-tuple-element.37), channel_id=1, source_target_pairs={{0,64},{16,80},{32,96},{48,112},{64,0},{80,16},{96,32},{112,48},{1... | collective-permute-start | bytes 417800 | tf_op jit(solution)/shard_map/ppermute | solution.py:644
  42.4 11.0 %collective-permute-start.3 = (f32[272,128]{1,0:T(8,128)}, f32[272,128]{1,0:T(8,128)S(1)}, u32[]{:S(2)}, u32[]{:S(2)}) collective-permute-start(f32[272,128]{1,0:T(8,128)} %get-tuple-element.36), channel_id=1, source_target_pairs={{0,96},{16,112},{32,0},{48,16},{64,32},{80,48},{96,64},{112,80},{1... | collective-permute-start | bytes 417800 | tf_op jit(solution)/shard_map/ppermute | solution.py:644
  49.4 10.9 %all-to-all-start.2 = ((f32[8,2,200]{2,1,0:T(2,128)}), f32[8,2,200]{2,1,0:T(2,128)S(1)}, u32[]{:S(2)}, u32[]{:S(2)}) async-start(f32[8,2,200]{2,1,0:T(2,128)} %shard_map.98), calls=%async_computation.2 | async-start | bytes 32768 | tf_op jit(solution)/shard_map/all_to_all | solution.py:633
  61.1 9.5 %all-to-all-start.3 = ((f32[8,2,200]{2,1,0:T(2,128)}), f32[8,2,200]{2,1,0:T(2,128)S(1)}, u32[]{:S(2)}, u32[]{:S(2)}) async-start(f32[8,2,200]{2,1,0:T(2,128)} %shard_map.103), calls=%async_computation.3 | async-start | bytes 32768 | tf_op jit(solution)/shard_map/all_to_all | solution.py:633
  66.0 4.7 %copy-start.15 = (s32[48,128]{1,0:T(8,128)S(1)}, s32[48,128]{1,0:T(8,128)}, u32[]{:S(2)}) copy-start(s32[48,128]{1,0:T(8,128)} %copy-done.14) | copy-start | bytes 73732
  66.0 4.7 %copy-start.17 = (s32[48,128]{1,0:T(8,128)S(1)}, s32[48,128]{1,0:T(8,128)}, u32[]{:S(2)}) copy-start(s32[48,128]{1,0:T(8,128)} %copy-done.16) | copy-start | bytes 73732
  68.5 26.2 %collective-permute-start.4 = (f32[4,272,128]{2,1,0:T(8,128)}, f32[4,272,128]{2,1,0:T(8,128)}, u32[]{:S(2)}, u32[]{:S(2)}) collective-permute-start(f32[4,272,128]{2,1,0:T(8,128)} %shard_map.108), channel_id=1, source_target_pairs={{0,16},{16,0},{32,48},{48,32},{64,80},{80,64},{96,112},{112,96},{1... | collective-permute-start | bytes 1671176 | tf_op jit(solution)/shard_map/ppermute | solution.py:639
  72.7 15.4 %all-to-all-start.4 = ((f32[128,2,128]{2,1,0:T(2,128)}), f32[128,2,128]{2,1,0:T(2,128)S(1)}, u32[]{:S(2)}, u32[]{:S(2)}) async-start(f32[128,2,128]{2,1,0:T(2,128)} %bitcast.14), calls=%async_computation.4 | async-start | bytes 262144 | tf_op jit(solution)/shard_map/all_to_all | solution.py:629
  78.2 9.9 %copy-start.13 = (f32[2,128,128]{2,1,0:T(8,128)S(1)}, f32[2,128,128]{2,1,0:T(8,128)}, u32[]{:S(2)}) copy-start(f32[2,128,128]{2,1,0:T(8,128)} %get-tuple-element.28.refs_1_) | copy-start | bytes 393220
  90.5 14.2 %all-to-all-start.5 = ((f32[128,2,128]{2,1,0:T(2,128)}), f32[128,2,128]{2,1,0:T(2,128)S(1)}, u32[]{:S(2)}, u32[]{:S(2)}) async-start(f32[128,2,128]{2,1,0:T(2,128)} %bitcast.16), calls=%async_computation.5 | async-start | bytes 262144 | tf_op jit(solution)/shard_map/all_to_all | solution.py:629
  96.7 15.6 %collective-permute-start.5 = (f32[272,128]{1,0:T(8,128)}, f32[272,128]{1,0:T(8,128)S(1)}, u32[]{:S(2)}, u32[]{:S(2)}) collective-permute-start(f32[272,128]{1,0:T(8,128)} %get-tuple-element.34), channel_id=1, source_target_pairs={{0,32},{16,48},{32,64},{48,80},{64,96},{80,112},{96,0},{112,16},{1... | collective-permute-start | bytes 417800 | tf_op jit(solution)/shard_map/ppermute | solution.py:644
  98.1 14.2 %collective-permute-start.6 = (f32[272,128]{1,0:T(8,128)}, f32[272,128]{1,0:T(8,128)S(1)}, u32[]{:S(2)}, u32[]{:S(2)}) collective-permute-start(f32[272,128]{1,0:T(8,128)} %get-tuple-element.33), channel_id=1, source_target_pairs={{0,64},{16,80},{32,96},{48,112},{64,0},{80,16},{96,32},{112,48},{1... | collective-permute-start | bytes 417800 | tf_op jit(solution)/shard_map/ppermute | solution.py:644
  100.5 11.7 %collective-permute-start.7 = (f32[272,128]{1,0:T(8,128)}, f32[272,128]{1,0:T(8,128)S(1)}, u32[]{:S(2)}, u32[]{:S(2)}) collective-permute-start(f32[272,128]{1,0:T(8,128)} %get-tuple-element.32), channel_id=1, source_target_pairs={{0,96},{16,112},{32,0},{48,16},{64,32},{80,48},{96,64},{112,80},{1... | collective-permute-start | bytes 417800 | tf_op jit(solution)/shard_map/ppermute | solution.py:644
  108.2 11.6 %all-to-all-start.6 = ((f32[8,2,200]{2,1,0:T(2,128)}), f32[8,2,200]{2,1,0:T(2,128)S(1)}, u32[]{:S(2)}, u32[]{:S(2)}) async-start(f32[8,2,200]{2,1,0:T(2,128)} %shard_map.106), calls=%async_computation.6 | async-start | bytes 32768 | tf_op jit(solution)/shard_map/all_to_all | solution.py:633
  (9 other events, 15.7 us)

commit v6 on v5

--- a/solution.py
+++ b/solution.py
@@ -14,7 +14,7 @@
 BF16 = jnp.bfloat16
 GRANT = 16 << 20
 FLOPS_PER_US = 10**9
-SPLIT = 10
+SPLIT = 8
 NT = (((1,), (1,)), ((), ()))
 TN = (((0,), (0,)), ((), ()))
 
@@ -56,7 +56,7 @@
         order_ref[pl.ds(r, 1), :] = jnp.sum(hot * (counts[:, :LANES] + base), axis=0, keepdims=True).astype(jnp.int32)
         return base + counts[:, LANES:]
 
-    counts = lax.fori_loop(0, chunks, rank, jnp.zeros((LANES, LANES), F32), unroll=24)
+    counts = lax.fori_loop(0, chunks, rank, jnp.zeros((LANES, LANES), F32), unroll=48)
     high = jnp.floor(counts * (1.0 / LANES))
     split = jnp.concatenate([high, counts - high * LANES], axis=1).astype(BF16)
     below = jnp.where(lane < sub, 1.0, 0.0).astype(BF16)
@@ -522,7 +522,7 @@
             return (panel, tuple(fresh), tuple(update_next(mat, k, fresh, base, tile)))
 
         if begin < end:
-            carry = lax.fori_loop(begin, end, step, carry, unroll=3)
+            carry = lax.fori_loop(begin, end, step, carry, unroll=5)
     update_all(mat, high - 1, carry[0], carry[1])
 
 

time: 132 us -> 131 us (level)
  no operation moved by 1% of the time
where the time goes in v6:
time: 131 us
  starting transfers between devices  49.8 us (38%)
  Pallas kernels  40.4 us (31%)
  waiting for transfers between devices  21.8 us (17%)
  blocking collectives  9.27 us (7%)
  local copies, waits for them, and re-layouts  4.65 us (4%)
  other arithmetic  3.82 us (3%)
    all_to_all x4, starting transfers between devices, exchange(): lax.all_to_all(x.reshape(peers, -1, LANES), everyone, split_axis=0, conca...  25.9 us
    all_to_all x4, waiting for transfers between devices, exchange(): lax.all_to_all(x.reshape(peers, -1, LANES), everyone, split_axis=0, conca...  19.7 us
    all_to_all x3, starting transfers between devices, over_pix(): return lax.all_to_all(x, 'pix', split_axis=0, concat_axis=0, tiled=True)  12.9 us
    ppermute x6, starting transfers between devices, norm_exchange(): lax.ppermute(part, 'pix', [(i, (i + 2 * d) % pixes) for i in range(pixes)])  9.93 us
    all_to_all x1, blocking collectives, over_pix(): return lax.all_to_all(x, 'pix', split_axis=0, concat_axis=0, tiled=True)  9.27 us
    pallas_call x4, Pallas kernels, gram(): pl.pallas_call(functools.partial(gram_body, k), grid_spec=pltpu.PrefetchS...  8.49 us
    pallas_call x1, Pallas kernels, invert(): call(invert_body, pltpu.HBM((terms, 2 * LANES), F32), (pltpu.VMEM((terms,...  7.51 us
    unnamed x37, local copies, waits for them, and re-layouts  4.65 us
  transfers between devices with their start and end apart: 15, of which 5 were waited for; matrix products, arithmetic and copies ran while one was open for 3% of the time, Pallas kernels for 26%

profile of v6, /device:TPU:1, one launch (start us, length us, event | category | flops | bytes accessed | tf_op | source)
XLA Modules:
  0.0 130.6 jit_solution(5581536763560310562)
XLA Ops:
  1.4 3.0 %shard_map.95 = (s32[48,128]{1,0:T(8,128)S(1)}, s32[48,128]{1,0:T(8,128)S(1)}, s32[48,128]{1,0:T(8,128)S(1)}, s32[128,128]{1,0:T(8,128)S(1)}, s32[128,128]{1,0:T(8,128)S(1)}, /*index=5*/s32[8,128]{1,0:T(8,128)S(1)}) custom-call(s32[48,128]{1,0:T(8,128)S(1)} %bitcast.34), custom_call_target="tpu_custom_call" | custom-call | flops 4000000000 | bytes 49152 | tf_op jit(solution)/shard_map/pallas_call | solution.py:91
  4.5 3.0 %shard_map.96 = (f32[2,6144]{1,0:T(2,128)}, f32[512,128]{1,0:T(8,128)}) custom-call(f32[8,2,200]{2,1,0:T(2,128)S(1)} %copy-done.5, bf16[200,6144]{1,0:T(8,128)(2,1)S(1)} %copy-done, s32[48,128]{1,0:T(8,128)S(1)} %get-tuple-element.17.refs_2_.refs_3_, s32[48,128]{1,0:T(8,128)S(1)} %get-tuple-element.18.refs_3_.refs_4_, ...), custom_call_target="tpu_custom_call" | custom-call | flops 5000000000 | bytes 2457600 | tf_op jit(solution)/shard_map/pallas_call | solution.py:208
  7.5 11.5 %all-to-all-start = ((f32[128,4,128]{2,1,0:T(4,128)}), f32[128,4,128]{2,1,0:T(4,128)S(1)}, u32[]{:S(2)}, u32[]{:S(2)}) async-start(f32[128,4,128]{2,1,0:T(4,128)} %bitcast.4), calls=%async_computation | async-start | bytes 524288 | tf_op jit(solution)/shard_map/all_to_all | solution.py:629
  19.0 2.6 %shard_map.100 = f32[4,272,128]{2,1,0:T(8,128)} custom-call(s32[1]{0:T(128)} %bitcast.me_ref.refs_0_, bf16[200,6144]{1,0:T(8,128)(2,1)S(1)} %copy-done, f32[1,6144]{1,0:T(1,128)S(1)} %bitcast.37, s32[2,6144]{1,0:T(2,128)S(1)} %copy-done.1), custom_call_target="tpu_custom_call" | custom-call | flops 2000000000 | bytes 2457600 | tf_op jit(solution)/shard_map/pallas_call | solution.py:435
  24.3 5.5 %all-to-all-done = f32[128,4,128]{2,1,0:T(4,128)S(1)} async-done(((f32[128,4,128]{2,1,0:T(4,128)}), f32[128,4,128]{2,1,0:T(4,128)S(1)}, u32[]{:S(2)}, u32[]{:S(2)}) %all-to-all-start) | async-done | bytes 262176 | tf_op jit(solution)/shard_map/all_to_all | solution.py:629
  29.9 2.4 %shard_map.97 = (f32[256,128]{1,0:T(8,128)}, f32[2,128,128]{2,1,0:T(8,128)}) custom-call(f32[512,128]{1,0:T(8,128)S(1)} %bitcast.30, f32[2,768]{1,0:T(2,128)S(1)} %copy-done.6, f32[6,128]{1,0:T(8,128)S(1)} %bitcast.43), custom_call_target="tpu_custom_call" | custom-call | flops 4000000000 | bytes 262144 | tf_op jit(solution)/shard_map/pallas_call | solution.py:314
  32.2 4.5 %all-to-all-start.1 = ((f32[128,2,128]{2,1,0:T(2,128)}), f32[128,2,128]{2,1,0:T(2,128)S(1)}, u32[]{:S(2)}, u32[]{:S(2)}) async-start(f32[128,2,128]{2,1,0:T(2,128)} %bitcast.7), calls=%async_computation.1 | async-start | bytes 262144 | tf_op jit(solution)/shard_map/all_to_all | solution.py:629
  40.1 2.5 %collective-permute-start.2 = (f32[272,128]{1,0:T(8,128)}, f32[272,128]{1,0:T(8,128)S(1)}, u32[]{:S(2)}, u32[]{:S(2)}) collective-permute-start(f32[272,128]{1,0:T(8,128)} %get-tuple-element.37), channel_id=1, source_target_pairs={{0,64},{16,80},{32,96},{48,112},{64,0},{80,16},{96,32},{112,48},{1... | collective-permute-start | bytes 417800 | tf_op jit(solution)/shard_map/ppermute | solution.py:644
  43.7 3.0 %all-to-all-done.1 = f32[128,2,128]{2,1,0:T(2,128)S(1)} async-done(((f32[128,2,128]{2,1,0:T(2,128)}), f32[128,2,128]{2,1,0:T(2,128)S(1)}, u32[]{:S(2)}, u32[]{:S(2)}) %all-to-all-start.1) | async-done | bytes 131104 | tf_op jit(solution)/shard_map/all_to_all | solution.py:629
  49.5 4.0 %all-to-all-start.2 = ((f32[8,2,200]{2,1,0:T(2,128)}), f32[8,2,200]{2,1,0:T(2,128)S(1)}, u32[]{:S(2)}, u32[]{:S(2)}) async-start(f32[8,2,200]{2,1,0:T(2,128)} %shard_map.98), calls=%async_computation.2 | async-start | bytes 32768 | tf_op jit(solution)/shard_map/all_to_all | solution.py:633
  55.6 4.5 %shard_map.102.refs_1_ = f32[200,256]{1,0:T(8,128)S(1)} custom-call(f32[200,256]{1,0:T(8,128)S(1)} %shard_map.101.part_ref), custom_call_target="tpu_custom_call" | custom-call | flops 4000000000 | bytes 409600 | tf_op jit(solution)/shard_map/pallas_call | solution.py:579
  60.9 4.8 %all-to-all-start.3 = ((f32[8,2,200]{2,1,0:T(2,128)}), f32[8,2,200]{2,1,0:T(2,128)S(1)}, u32[]{:S(2)}, u32[]{:S(2)}) async-start(f32[8,2,200]{2,1,0:T(2,128)} %shard_map.103), calls=%async_computation.3 | async-start | bytes 32768 | tf_op jit(solution)/shard_map/all_to_all | solution.py:633
  65.8 2.6 %shard_map.108 = f32[4,272,128]{2,1,0:T(8,128)} custom-call(s32[1]{0:T(128)} %bitcast.me_ref.refs_0_, bf16[200,6144]{1,0:T(8,128)(2,1)S(1)} %copy-done, f32[1,6144]{1,0:T(1,128)S(1)} %bitcast.40, s32[2,6144]{1,0:T(2,128)S(1)} %copy-done.1), custom_call_target="tpu_custom_call" | custom-call | flops 2000000000 | bytes 2457600 | tf_op jit(solution)/shard_map/pallas_call | solution.py:435
  68.4 2.1 %all-to-all-done.3.refs_1_ = f32[8,2,200]{2,1,0:T(2,128)S(1)} async-done(((f32[8,2,200]{2,1,0:T(2,128)}), f32[8,2,200]{2,1,0:T(2,128)S(1)}, u32[]{:S(2)}, u32[]{:S(2)}) %all-to-all-start.3) | async-done | bytes 12832 | tf_op jit(solution)/shard_map/all_to_all | solution.py:633
  70.4 2.1 %shard_map.104 = (f32[2,6144]{1,0:T(2,128)}, f32[256,128]{1,0:T(8,128)}, f32[8,2,200]{2,1,0:T(2,128)S(1)}) custom-call(f32[8,2,200]{2,1,0:T(2,128)S(1)} %copy-done.5, f32[8,2,200]{2,1,0:T(2,128)S(1)} %all-to-all-done.3.refs_1_, bf16[200,6144]{1,0:T(8,128)(2,1)S(1)} %copy-done, s32[48,128]{1,0:T(8,128)S(1)} %copy-done.15, s32[48,128]{1,0:T(8,128)S(1)} %copy-done.17, ...), custom_call_target="tpu_custom_call" | custom-call | flops 3000000000 | bytes 2457600 | tf_op jit(solution)/shard_map/pallas_call | solution.py:219
  72.5 5.5 %all-to-all-start.4 = ((f32[128,2,128]{2,1,0:T(2,128)}), f32[128,2,128]{2,1,0:T(2,128)S(1)}, u32[]{:S(2)}, u32[]{:S(2)}) async-start(f32[128,2,128]{2,1,0:T(2,128)} %bitcast.14), calls=%async_computation.4 | async-start | bytes 262144 | tf_op jit(solution)/shard_map/all_to_all | solution.py:629
  79.8 8.2 %all-to-all-done.4 = f32[128,2,128]{2,1,0:T(2,128)S(1)} async-done(((f32[128,2,128]{2,1,0:T(2,128)}), f32[128,2,128]{2,1,0:T(2,128)S(1)}, u32[]{:S(2)}, u32[]{:S(2)}) %all-to-all-start.4) | async-done | bytes 131104 | tf_op jit(solution)/shard_map/all_to_all | solution.py:629
  87.9 2.4 %shard_map.105 = (f32[256,128]{1,0:T(8,128)}, f32[2,768]{1,0:T(2,128)}) custom-call(f32[256,128]{1,0:T(8,128)S(1)} %bitcast.33, f32[2,128,128]{2,1,0:T(8,128)S(1)} %copy-done.13, f32[2,768]{1,0:T(2,128)S(1)} %copy-done.6, f32[6,128]{1,0:T(8,128)S(1)} %bitcast.44), custom_call_target="tpu_custom_call" | custom-call | flops 3000000000 | bytes 131072 | tf_op jit(solution)/shard_map/pallas_call | solution.py:327
  90.3 4.3 %all-to-all-start.5 = ((f32[128,2,128]{2,1,0:T(2,128)}), f32[128,2,128]{2,1,0:T(2,128)S(1)}, u32[]{:S(2)}, u32[]{:S(2)}) async-start(f32[128,2,128]{2,1,0:T(2,128)} %bitcast.16), calls=%async_computation.5 | async-start | bytes 262144 | tf_op jit(solution)/shard_map/all_to_all | solution.py:629
  97.9 2.5 %collective-permute-start.6 = (f32[272,128]{1,0:T(8,128)}, f32[272,128]{1,0:T(8,128)S(1)}, u32[]{:S(2)}, u32[]{:S(2)}) collective-permute-start(f32[272,128]{1,0:T(8,128)} %get-tuple-element.33), channel_id=1, source_target_pairs={{0,64},{16,80},{32,96},{48,112},{64,0},{80,16},{96,32},{112,48},{1... | collective-permute-start | bytes 417800 | tf_op jit(solution)/shard_map/ppermute | solution.py:644
  101.4 3.0 %all-to-all-done.5 = f32[128,2,128]{2,1,0:T(2,128)S(1)} async-done(((f32[128,2,128]{2,1,0:T(2,128)}), f32[128,2,128]{2,1,0:T(2,128)S(1)}, u32[]{:S(2)}, u32[]{:S(2)}) %all-to-all-start.5) | async-done | bytes 131104 | tf_op jit(solution)/shard_map/all_to_all | solution.py:629
  108.0 4.0 %all-to-all-start.6 = ((f32[8,2,200]{2,1,0:T(2,128)}), f32[8,2,200]{2,1,0:T(2,128)S(1)}, u32[]{:S(2)}, u32[]{:S(2)}) async-start(f32[8,2,200]{2,1,0:T(2,128)} %shard_map.106), calls=%async_computation.6 | async-start | bytes 32768 | tf_op jit(solution)/shard_map/all_to_all | solution.py:633
  112.1 7.5 %shard_map.109.refs_3_ = f32[200,256]{1,0:T(8,128)} custom-call(f32[272,128]{1,0:T(8,128)S(1)} %get-tuple-element.35.refs_0_, f32[272,128]{1,0:T(8,128)S(1)} %collective-permute-done.5.refs_1_, f32[272,128]{1,0:T(8,128)S(1)} %collective-permute-done.6.refs_2_, f32[272,128]{1,0:T(8,128)S(1)} %collective-permute-done.7.refs_3_), custom_call_target="tpu_custom_call" | custom-call | flops 8000000000 | bytes 557056 | tf_op jit(solution)/shard_map/pallas_call | solution.py:548
  120.7 9.3 %all_to_all.40 = f32[8,2,200]{2,1,0:T(2,128)S(1)} all-to-all(f32[8,2,200]{2,1,0:T(2,128)S(1)} %shard_map.110), channel_id=1, replica_groups=mesh['pix'=8,'exp'=16] {'pix'}, dimensions={0} | all-to-all | bytes 25600 | tf_op jit(solution)/shard_map/all_to_all | solution.py:633
  (62 shorter events, 24.9 us)
Async XLA Ops:
  1.4 3.1 %copy-start.4 = (f32[6144]{0:T(1024)S(1)}, f32[6144]{0:T(1024)}, u32[]{:S(2)}) copy-start(f32[6144]{0:T(1024)} %param.9) | copy-start | bytes 73732
  1.4 3.1 %copy-start.5 = (f32[8,2,200]{2,1,0:T(2,128)S(1)}, f32[8,2,200]{2,1,0:T(2,128)}, u32[]{:S(2)}) copy-start(f32[8,2,200]{2,1,0:T(2,128)} %refs_0_.3) | copy-start | bytes 38404
  4.4 3.1 %copy-start.14 = (s32[48,128]{1,0:T(8,128)}, s32[48,128]{1,0:T(8,128)S(1)}, u32[]{:S(2)}) copy-start(s32[48,128]{1,0:T(8,128)S(1)} %get-tuple-element.17.refs_2_.refs_3_) | copy-start | bytes 73732
  4.4 42.3 %copy-start.11 = (s32[48,128]{1,0:T(8,128)}, s32[48,128]{1,0:T(8,128)S(1)}, u32[]{:S(2)}) copy-start(s32[48,128]{1,0:T(8,128)S(1)} %get-tuple-element.23.refs_1_) | copy-start | bytes 73732
  7.5 22.3 %all-to-all-start = ((f32[128,4,128]{2,1,0:T(4,128)}), f32[128,4,128]{2,1,0:T(4,128)S(1)}, u32[]{:S(2)}, u32[]{:S(2)}) async-start(f32[128,4,128]{2,1,0:T(4,128)} %bitcast.4), calls=%async_computation | async-start | bytes 524288 | tf_op jit(solution)/shard_map/all_to_all | solution.py:629
  21.6 8.3 %copy-start.6 = (f32[2,768]{1,0:T(2,128)S(1)}, f32[2,768]{1,0:T(2,128)}, u32[]{:S(2)}) copy-start(f32[2,768]{1,0:T(2,128)} %refs_2_.3) | copy-start | bytes 18436
  21.6 8.3 %copy-start.7 = (f32[768]{0:T(1024)S(1)}, f32[768]{0:T(1024)}, u32[]{:S(2)}) copy-start(f32[768]{0:T(1024)} %param.15) | copy-start | bytes 9220
  21.6 15.2 %collective-permute-start = (f32[4,272,128]{2,1,0:T(8,128)}, f32[4,272,128]{2,1,0:T(8,128)}, u32[]{:S(2)}, u32[]{:S(2)}) collective-permute-start(f32[4,272,128]{2,1,0:T(8,128)} %shard_map.100), channel_id=1, source_target_pairs={{0,16},{16,0},{32,48},{48,32},{64,80},{80,64},{96,112},{112,96},{1... | collective-permute-start | bytes 1671176 | tf_op jit(solution)/shard_map/ppermute | solution.py:639
  32.2 14.5 %all-to-all-start.1 = ((f32[128,2,128]{2,1,0:T(2,128)}), f32[128,2,128]{2,1,0:T(2,128)S(1)}, u32[]{:S(2)}, u32[]{:S(2)}) async-start(f32[128,2,128]{2,1,0:T(2,128)} %bitcast.7), calls=%async_computation.1 | async-start | bytes 262144 | tf_op jit(solution)/shard_map/all_to_all | solution.py:629
  38.7 14.9 %collective-permute-start.1 = (f32[272,128]{1,0:T(8,128)}, f32[272,128]{1,0:T(8,128)S(1)}, u32[]{:S(2)}, u32[]{:S(2)}) collective-permute-start(f32[272,128]{1,0:T(8,128)} %get-tuple-element.38), channel_id=1, source_target_pairs={{0,32},{16,48},{32,64},{48,80},{64,96},{80,112},{96,0},{112,16},{1... | collective-permute-start | bytes 417800 | tf_op jit(solution)/shard_map/ppermute | solution.py:644
  40.1 13.5 %collective-permute-start.2 = (f32[272,128]{1,0:T(8,128)}, f32[272,128]{1,0:T(8,128)S(1)}, u32[]{:S(2)}, u32[]{:S(2)}) collective-permute-start(f32[272,128]{1,0:T(8,128)} %get-tuple-element.37), channel_id=1, source_target_pairs={{0,64},{16,80},{32,96},{48,112},{64,0},{80,16},{96,32},{112,48},{1... | collective-permute-start | bytes 417800 | tf_op jit(solution)/shard_map/ppermute | solution.py:644
  42.6 11.0 %collective-permute-start.3 = (f32[272,128]{1,0:T(8,128)}, f32[272,128]{1,0:T(8,128)S(1)}, u32[]{:S(2)}, u32[]{:S(2)}) collective-permute-start(f32[272,128]{1,0:T(8,128)} %get-tuple-element.36), channel_id=1, source_target_pairs={{0,96},{16,112},{32,0},{48,16},{64,32},{80,48},{96,64},{112,80},{1... | collective-permute-start | bytes 417800 | tf_op jit(solution)/shard_map/ppermute | solution.py:644
  49.5 10.6 %all-to-all-start.2 = ((f32[8,2,200]{2,1,0:T(2,128)}), f32[8,2,200]{2,1,0:T(2,128)S(1)}, u32[]{:S(2)}, u32[]{:S(2)}) async-start(f32[8,2,200]{2,1,0:T(2,128)} %shard_map.98), calls=%async_computation.2 | async-start | bytes 32768 | tf_op jit(solution)/shard_map/all_to_all | solution.py:633
  60.9 9.5 %all-to-all-start.3 = ((f32[8,2,200]{2,1,0:T(2,128)}), f32[8,2,200]{2,1,0:T(2,128)S(1)}, u32[]{:S(2)}, u32[]{:S(2)}) async-start(f32[8,2,200]{2,1,0:T(2,128)} %shard_map.103), calls=%async_computation.3 | async-start | bytes 32768 | tf_op jit(solution)/shard_map/all_to_all | solution.py:633
  65.8 4.7 %copy-start.15 = (s32[48,128]{1,0:T(8,128)S(1)}, s32[48,128]{1,0:T(8,128)}, u32[]{:S(2)}) copy-start(s32[48,128]{1,0:T(8,128)} %copy-done.14) | copy-start | bytes 73732
  65.8 4.7 %copy-start.17 = (s32[48,128]{1,0:T(8,128)S(1)}, s32[48,128]{1,0:T(8,128)}, u32[]{:S(2)}) copy-start(s32[48,128]{1,0:T(8,128)} %copy-done.16) | copy-start | bytes 73732
  68.3 26.2 %collective-permute-start.4 = (f32[4,272,128]{2,1,0:T(8,128)}, f32[4,272,128]{2,1,0:T(8,128)}, u32[]{:S(2)}, u32[]{:S(2)}) collective-permute-start(f32[4,272,128]{2,1,0:T(8,128)} %shard_map.108), channel_id=1, source_target_pairs={{0,16},{16,0},{32,48},{48,32},{64,80},{80,64},{96,112},{112,96},{1... | collective-permute-start | bytes 1671176 | tf_op jit(solution)/shard_map/ppermute | solution.py:639
  72.5 15.4 %all-to-all-start.4 = ((f32[128,2,128]{2,1,0:T(2,128)}), f32[128,2,128]{2,1,0:T(2,128)S(1)}, u32[]{:S(2)}, u32[]{:S(2)}) async-start(f32[128,2,128]{2,1,0:T(2,128)} %bitcast.14), calls=%async_computation.4 | async-start | bytes 262144 | tf_op jit(solution)/shard_map/all_to_all | solution.py:629
  78.1 9.9 %copy-start.13 = (f32[2,128,128]{2,1,0:T(8,128)S(1)}, f32[2,128,128]{2,1,0:T(8,128)}, u32[]{:S(2)}) copy-start(f32[2,128,128]{2,1,0:T(8,128)} %get-tuple-element.28.refs_1_) | copy-start | bytes 393220
  90.3 14.2 %all-to-all-start.5 = ((f32[128,2,128]{2,1,0:T(2,128)}), f32[128,2,128]{2,1,0:T(2,128)S(1)}, u32[]{:S(2)}, u32[]{:S(2)}) async-start(f32[128,2,128]{2,1,0:T(2,128)} %bitcast.16), calls=%async_computation.5 | async-start | bytes 262144 | tf_op jit(solution)/shard_map/all_to_all | solution.py:629
  96.5 15.6 %collective-permute-start.5 = (f32[272,128]{1,0:T(8,128)}, f32[272,128]{1,0:T(8,128)S(1)}, u32[]{:S(2)}, u32[]{:S(2)}) collective-permute-start(f32[272,128]{1,0:T(8,128)} %get-tuple-element.34), channel_id=1, source_target_pairs={{0,32},{16,48},{32,64},{48,80},{64,96},{80,112},{96,0},{112,16},{1... | collective-permute-start | bytes 417800 | tf_op jit(solution)/shard_map/ppermute | solution.py:644
  97.9 14.2 %collective-permute-start.6 = (f32[272,128]{1,0:T(8,128)}, f32[272,128]{1,0:T(8,128)S(1)}, u32[]{:S(2)}, u32[]{:S(2)}) collective-permute-start(f32[272,128]{1,0:T(8,128)} %get-tuple-element.33), channel_id=1, source_target_pairs={{0,64},{16,80},{32,96},{48,112},{64,0},{80,16},{96,32},{112,48},{1... | collective-permute-start | bytes 417800 | tf_op jit(solution)/shard_map/ppermute | solution.py:644
  100.3 11.7 %collective-permute-start.7 = (f32[272,128]{1,0:T(8,128)}, f32[272,128]{1,0:T(8,128)S(1)}, u32[]{:S(2)}, u32[]{:S(2)}) collective-permute-start(f32[272,128]{1,0:T(8,128)} %get-tuple-element.32), channel_id=1, source_target_pairs={{0,96},{16,112},{32,0},{48,16},{64,32},{80,48},{96,64},{112,80},{1... | collective-permute-start | bytes 417800 | tf_op jit(solution)/shard_map/ppermute | solution.py:644
  108.0 11.6 %all-to-all-start.6 = ((f32[8,2,200]{2,1,0:T(2,128)}), f32[8,2,200]{2,1,0:T(2,128)S(1)}, u32[]{:S(2)}, u32[]{:S(2)}) async-start(f32[8,2,200]{2,1,0:T(2,128)} %shard_map.106), calls=%async_computation.6 | async-start | bytes 32768 | tf_op jit(solution)/shard_map/all_to_all | solution.py:633
  (9 other events, 16.3 us)
